TPU v7x, 32 devices: a whole 2x2x4 slice. The times are simulated.
32 devices in a mesh: tile: 8 (over y, x, core), bin: 4 (over z).
Axes of the slice: x: 2, y: 2, z: 4, core: 2. Of those that a mesh axis runs over, the one named last changes fastest.
Arguments:
- dust_density: float32 [64, 64, 512], P('bin', 'tile'), may hold values from 0.05 to 2
- dust_vr: float32 [64, 64, 512], P('bin', 'tile'), may hold values from -1 to 1
- dust_va: float32 [64, 64, 512], P('bin', 'tile'), may hold values from -1 to 1
- gas_density: float32 [64, 512], P('tile'), may hold values from 0.5 to 2
- gas_vr: float32 [64, 512], P('tile'), may hold values from -1 to 1
- gas_va: float32 [64, 512], P('tile'), may hold values from -1 to 1
- stop_time: float32 [64], P('bin'), may hold values from 0.05 to 20
- gain_coef: bfloat16 [64, 64, 64], P('bin'), may hold values from -0.09375 to 0.09375
Outputs:
- density_out: float32 [64, 64, 512], P('bin', 'tile')
- vr_out: float32 [64, 64, 512], P('bin', 'tile')
- va_out: float32 [64, 64, 512], P('bin', 'tile')
- gas_vr_out: float32 [64, 512], P('tile')
- gas_va_out: float32 [64, 512], P('tile')
All inputs are finite; a program needn't handle non-finite values.
Results may differ from a plain program's by a relative error of at most 0.0017.
Values may be sent and summed in bfloat16 or wider, within the bound.
No kernel may reach another device: no remote copies, remote signals or barrier semaphores. Data moves between devices by JAX's collectives and lax.ppermute only.
A program may use at most 64 MiB of HBM per device.

v0:
```python
import jax
import jax.numpy as jnp
from jax import lax
from jax.sharding import PartitionSpec as P

COURANT = 0.2
COAGULATION = 0.5


def padded_2(shard, sides, width):
    for axis, dim in sides:
        count, length = (lax.axis_size(axis), shard.shape[dim])
        up = [(i, (i + 1) % count) for i in range(count - 1)]
        down = [(j, i) for i, j in up]
        last = lax.slice_in_dim(shard, length - width, length, axis=dim)
        initial = lax.slice_in_dim(shard, 0, width, axis=dim)
        before = lax.ppermute(last, axis, up)
        after = lax.ppermute(initial, axis, down)
        shard = jnp.concatenate([before, shard, after], axis=dim)
    return shard


def minmod(first, second):
    smaller = jnp.sign(first) * jnp.minimum(jnp.abs(first), jnp.abs(second))
    return jnp.where(first * second > 0, smaller, jnp.zeros_like(first))


def faces_div(values, speeds, along):
    length = values.shape[along]

    def part(array, lower, upper_cut):
        return lax.slice_in_dim(array, lower, length - upper_cut, axis=along)

    slope = minmod(part(values, 1, 1) - part(values, 0, 2), part(values, 2, 0) - part(values, 1, 1))
    centre = part(values, 1, 1)
    centre_speed = part(speeds, 1, 1)
    inner_len = length - 2

    def sub(array, lower, upper_cut):
        return lax.slice_in_dim(array, lower, inner_len - upper_cut, axis=along)

    speed = 0.5 * (sub(centre_speed, 0, 1) + sub(centre_speed, 1, 0))
    left = sub(centre, 0, 1) + 0.5 * (1.0 - speed * COURANT) * sub(slope, 0, 1)
    right = sub(centre, 1, 0) - 0.5 * (1.0 + speed * COURANT) * sub(slope, 1, 0)
    flux = jnp.maximum(speed, 0.0) * left + jnp.minimum(speed, 0.0) * right
    face_count = inner_len - 1
    return lax.slice_in_dim(flux, 1, face_count, axis=along) - lax.slice_in_dim(
        flux, 0, face_count - 1, axis=along
    )


def wrap_azimuth(field):
    return jnp.concatenate([field[..., -2:], field, field[..., :2]], axis=-1)


def coef_gain(coef_piece, densities):
    piece_bins, bin_total, _ = coef_piece.shape
    inner = jnp.dot(
        coef_piece.reshape(piece_bins * bin_total, bin_total),
        densities,
        preferred_element_type=jnp.float32,
    )
    inner = inner.reshape(piece_bins, bin_total, densities.shape[1])
    return jnp.sum(inner * densities.astype(jnp.float32)[None], axis=1)


def body(dust_density, dust_vr, dust_va, gas_density, gas_vr, gas_va, stop_time, gain_coef):
    bins_here, row_count, cells_cycle = dust_density.shape
    stacked = jnp.stack([dust_density, dust_vr])
    padded = padded_2(stacked, (("tile", 2),), 2)
    padded_rho = padded[0]
    padded_speed = padded[1]
    radial_div = faces_div(padded_rho, padded_speed, 1)
    azimuth_div = faces_div(wrap_azimuth(dust_density), wrap_azimuth(dust_va), 2)
    density_adv = dust_density - COURANT * (radial_div + azimuth_div)
    drag_rate = 1.0 / stop_time
    coupling = drag_rate / (1.0 + drag_rate)
    weight = density_adv * coupling[:, None, None]
    partials = (
        jnp.sum(weight * dust_vr, axis=0),
        jnp.sum(weight * dust_va, axis=0),
        jnp.sum(weight, axis=0),
    )
    sum_radial, sum_azimuth, sum_weight = lax.psum((partials[0], partials[1], partials[2]), "bin")
    denom = gas_density + sum_weight
    gas_vr_out = (gas_density * gas_vr + sum_radial) / denom
    gas_va_out = (gas_density * gas_va + sum_azimuth) / denom
    rate_col = drag_rate[:, None, None]
    vr_out = (dust_vr + rate_col * gas_vr_out[None]) / (1.0 + rate_col)
    va_out = (dust_va + rate_col * gas_va_out[None]) / (1.0 + rate_col)
    density_low = density_adv.astype(jnp.bfloat16).reshape(bins_here, row_count * cells_cycle)
    cell_bins = lax.all_to_all(density_low, "bin", split_axis=1, concat_axis=0, tiled=True)
    coef_piece = lax.all_gather(gain_coef, "bin", axis=0, tiled=True)
    piece_bins = coef_piece.shape[0]
    grouped = coef_piece.reshape(piece_bins // 16, 16, coef_piece.shape[1], coef_piece.shape[2])
    pieces = lax.map(lambda group: coef_gain(group, cell_bins), grouped)
    partial_gain = pieces.reshape(piece_bins, cell_bins.shape[1])
    gain = lax.all_to_all(partial_gain, "bin", split_axis=0, concat_axis=1, tiled=True)
    density_out = density_adv + COAGULATION * gain.reshape(density_adv.shape)
    return (density_out, vr_out, va_out, gas_vr_out, gas_va_out)


def solution(mesh):
    in_specs = (
        P("bin", "tile", None),
        P("bin", "tile", None),
        P("bin", "tile", None),
        P("tile", None),
        P("tile", None),
        P("tile", None),
        P("bin"),
        P("bin", None, None),
    )
    out_specs = (
        P("bin", "tile", None),
        P("bin", "tile", None),
        P("bin", "tile", None),
        P("tile", None),
        P("tile", None),
    )
    return jax.shard_map(body, mesh=mesh, in_specs=in_specs, out_specs=out_specs, check_vma=False)
```

profile of v0, /device:TPU:0, one launch (start us, length us, event | category | flops | bytes accessed | tf_op | source)
XLA Modules:
  0.0 76.3 jit_solution(7310223411598829857)
XLA Ops:
  0.7 1.3 %pad_maximum_fusion.8 = (f32[2,16,2,512]{3,2,1,0:T(2,128)S(1)}, f32[2,16,2,512]{3,2,1,0:T(2,128)S(1)}) fusion(f32[1,16,8,512]{3,2,1,0:T(8,128)} %bitcast.29, f32[1,16,8,512]{3,2,1,0:T(8,128)} %bitcast.26), kind=kLoop, calls=%fused_computation.57 | loop fusion | flops 65536 | bytes 786432 | tf_op jit(solution)/shard_map/slice | solution.py:15
  2.0 1.3 %collective-permute-start.1 = (f32[2,16,2,512]{3,2,1,0:T(2,128)S(1)}, f32[2,16,2,512]{3,2,1,0:T(2,128)S(1)}, u32[]{:S(2)}, u32[]{:S(2)}) collective-permute-start(f32[2,16,2,512]{3,2,1,0:T(2,128)S(1)} %get-tuple-element.48), channel_id=1, source_target_pairs={{4,0},{8,4},{12,8},{16,12},{20,16},{24,20},{28,24},{5,1},{9,5},{13... | collective-permute-start | bytes 393224 | tf_op jit(solution)/shard_map/ppermute | solution.py:18
  3.3 3.0 %collective-permute-start = (f32[2,16,2,512]{3,2,1,0:T(2,128)S(1)}, f32[2,16,2,512]{3,2,1,0:T(2,128)S(1)}, u32[]{:S(2)}, u32[]{:S(2)}) collective-permute-start(f32[2,16,2,512]{3,2,1,0:T(2,128)S(1)} %get-tuple-element.47), channel_id=1, source_target_pairs={{0,4},{4,8},{8,12},{12,16},{16,20},{20,24},{24,28},{1,5},{5,9},{9,... | collective-permute-start | bytes 393224 | tf_op jit(solution)/shard_map/ppermute | solution.py:17
  6.4 1.0 %fusion.24 = (f32[16,8,2]{2,1,0:T(8,128)S(1)}, f32[16,8,2]{2,1,0:T(8,128)S(1)}) fusion(f32[16,8,512]{2,1,0:T(8,128)} %param.10), kind=kLoop, calls=%fused_computation.64 | loop fusion | bytes 4096 | tf_op jit(solution)/shard_map/slice | solution.py:53
  7.4 0.3 multiply_select_fusion.1
  7.8 0.4 fusion.12
  8.2 0.5 copy-done.1
  8.7 0.2 pad_maximum_fusion
  8.9 0.1 slice_bitcast_fusion.1
  9.0 0.3 multiply_select_fusion
  9.4 0.4 fusion.6
  9.8 0.2 multiply_reduce_fusion.1
  10.0 0.1 all_to_all.22
  10.1 0.7 copy.16
  10.8 6.3 %all-to-all-start = ((bf16[16,4,1024]{2,0,1:T(8,128)(2,1)}), bf16[16,4,1024]{2,0,1:T(8,128)(2,1)S(1)}, u32[]{:S(2)}, u32[]{:S(2)}) async-start(bf16[16,4,1024]{2,0,1:T(8,128)(2,1)} %copy.16), calls=%async_computation | async-start | bytes 262144 | tf_op jit(solution)/shard_map/all_to_all | solution.py:92
  17.2 23.8 %all_gather.3 = bf16[64,64,64]{2,1,0:T(8,128)(2,1)S(1)} all-gather(bf16[16,64,64]{2,1,0:T(8,128)(2,1)S(1)} %copy-done.3), channel_id=1, replica_groups=mesh['tile'=8,'bin'=4] {'bin'}, dimensions={0}, use_global_device_ids=true | all-gather | bytes 655360 | tf_op jit(solution)/shard_map/all_gather | solution.py:93
  41.0 18.5 %all-reduce = (f32[8,512]{1,0:T(8,128)S(1)}, f32[8,512]{1,0:T(8,128)S(1)}, f32[8,512]{1,0:T(8,128)S(1)}) all-reduce(f32[8,512]{1,0:T(8,128)S(1)} %get-tuple-element.30, f32[8,512]{1,0:T(8,128)S(1)} %get-tuple-element.29, f32[8,512]{1,0:T(8,128)S(1)} %get-tuple-element.28), channel_id=1, replica_groups=mesh['tile'=8,'bin'=4] {'bin'}, use_global_device_ids=true, to_apply=%region_4.5 | all-reduce | flops 12288 | bytes 98304 | tf_op jit(solution)/shard_map/psum | solution.py:84
  59.6 5.5 %while.10 = (s32[]{:T(128)}, f32[4,16,1024]{2,1,0:T(8,128)}, bf16[4,16,64,64]{3,2,1,0:T(8,128)(2,1)S(1)}, bf16[64,1024]{1,0:T(8,128)(2,1)S(1)}, s32[]{:T(128)}) while((s32[]{:T(128)}, f32[4,16,1024]{2,1,0:T(8,128)}, bf16[4,16,64,64]{3,2,1,0:T(8,128)(2,1)S(1)}, bf16[64,1024]{1,0:T(8,128)(2,1)S(1)}, s32[]{:T(128)}) %tuple.36), condition=%wide.region_2.3_spmd, body=%wide.region_0.2_spmd.sunk | while | flops 136364032 | bytes 1245261 | solution.py:96
  59.6 0.7 multiply_reduce_fusion.5
  60.3 0.6 bitcast_dynamic-update-slice_fusion.2
  61.0 0.7 multiply_reduce_fusion.5
  61.7 0.6 bitcast_dynamic-update-slice_fusion.2
  62.3 0.7 multiply_reduce_fusion.5
  63.0 0.6 bitcast_dynamic-update-slice_fusion.2
  63.7 0.7 multiply_reduce_fusion.5
  64.4 0.6 bitcast_dynamic-update-slice_fusion.2
  65.0 3.4 %all-to-all-start.1 = ((f32[4,16,1024]{2,1,0:T(8,128)}), f32[4,16,1024]{2,1,0:T(8,128)S(1)}, u32[]{:S(2)}, u32[]{:S(2)}) async-start(f32[4,16,1024]{2,1,0:T(8,128)} %get-tuple-element.27), calls=%async_computation.1 | async-start | bytes 524288 | tf_op jit(solution)/shard_map/all_to_all | solution.py:98
  68.5 1.0 %add_divide_fusion = (f32[16,8,512]{2,1,0:T(8,128)}, f32[16,8,512]{2,1,0:T(8,128)}) fusion(f32[16,8,512]{2,1,0:T(8,128)S(1)} %copy-done.2, f32[8,512]{1,0:T(8,128)S(1)} %get-tuple-element.53, f32[16]{0:T(128)S(1)} %broadcast_add_fusion, f32[16]{0:T(128)S(1)} %get-tuple-element.44, f32[16,8,512]{2,1,0:T(8,128)S(1)} %copy-done.1, ...), kind=kLoop, calls=%fused_computation.50 | loop fusion | flops 393216 | bytes 1081472 | tf_op jit(solution)/shard_map/div | solution.py:90
  69.5 5.7 %all-to-all-done.1 = f32[4,16,1024]{2,1,0:T(8,128)S(1)} async-done(((f32[4,16,1024]{2,1,0:T(8,128)}), f32[4,16,1024]{2,1,0:T(8,128)S(1)}, u32[]{:S(2)}, u32[]{:S(2)}) %all-to-all-start.1) | async-done | bytes 262176 | tf_op jit(solution)/shard_map/all_to_all | solution.py:98
  75.2 0.2 copy.17
  75.4 0.1 mul.163
  75.5 0.7 add.69
  (33 shorter events, 0.3 us)
Async XLA Ops:
  0.6 6.8 %copy-start = (f32[16,8,512]{2,1,0:T(8,128)S(1)}, f32[16,8,512]{2,1,0:T(8,128)}, u32[]{:S(2)}) copy-start(f32[16,8,512]{2,1,0:T(8,128)} %param.10) | copy-start | bytes 786436
  0.6 6.7 %copy-start.9 = (f32[16]{0:T(128)S(1)}, f32[16]{0:T(128)}, u32[]{:S(2)}) copy-start(f32[16]{0:T(128)} %param.16) | copy-start | bytes 196
  0.7 6.7 %copy-start.2 = (f32[16,8,512]{2,1,0:T(8,128)S(1)}, f32[16,8,512]{2,1,0:T(8,128)}, u32[]{:S(2)}) copy-start(f32[16,8,512]{2,1,0:T(8,128)} %param.12) | copy-start | bytes 786436
  2.0 6.1 %collective-permute-start.1 = (f32[2,16,2,512]{3,2,1,0:T(2,128)S(1)}, f32[2,16,2,512]{3,2,1,0:T(2,128)S(1)}, u32[]{:S(2)}, u32[]{:S(2)}) collective-permute-start(f32[2,16,2,512]{3,2,1,0:T(2,128)S(1)} %get-tuple-element.48), channel_id=1, source_target_pairs={{4,0},{8,4},{12,8},{16,12},{20,16},{24,20},{28,24},{5,1},{9,5},{13... | collective-permute-start | bytes 393224 | tf_op jit(solution)/shard_map/ppermute | solution.py:18
  3.3 4.8 %collective-permute-start = (f32[2,16,2,512]{3,2,1,0:T(2,128)S(1)}, f32[2,16,2,512]{3,2,1,0:T(2,128)S(1)}, u32[]{:S(2)}, u32[]{:S(2)}) collective-permute-start(f32[2,16,2,512]{3,2,1,0:T(2,128)S(1)} %get-tuple-element.47), channel_id=1, source_target_pairs={{0,4},{4,8},{8,12},{12,16},{16,20},{20,24},{24,28},{1,5},{5,9},{9,... | collective-permute-start | bytes 393224 | tf_op jit(solution)/shard_map/ppermute | solution.py:17
  7.7 1.0 %copy-start.1 = (f32[16,8,512]{2,1,0:T(8,128)S(1)}, f32[16,8,512]{2,1,0:T(8,128)}, u32[]{:S(2)}) copy-start(f32[16,8,512]{2,1,0:T(8,128)} %param.11) | copy-start | bytes 786436
  10.0 7.2 %copy-start.3 = (bf16[16,64,64]{2,1,0:T(8,128)(2,1)S(1)}, bf16[16,64,64]{2,1,0:T(8,128)(2,1)}, u32[]{:S(2)}) copy-start(bf16[16,64,64]{2,1,0:T(8,128)(2,1)} %param.17) | copy-start | bytes 393220
  10.8 48.7 %all-to-all-start = ((bf16[16,4,1024]{2,0,1:T(8,128)(2,1)}), bf16[16,4,1024]{2,0,1:T(8,128)(2,1)S(1)}, u32[]{:S(2)}, u32[]{:S(2)}) async-start(bf16[16,4,1024]{2,0,1:T(8,128)(2,1)} %copy.16), calls=%async_computation | async-start | bytes 262144 | tf_op jit(solution)/shard_map/all_to_all | solution.py:92
  59.5 8.9 %copy-start.6 = (f32[8,512]{1,0:T(8,128)S(1)}, f32[8,512]{1,0:T(8,128)}, u32[]{:S(2)}) copy-start(f32[8,512]{1,0:T(8,128)} %param.13) | copy-start | bytes 49156
  59.5 8.9 %copy-start.7 = (f32[8,512]{1,0:T(8,128)S(1)}, f32[8,512]{1,0:T(8,128)}, u32[]{:S(2)}) copy-start(f32[8,512]{1,0:T(8,128)} %param.15) | copy-start | bytes 49156
  59.5 8.9 %copy-start.8 = (f32[8,512]{1,0:T(8,128)S(1)}, f32[8,512]{1,0:T(8,128)}, u32[]{:S(2)}) copy-start(f32[8,512]{1,0:T(8,128)} %param.14) | copy-start | bytes 49156
  65.0 10.2 %all-to-all-start.1 = ((f32[4,16,1024]{2,1,0:T(8,128)}), f32[4,16,1024]{2,1,0:T(8,128)S(1)}, u32[]{:S(2)}, u32[]{:S(2)}) async-start(f32[4,16,1024]{2,1,0:T(8,128)} %get-tuple-element.27), calls=%async_computation.1 | async-start | bytes 524288 | tf_op jit(solution)/shard_map/all_to_all | solution.py:98
  68.5 6.9 %copy-start.4 = (f32[8,512]{1,0:T(8,128)}, f32[8,512]{1,0:T(8,128)S(1)}, u32[]{:S(2)}) copy-start(f32[8,512]{1,0:T(8,128)S(1)} %get-tuple-element.53) | copy-start | bytes 49156
  68.5 6.9 %copy-start.5 = (f32[8,512]{1,0:T(8,128)}, f32[8,512]{1,0:T(8,128)S(1)}, u32[]{:S(2)}) copy-start(f32[8,512]{1,0:T(8,128)S(1)} %get-tuple-element.54) | copy-start | bytes 49156
where the time goes:
time: 76.7 us; the launch traced here: 76.3 us
  blocking collectives  42.3 us (55%)
  starting transfers between devices  14.1 us (18%)
  waiting for transfers between devices  5.72 us (7%)
  local copies, waits for them, and re-layouts  5.37 us (7%)
  other arithmetic  5 us (7%)
  matrix products  2.76 us (4%)
  between operations  0.94 us (1%)
    all_gather x1, blocking collectives, body(): coef_piece = lax.all_gather(gain_coef, 'bin', axis=0, tiled=True)  23.8 us
    psum x1, blocking collectives, body(): lax.psum((partials[0], partials[1], partials[2]), 'bin')  18.5 us
    all_to_all x1, starting transfers between devices, body(): lax.all_to_all(density_low, 'bin', split_axis=1, concat_axis=0, tiled=True)  6.35 us
    all_to_all x1, waiting for transfers between devices, body(): lax.all_to_all(partial_gain, 'bin', split_axis=0, concat_axis=1, tiled=True)  5.71 us
    all_to_all x1, starting transfers between devices, body(): lax.all_to_all(partial_gain, 'bin', split_axis=0, concat_axis=1, tiled=True)  3.41 us
    ppermute x1, starting transfers between devices, padded_2(): before = lax.ppermute(last, axis, up)  3.04 us
    dot_general x4, matrix products, coef_gain(): jnp.dot(coef_piece.reshape(piece_bins * bin_total, bin_total), densities,...  2.76 us
    dynamic_update_slice x4, local copies, waits for them, and re-layouts, body(): pieces = lax.map(lambda group: coef_gain(group, cell_bins), grouped)  2.56 us
  transfers between devices with their start and end apart: 4, of which 1 were waited for; matrix products, arithmetic and copies ran while one was open for 3% of the time, Pallas kernels for 0%

commit v1 on v0

v1 whole, which is shorter than its diff:
```python
import jax
import jax.numpy as jnp
from jax import lax
from jax.experimental import pallas as pl
from jax.experimental.pallas import tpu as pltpu
from jax.sharding import PartitionSpec as P

COURANT = 0.2
COAGULATION = 0.5
HALO = 2
F32 = jnp.float32
BF16 = jnp.bfloat16

VMEM = pl.BlockSpec(memory_space=pltpu.VMEM)
SMEM = pl.BlockSpec(memory_space=pltpu.SMEM)


def minmod(a, b):
    return jnp.maximum(jnp.minimum(a, b), 0.0) + jnp.minimum(jnp.maximum(a, b), 0.0)


def face_flux(low, low_slope, high, high_slope, u):
    cu = COURANT * u
    left = low + (0.5 - 0.5 * cu) * low_slope
    right = high - (0.5 + 0.5 * cu) * high_slope
    return jnp.maximum(u, 0.0) * left + jnp.minimum(u, 0.0) * right


def shift(x, by, axis):
    return pltpu.roll(x, by % x.shape[axis], axis)


def edge_kernel(rho_ref, vr_ref, to_a_ref, to_b_ref):
    rows = rho_ref.shape[1]
    even = lax.axis_index("tile") % 2 == 0
    up = (rho_ref[:, 0, :], rho_ref[:, 1, :], vr_ref[:, 0, :])
    down = (rho_ref[:, rows - 1, :], rho_ref[:, rows - 2, :], vr_ref[:, rows - 1, :])
    for n in range(3):
        to_a_ref[n] = jnp.where(even, down[n], up[n]).astype(BF16)
        to_b_ref[n] = jnp.where(even, up[n], down[n]).astype(BF16)


def radial(q, v, top, bottom):
    rows = q.shape[0]
    row = lax.broadcasted_iota(jnp.int32, q.shape, 0)
    first, last = row == 0, row == rows - 1
    q_next = jnp.where(last, bottom[0], shift(q, -1, 0))
    q_prev = jnp.where(first, top[0], shift(q, 1, 0))
    v_next = jnp.where(last, bottom[2], shift(v, -1, 0))
    v_prev = jnp.where(first, top[2], shift(v, 1, 0))
    d_next = q_next - q
    d_prev = q - q_prev
    s = minmod(d_prev, d_next)
    s_top = minmod(top[0] - top[1], d_prev)
    s_bottom = minmod(d_next, bottom[1] - bottom[0])
    s_prev = jnp.where(first, s_top, shift(s, 1, 0))
    s_next = jnp.where(last, s_bottom, shift(s, -1, 0))
    out = face_flux(q, s, q_next, s_next, 0.5 * (v + v_next))
    into = face_flux(q_prev, s_prev, q, s, 0.5 * (v_prev + v))
    return out - into


def azimuthal(q, v):
    q_next = shift(q, -1, 1)
    d = q_next - q
    s = minmod(shift(d, 1, 1), d)
    flux = face_flux(q, s, q_next, shift(s, -1, 1), 0.5 * (v + shift(v, -1, 1)))
    return flux - shift(flux, 1, 1)


def inner_kernel(rho_ref, vr_ref, va_ref, base_ref, low_ref, adv_ref):
    bins, rows, _ = rho_ref.shape

    def one_bin(b, carry):
        q = rho_ref[b]
        zero = jnp.zeros_like(q)
        base = q - COURANT * azimuthal(q, va_ref[b])
        base_ref[b] = base
        none = (zero, zero, zero)
        adv_ref[b] = base - COURANT * radial(q, vr_ref[b], none, none)
        return carry

    lax.fori_loop(0, bins, one_bin, 0)
    for n in range(rows - 2 * HALO):
        low_ref[n] = adv_ref[:, HALO + n, :].astype(BF16)


def outer_kernel(scal_ref, rho_ref, vr_ref, va_ref, base_ref, from_a_ref, from_b_ref, adv_ref, low_ref, sums_ref, top_ref, bottom_ref):
    bins, rows, _ = rho_ref.shape
    tile, tiles = lax.axis_index("tile"), lax.axis_size("tile")
    even = tile % 2 == 0
    has_top = jnp.where(tile > 0, 1.0, 0.0)
    has_bottom = jnp.where(tile < tiles - 1, 1.0, 0.0)
    for n in range(3):
        a, b = from_a_ref[n].astype(F32), from_b_ref[n].astype(F32)
        top_ref[n] = jnp.where(even, b, a) * has_top
        bottom_ref[n] = jnp.where(even, a, b) * has_bottom
    shape = sums_ref.shape[1:]

    def one_bin(b, sums):
        top = tuple(jnp.broadcast_to(top_ref[n, pl.ds(b, 1), :], shape) for n in range(3))
        bottom = tuple(jnp.broadcast_to(bottom_ref[n, pl.ds(b, 1), :], shape) for n in range(3))
        vr = vr_ref[b]
        adv = base_ref[b] - COURANT * radial(rho_ref[b], vr, top, bottom)
        adv_ref[b] = adv
        weight = adv * scal_ref[0, b]
        return (sums[0] + weight * vr, sums[1] + weight * va_ref[b], sums[2] + weight)

    zero = jnp.zeros(shape, F32)
    sums = lax.fori_loop(0, bins, one_bin, (zero, zero, zero))
    for n in range(3):
        sums_ref[n] = sums[n]
    for n, r in enumerate(edge_rows(rows)):
        low_ref[n] = adv_ref[:, r, :].astype(BF16)


def edge_rows(rows):
    return list(range(HALO)) + list(range(rows - HALO, rows))


def drag_kernel(scal_ref, sums_ref, more_ref, gas_ref, gvr_ref, gva_ref, vr_ref, va_ref, vr_out, va_out, gvr_out, gva_out):
    bins = vr_ref.shape[0]
    gas = gas_ref[...]
    denom = gas + (sums_ref[2] + more_ref[2])
    new_r = (gas * gvr_ref[...] + (sums_ref[0] + more_ref[0])) / denom
    new_a = (gas * gva_ref[...] + (sums_ref[1] + more_ref[1])) / denom
    gvr_out[...] = new_r
    gva_out[...] = new_a
    for b in range(bins):
        rate, scale = scal_ref[1, b], scal_ref[2, b]
        vr_out[b] = (vr_ref[b] + rate * new_r) * scale
        va_out[b] = (va_ref[b] + rate * new_a) * scale


def gather_low(parts, dens_ref, n_rows):
    here = lax.axis_index("bin")
    for offset, part in enumerate(parts):
        bins = part.shape[1]
        at = pl.multiple_of((here ^ offset) * bins, bins)
        for n in range(n_rows):
            dens_ref[n, pl.ds(at, bins), :] = part[n]


def gain_rows(coef_ref, dens_ref, gain_ref, bins, n_rows):
    total = dens_ref.shape[1]
    group = 8

    def one_row(n, carry):
        low = dens_ref[n]
        wide = low.astype(F32)
        acc = jnp.zeros((bins, low.shape[1]), F32)
        for i in range(0, total, group):
            inner = jnp.dot(coef_ref[i * bins:(i + group) * bins, :], low, preferred_element_type=F32)
            for g in range(group):
                acc = acc + inner[g * bins:(g + 1) * bins] * wide[i + g:i + g + 1]
        gain_ref[n] = acc
        return carry

    lax.fori_loop(0, n_rows, one_row, 0)


def inner_gain_kernel(coef_ref, *refs):
    *parts, gain_ref, dens_ref = refs
    n_rows, bins, _ = parts[0].shape
    gather_low(parts, dens_ref, n_rows)
    gain_rows(coef_ref, dens_ref, gain_ref, bins, n_rows)


def outer_gain_kernel(coef_ref, adv_ref, inner_ref, *refs):
    *parts, out_ref, dens_ref, gain_ref = refs
    n_rows, bins, _ = parts[0].shape
    rows = adv_ref.shape[1]
    gather_low(parts, dens_ref, n_rows)
    gain_rows(coef_ref, dens_ref, gain_ref, bins, n_rows)
    for n, r in enumerate(edge_rows(rows)):
        out_ref[:, r, :] = adv_ref[:, r, :] + COAGULATION * gain_ref[n]
    for n in range(rows - 2 * HALO):
        out_ref[:, HALO + n, :] = adv_ref[:, HALO + n, :] + COAGULATION * inner_ref[n]


def struct(shape, dtype=F32):
    return jax.ShapeDtypeStruct(shape, dtype)


def call(kernel, outs, specs, *args, scratch=()):
    return pl.pallas_call(
        kernel,
        out_shape=outs,
        in_specs=specs,
        out_specs=jax.tree.map(lambda _: VMEM, outs),
        scratch_shapes=scratch,
    )(*args)


def xor_pairs(axis, bit):
    return [(i, i ^ bit) for i in range(lax.axis_size(axis))]


def even_pairs(axis):
    return xor_pairs(axis, 1)


def odd_pairs(axis):
    count = lax.axis_size(axis)
    pairs = [(0, count - 1), (count - 1, 0)]
    for i in range(1, count - 1, 2):
        pairs += [(i, i + 1), (i + 1, i)]
    return pairs


def gather_bins(x):
    parts = {0: x}
    bit = lax.axis_size("bin") // 2
    while bit:
        parts.update({at ^ bit: lax.ppermute(part, "bin", xor_pairs("bin", bit)) for at, part in list(parts.items())})
        bit //= 2
    return [parts[at] for at in range(len(parts))]


def gather_direct(x):
    count = lax.axis_size("bin")
    sent = {at: lax.ppermute(x, "bin", xor_pairs("bin", at)) for at in range(count - 1, 0, -1)}
    return [x] + [sent[at] for at in range(1, count)]


def body(rho, vr, va, gas, gvr, gva, stop_time, coef):
    bins, rows, cells = rho.shape
    total = coef.shape[1]
    inner_rows, outer_rows = rows - 2 * HALO, 2 * HALO
    rate = 1.0 / stop_time
    scal = jnp.stack([rate / (1.0 + rate), rate, 1.0 / (1.0 + rate)])
    coef_rows = jnp.transpose(coef, (1, 0, 2)).reshape(total * bins, total)
    field = struct(rho.shape)

    halo = struct((3, bins, cells), BF16)
    to_a, to_b = call(edge_kernel, (halo, halo), [VMEM] * 2, rho, vr)
    from_b = lax.ppermute(to_b, "tile", odd_pairs("tile"))
    from_a = lax.ppermute(to_a, "tile", even_pairs("tile"))

    base, low_in = call(
        inner_kernel, (field, struct((inner_rows, bins, cells), BF16)), [VMEM] * 3, rho, vr, va,
        scratch=[pltpu.VMEM(rho.shape, F32)],
    )
    parts_in = gather_bins(low_in)

    adv, low_out, sums = call(
        outer_kernel, (field, struct((outer_rows, bins, cells), BF16), struct((3, rows, cells))),
        [SMEM] + [VMEM] * 6, scal, rho, vr, va, base, from_a, from_b,
        scratch=[pltpu.VMEM((3, bins, cells), F32)] * 2,
    )
    parts_out = gather_direct(low_out)

    bit = lax.axis_size("bin") // 2
    others = None
    step = 1
    while True:
        others = lax.ppermute(sums, "bin", xor_pairs("bin", step))
        step *= 2
        if step > bit:
            break
        sums = sums + others
    vr_out, va_out, gvr_out, gva_out = call(
        drag_kernel, (field, field, struct(gas.shape), struct(gas.shape)), [SMEM] + [VMEM] * 7,
        scal, sums, others, gas, gvr, gva, vr, va,
    )

    gain_in = call(
        inner_gain_kernel, struct((inner_rows, bins, cells)), [VMEM] * (1 + len(parts_in)), coef_rows, *parts_in,
        scratch=[pltpu.VMEM((inner_rows, total, cells), BF16)],
    )
    density_out = call(
        outer_gain_kernel, field, [VMEM] * (3 + len(parts_out)), coef_rows, adv, gain_in, *parts_out,
        scratch=[pltpu.VMEM((outer_rows, total, cells), BF16), pltpu.VMEM((outer_rows, bins, cells), F32)],
    )
    return density_out, vr_out, va_out, gvr_out, gva_out


def solution(mesh):
    field, flat = P("bin", "tile", None), P("tile", None)
    return jax.shard_map(
        body,
        mesh=mesh,
        in_specs=(field, field, field, flat, flat, flat, P("bin"), P("bin", None, None)),
        out_specs=(field, field, field, flat, flat),
        check_vma=False,
    )
```

time: 76.7 us -> 40.9 us (0.53)
  blocking collectives: 42.3 us -> 0 us
  Pallas kernels: 0 us -> 20.4 us
  waiting for transfers between devices: 5.72 us -> 0.14 us
  other arithmetic: 5 us -> 1.43 us
  matrix products: 2.76 us -> 0 us
  local copies, waits for them, and re-layouts: 5.37 us -> 3.38 us
    all_gather x1 -> x0, blocking collectives: 23.8 us -> none  [body(): coef_piece = lax.all_gather(gain_coef, 'bin', axis=0, tiled=True)]
    pallas_call x0 -> x6, Pallas kernels: none -> 20.4 us  [call(): pl.pallas_call(kernel, out_shape=outs, in_specs=specs, out_specs=jax.tree...]
    psum x1 -> x0, blocking collectives: 18.5 us -> none  [body(): lax.psum((partials[0], partials[1], partials[2]), 'bin')]
    ppermute x2 -> x10, starting transfers between devices: 4.33 us -> 14.6 us  [the longest x3 4.62 us: gather_bins(): lax.ppermute(part, 'bin', xor_pairs('bin', bit))]
    all_to_all x2 -> x0, starting transfers between devices: 9.75 us -> none  [the longest x1 6.35 us: body(): lax.all_to_all(density_low, 'bin', split_axis=1, concat_axis=0, tiled=True)]
    all_to_all x2 -> x0, waiting for transfers between devices: 5.71 us -> none  [the longest x1 5.71 us: body(): lax.all_to_all(partial_gain, 'bin', split_axis=0, concat_axis=1, tiled=True)]
    dot_general x4 -> x0, matrix products: 2.76 us -> none  [coef_gain(): jnp.dot(coef_piece.reshape(piece_bins * bin_total, bin_total), densities,...]
    dynamic_update_slice x4 -> x0, local copies, waits for them, and re-layouts: 2.56 us -> none  [body(): pieces = lax.map(lambda group: coef_gain(group, cell_bins), grouped)]
  transfers between devices with their start and end apart: 4 -> 10, of which waited for: 1 -> 1; matrix products, arithmetic and copies ran while one was open for 3% -> 6% of each run, Pallas kernels for 0% -> 41%
where the time goes in v1:
time: 40.9 us; the launch traced here: 40.6 us
  Pallas kernels  20.4 us (50%)
  starting transfers between devices  14.6 us (36%)
  local copies, waits for them, and re-layouts  3.38 us (8%)
  other arithmetic  1.43 us (3%)
  between operations  0.74 us (2%)
    pallas_call x6, Pallas kernels, call(): pl.pallas_call(kernel, out_shape=outs, in_specs=specs, out_specs=jax.tree...  20.4 us
    ppermute x3, starting transfers between devices, gather_bins(): lax.ppermute(part, 'bin', xor_pairs('bin', bit))  4.62 us
    ppermute x3, starting transfers between devices, gather_direct(): lax.ppermute(x, 'bin', xor_pairs('bin', at))  4.28 us
    ppermute x1, starting transfers between devices, body(): from_b = lax.ppermute(to_b, 'tile', odd_pairs('tile'))  3.54 us
    unnamed x26, local copies, waits for them, and re-layouts  2.5 us
    ppermute x2, starting transfers between devices, body(): others = lax.ppermute(sums, 'bin', xor_pairs('bin', step))  1.65 us
    transpose x1, local copies, waits for them, and re-layouts, body(): coef_rows = jnp.transpose(coef, (1, 0, 2)).reshape(total * bins, total)  0.88 us
  transfers between devices with their start and end apart: 10, of which 1 were waited for; matrix products, arithmetic and copies ran while one was open for 6% of the time, Pallas kernels for 41%

profile of v1, /device:TPU:0, one launch (start us, length us, event | category | flops | bytes accessed | tf_op | source)
XLA Modules:
  0.0 40.6 jit_solution(2674331598225706442)
XLA Ops:
  0.6 1.9 %shard_map.120 = (bf16[3,16,512]{2,1,0:T(8,128)(2,1)}, bf16[3,16,512]{2,1,0:T(8,128)(2,1)}) custom-call(f32[16,8,512]{2,1,0:T(8,128)} %rho_ref.5, f32[16,8,512]{2,1,0:T(8,128)} %vr_ref.7), custom_call_target="tpu_custom_call" | custom-call | tf_op jit(solution)/shard_map/pallas_call | solution.py:186
  2.5 0.5 %collective-permute-start = (bf16[3,16,512]{2,1,0:T(8,128)(2,1)}, bf16[3,16,512]{2,1,0:T(8,128)(2,1)S(1)}, u32[]{:S(2)}, u32[]{:S(2)}) collective-permute-start(bf16[3,16,512]{2,1,0:T(8,128)(2,1)} %get-tuple-element.17), channel_id=1, source_target_pairs={{0,4},{4,0},{8,12},{12,8},{16,20},{20,16},{24,28},{28,24},{1,5},{5... | collective-permute-start | bytes 147464 | tf_op jit(solution)/shard_map/ppermute | solution.py:238
  3.0 3.5 %collective-permute-start.1 = (bf16[3,16,512]{2,1,0:T(8,128)(2,1)}, bf16[3,16,512]{2,1,0:T(8,128)(2,1)S(1)}, u32[]{:S(2)}, u32[]{:S(2)}) collective-permute-start(bf16[3,16,512]{2,1,0:T(8,128)(2,1)} %get-tuple-element.18), channel_id=1, source_target_pairs={{0,28},{28,0},{4,8},{8,4},{12,16},{16,12},{20,24},{24,20},{1,29},{... | collective-permute-start | bytes 147464 | tf_op jit(solution)/shard_map/ppermute | solution.py:237
  6.6 6.6 %shard_map.119 = (f32[16,8,512]{2,1,0:T(8,128)}, bf16[4,16,512]{2,1,0:T(8,128)(2,1)}) custom-call(f32[16,8,512]{2,1,0:T(8,128)} %rho_ref.5, f32[16,8,512]{2,1,0:T(8,128)} %vr_ref.7, f32[16,8,512]{2,1,0:T(8,128)} %va_ref.5), custom_call_target="tpu_custom_call" | custom-call | tf_op jit(solution)/shard_map/pallas_call | solution.py:186
  13.2 2.6 %collective-permute-start.3 = (bf16[4,16,512]{2,1,0:T(8,128)(2,1)}, bf16[4,16,512]{2,1,0:T(8,128)(2,1)S(1)}, u32[]{:S(2)}, u32[]{:S(2)}) collective-permute-start(bf16[4,16,512]{2,1,0:T(8,128)(2,1)} %get-tuple-element.20.refs_0_), channel_id=1, source_target_pairs={{0,2},{1,3},{2,0},{3,1},{4,6},{5,7},{6,4},{7,5},{8,10},{9,11},{10,... | collective-permute-start | bytes 196616 | tf_op jit(solution)/shard_map/ppermute | solution.py:215
  15.8 0.6 %pad_maximum_fusion.scal_ref = f32[3,16]{1,0:T(4,128)} fusion(f32[1,16]{1,0:T(1,128)S(1)} %divide_bitcast_fusion, f32[1,16]{1,0:T(1,128)S(1)} %bitcast.10, f32[1,16]{1,0:T(1,128)S(1)} %get-tuple-element.27), kind=kLoop, calls=%fused_computation | loop fusion | flops 96 | bytes 384 | tf_op jit(solution)/shard_map/stack | solution.py:231
  16.4 0.0 collective-permute-done.from_a_ref
  16.4 0.0 collective-permute-done.1.from_b_ref
  16.4 0.6 %copy-done.9 = bf16[3,16,512]{2,1,0:T(8,128)(2,1)} copy-done((bf16[3,16,512]{2,1,0:T(8,128)(2,1)}, bf16[3,16,512]{2,1,0:T(8,128)(2,1)S(1)}, u32[]{:S(2)}) %copy-start.9) | copy-done | bytes 49176
  17.0 0.0 copy-done.10
  17.0 2.9 %shard_map.121 = (f32[16,8,512]{2,1,0:T(8,128)}, bf16[4,16,512]{2,1,0:T(8,128)(2,1)}, f32[3,8,512]{2,1,0:T(8,128)}) custom-call(f32[3,16]{1,0:T(4,128)} %pad_maximum_fusion.scal_ref, f32[16,8,512]{2,1,0:T(8,128)} %rho_ref.5, f32[16,8,512]{2,1,0:T(8,128)} %vr_ref.7, f32[16,8,512]{2,1,0:T(8,128)} %va_ref.5, f32[16,8,512]{2,1,0:T(8,128)} %get-tuple-element.16.base_ref, ...), custom_call_target="tpu_custom_call" | custom-call | tf_op jit(solution)/shard_map/pallas_call | solution.py:186
  19.9 1.6 %collective-permute-start.8 = (f32[3,8,512]{2,1,0:T(8,128)}, f32[3,8,512]{2,1,0:T(8,128)S(1)}, u32[]{:S(2)}, u32[]{:S(2)}) collective-permute-start(f32[3,8,512]{2,1,0:T(8,128)} %get-tuple-element.22), channel_id=1, source_target_pairs={{0,1},{1,0},{2,3},{3,2},{4,5},{5,4},{6,7},{7,6},{8,9},{9,8},{10,11... | collective-permute-start | bytes 147464 | tf_op jit(solution)/shard_map/ppermute | solution.py:257
  21.5 0.4 %collective-permute-start.2 = (bf16[4,16,512]{2,1,0:T(8,128)(2,1)S(1)}, bf16[4,16,512]{2,1,0:T(8,128)(2,1)S(1)}, u32[]{:S(2)}, u32[]{:S(2)}) collective-permute-start(bf16[4,16,512]{2,1,0:T(8,128)(2,1)S(1)} %copy-done.2), channel_id=1, source_target_pairs={{0,1},{1,0},{2,3},{3,2},{4,5},{5,4},{6,7},{7,6},{8,9},{9,8},{10,11... | collective-permute-start | bytes 196616 | tf_op jit(solution)/shard_map/ppermute | solution.py:215
  21.9 1.6 %collective-permute-start.4 = (bf16[4,16,512]{2,1,0:T(8,128)(2,1)S(1)}, bf16[4,16,512]{2,1,0:T(8,128)(2,1)S(1)}, u32[]{:S(2)}, u32[]{:S(2)}) collective-permute-start(bf16[4,16,512]{2,1,0:T(8,128)(2,1)S(1)} %collective-permute-done.3.refs_2_), channel_id=1, source_target_pairs={{0,1},{1,0},{2,3},{3,2},{4,5},{5,4},{6,7},{7,6},{8,9},{9,8},{10,11... | collective-permute-start | bytes 196616 | tf_op jit(solution)/shard_map/ppermute | solution.py:215
  23.5 0.4 %collective-permute-start.5 = (bf16[4,16,512]{2,1,0:T(8,128)(2,1)}, bf16[4,16,512]{2,1,0:T(8,128)(2,1)S(1)}, u32[]{:S(2)}, u32[]{:S(2)}) collective-permute-start(bf16[4,16,512]{2,1,0:T(8,128)(2,1)} %get-tuple-element.21.refs_0_), channel_id=1, source_target_pairs={{0,1},{1,0},{2,3},{3,2},{4,5},{5,4},{6,7},{7,6},{8,9},{9,8},{10,11... | collective-permute-start | bytes 196616 | tf_op jit(solution)/shard_map/ppermute | solution.py:222
  24.0 0.7 %collective-permute-start.6 = (bf16[4,16,512]{2,1,0:T(8,128)(2,1)}, bf16[4,16,512]{2,1,0:T(8,128)(2,1)S(1)}, u32[]{:S(2)}, u32[]{:S(2)}) collective-permute-start(bf16[4,16,512]{2,1,0:T(8,128)(2,1)} %get-tuple-element.21.refs_0_), channel_id=1, source_target_pairs={{0,2},{1,3},{2,0},{3,1},{4,6},{5,7},{6,4},{7,5},{8,10},{9,11},{10,... | collective-permute-start | bytes 196616 | tf_op jit(solution)/shard_map/ppermute | solution.py:222
  24.6 0.1 collective-permute-done.8
  24.7 3.2 %collective-permute-start.7 = (bf16[4,16,512]{2,1,0:T(8,128)(2,1)}, bf16[4,16,512]{2,1,0:T(8,128)(2,1)S(1)}, u32[]{:S(2)}, u32[]{:S(2)}) collective-permute-start(bf16[4,16,512]{2,1,0:T(8,128)(2,1)} %get-tuple-element.21.refs_0_), channel_id=1, source_target_pairs={{0,3},{1,2},{2,1},{3,0},{4,7},{5,6},{6,5},{7,4},{8,11},{9,10},{10,... | collective-permute-start | bytes 196616 | tf_op jit(solution)/shard_map/ppermute | solution.py:222
  27.9 0.8 %add.8.sums_ref = f32[3,8,512]{2,1,0:T(8,128)S(1)} add(f32[3,8,512]{2,1,0:T(8,128)} %get-tuple-element.22, f32[3,8,512]{2,1,0:T(8,128)S(1)} %collective-permute-done.8) | non-fusion elementwise | flops 12288 | bytes 147456 | tf_op jit(solution)/shard_map/add | solution.py:261
  28.8 0.1 collective-permute-start.9
  28.8 0.9 %copy.13 = bf16[64,16,64]{2,1,0:T(8,128)(2,1)} copy(bf16[64,16,64]{2,0,1:T(8,128)(2,1)S(1)} %bitcast.9) | data formatting | bytes 262144 | tf_op jit(solution)/shard_map/transpose | solution.py:232
  29.7 0.6 %copy-done.8 = bf16[4,16,512]{2,1,0:T(8,128)(2,1)} copy-done((bf16[4,16,512]{2,1,0:T(8,128)(2,1)}, bf16[4,16,512]{2,1,0:T(8,128)(2,1)S(1)}, u32[]{:S(2)}) %copy-start.8) | copy-done | bytes 65560
  30.3 3.4 %shard_map.122.inner_ref = f32[4,16,512]{2,1,0:T(8,128)} custom-call(bf16[1024,64]{1,0:T(8,128)(2,1)} %bitcast.7, bf16[4,16,512]{2,1,0:T(8,128)(2,1)} %get-tuple-element.20.refs_0_, bf16[4,16,512]{2,1,0:T(8,128)(2,1)} %copy-done.6, bf16[4,16,512]{2,1,0:T(8,128)(2,1)} %copy-done.3, bf16[4,16,512]{2,1,0:T(8,128)(2,1)} %copy-done.8), custom_call_target="tpu_custom_call" | custom-call | tf_op jit(solution)/shard_map/pallas_call | solution.py:186
  33.7 0.0 collective-permute-done.5.refs_1_
  33.7 0.0 collective-permute-done.6.refs_2_
  33.8 0.6 %copy-done.4 = bf16[4,16,512]{2,1,0:T(8,128)(2,1)} copy-done((bf16[4,16,512]{2,1,0:T(8,128)(2,1)}, bf16[4,16,512]{2,1,0:T(8,128)(2,1)S(1)}, u32[]{:S(2)}) %copy-start.4) | copy-done | bytes 65560
  34.3 0.0 copy-done.5
  34.4 0.0 copy-done.7
  34.4 3.6 %shard_map.123 = f32[16,8,512]{2,1,0:T(8,128)} custom-call(bf16[1024,64]{1,0:T(8,128)(2,1)} %bitcast.8, f32[16,8,512]{2,1,0:T(8,128)} %get-tuple-element.19.adv_ref, f32[4,16,512]{2,1,0:T(8,128)} %shard_map.122.inner_ref, bf16[4,16,512]{2,1,0:T(8,128)(2,1)} %get-tuple-element.21.refs_0_, bf16[4,16,512]{2,1,0:T(8,128)(2,1)} %copy-done.4, ...), custom_call_target="tpu_custom_call" | custom-call | tf_op jit(solution)/shard_map/pallas_call | solution.py:186
  38.0 0.0 collective-permute-done.9.more_ref
  38.0 0.6 %copy-done.11 = f32[3,8,512]{2,1,0:T(8,128)} copy-done((f32[3,8,512]{2,1,0:T(8,128)}, f32[3,8,512]{2,1,0:T(8,128)S(1)}, u32[]{:S(2)}) %copy-start.11) | copy-done | bytes 49176
  38.7 2.0 %shard_map.124 = (f32[16,8,512]{2,1,0:T(8,128)}, f32[16,8,512]{2,1,0:T(8,128)}, f32[8,512]{1,0:T(8,128)}, f32[8,512]{1,0:T(8,128)}) custom-call(f32[3,16]{1,0:T(4,128)} %pad_maximum_fusion.scal_ref, f32[3,8,512]{2,1,0:T(8,128)} %copy-done.1, f32[3,8,512]{2,1,0:T(8,128)} %copy-done.11, f32[8,512]{1,0:T(8,128)} %gas_ref.1, f32[8,512]{1,0:T(8,128)} %gvr_ref.1, ...), custom_call_target="tpu_custom_call" | custom-call | tf_op jit(solution)/shard_map/pallas_call | solution.py:186
  (25 shorter events, 0.1 us)
Async XLA Ops:
  2.5 13.8 %collective-permute-start = (bf16[3,16,512]{2,1,0:T(8,128)(2,1)}, bf16[3,16,512]{2,1,0:T(8,128)(2,1)S(1)}, u32[]{:S(2)}, u32[]{:S(2)}) collective-permute-start(bf16[3,16,512]{2,1,0:T(8,128)(2,1)} %get-tuple-element.17), channel_id=1, source_target_pairs={{0,4},{4,0},{8,12},{12,8},{16,20},{20,16},{24,28},{28,24},{1,5},{5... | collective-permute-start | bytes 147464 | tf_op jit(solution)/shard_map/ppermute | solution.py:238
  3.0 13.4 %collective-permute-start.1 = (bf16[3,16,512]{2,1,0:T(8,128)(2,1)}, bf16[3,16,512]{2,1,0:T(8,128)(2,1)S(1)}, u32[]{:S(2)}, u32[]{:S(2)}) collective-permute-start(bf16[3,16,512]{2,1,0:T(8,128)(2,1)} %get-tuple-element.18), channel_id=1, source_target_pairs={{0,28},{28,0},{4,8},{8,4},{12,16},{16,12},{20,24},{24,20},{1,29},{... | collective-permute-start | bytes 147464 | tf_op jit(solution)/shard_map/ppermute | solution.py:237
  13.2 2.6 %copy-start.12 = (f32[16]{0:T(128)S(1)}, f32[16]{0:T(128)}, u32[]{:S(2)}) copy-start(f32[16]{0:T(128)} %param.14) | copy-start | bytes 196
  13.2 8.8 %collective-permute-start.3 = (bf16[4,16,512]{2,1,0:T(8,128)(2,1)}, bf16[4,16,512]{2,1,0:T(8,128)(2,1)S(1)}, u32[]{:S(2)}, u32[]{:S(2)}) collective-permute-start(bf16[4,16,512]{2,1,0:T(8,128)(2,1)} %get-tuple-element.20.refs_0_), channel_id=1, source_target_pairs={{0,2},{1,3},{2,0},{3,1},{4,6},{5,7},{6,4},{7,5},{8,10},{9,11},{10,... | collective-permute-start | bytes 196616 | tf_op jit(solution)/shard_map/ppermute | solution.py:215
  16.4 0.6 %copy-start.9 = (bf16[3,16,512]{2,1,0:T(8,128)(2,1)}, bf16[3,16,512]{2,1,0:T(8,128)(2,1)S(1)}, u32[]{:S(2)}) copy-start(bf16[3,16,512]{2,1,0:T(8,128)(2,1)S(1)} %collective-permute-done.from_a_ref) | copy-start | bytes 147460
  16.4 0.6 %copy-start.10 = (bf16[3,16,512]{2,1,0:T(8,128)(2,1)}, bf16[3,16,512]{2,1,0:T(8,128)(2,1)S(1)}, u32[]{:S(2)}) copy-start(bf16[3,16,512]{2,1,0:T(8,128)(2,1)S(1)} %collective-permute-done.1.from_b_ref) | copy-start | bytes 147460
  17.0 4.5 %copy-start.2 = (bf16[4,16,512]{2,1,0:T(8,128)(2,1)S(1)}, bf16[4,16,512]{2,1,0:T(8,128)(2,1)}, u32[]{:S(2)}) copy-start(bf16[4,16,512]{2,1,0:T(8,128)(2,1)} %get-tuple-element.20.refs_0_) | copy-start | bytes 196612
  17.0 11.8 %copy-start = (bf16[16,64,64]{2,1,0:T(8,128)(2,1)S(1)}, bf16[16,64,64]{2,1,0:T(8,128)(2,1)}, u32[]{:S(2)}) copy-start(bf16[16,64,64]{2,1,0:T(8,128)(2,1)} %param.15) | copy-start | bytes 393220
  19.9 4.8 %collective-permute-start.8 = (f32[3,8,512]{2,1,0:T(8,128)}, f32[3,8,512]{2,1,0:T(8,128)S(1)}, u32[]{:S(2)}, u32[]{:S(2)}) collective-permute-start(f32[3,8,512]{2,1,0:T(8,128)} %get-tuple-element.22), channel_id=1, source_target_pairs={{0,1},{1,0},{2,3},{3,2},{4,5},{5,4},{6,7},{7,6},{8,9},{9,8},{10,11... | collective-permute-start | bytes 147464 | tf_op jit(solution)/shard_map/ppermute | solution.py:257
  21.5 7.2 %collective-permute-start.2 = (bf16[4,16,512]{2,1,0:T(8,128)(2,1)S(1)}, bf16[4,16,512]{2,1,0:T(8,128)(2,1)S(1)}, u32[]{:S(2)}, u32[]{:S(2)}) collective-permute-start(bf16[4,16,512]{2,1,0:T(8,128)(2,1)S(1)} %copy-done.2), channel_id=1, source_target_pairs={{0,1},{1,0},{2,3},{3,2},{4,5},{5,4},{6,7},{7,6},{8,9},{9,8},{10,11... | collective-permute-start | bytes 196616 | tf_op jit(solution)/shard_map/ppermute | solution.py:215
  21.9 6.8 %copy-start.3 = (bf16[4,16,512]{2,1,0:T(8,128)(2,1)}, bf16[4,16,512]{2,1,0:T(8,128)(2,1)S(1)}, u32[]{:S(2)}) copy-start(bf16[4,16,512]{2,1,0:T(8,128)(2,1)S(1)} %collective-permute-done.3.refs_2_) | copy-start | bytes 196612
  21.9 7.8 %collective-permute-start.4 = (bf16[4,16,512]{2,1,0:T(8,128)(2,1)S(1)}, bf16[4,16,512]{2,1,0:T(8,128)(2,1)S(1)}, u32[]{:S(2)}, u32[]{:S(2)}) collective-permute-start(bf16[4,16,512]{2,1,0:T(8,128)(2,1)S(1)} %collective-permute-done.3.refs_2_), channel_id=1, source_target_pairs={{0,1},{1,0},{2,3},{3,2},{4,5},{5,4},{6,7},{7,6},{8,9},{9,8},{10,11... | collective-permute-start | bytes 196616 | tf_op jit(solution)/shard_map/ppermute | solution.py:215
  23.5 10.2 %collective-permute-start.5 = (bf16[4,16,512]{2,1,0:T(8,128)(2,1)}, bf16[4,16,512]{2,1,0:T(8,128)(2,1)S(1)}, u32[]{:S(2)}, u32[]{:S(2)}) collective-permute-start(bf16[4,16,512]{2,1,0:T(8,128)(2,1)} %get-tuple-element.21.refs_0_), channel_id=1, source_target_pairs={{0,1},{1,0},{2,3},{3,2},{4,5},{5,4},{6,7},{7,6},{8,9},{9,8},{10,11... | collective-permute-start | bytes 196616 | tf_op jit(solution)/shard_map/ppermute | solution.py:222
  24.0 9.8 %collective-permute-start.6 = (bf16[4,16,512]{2,1,0:T(8,128)(2,1)}, bf16[4,16,512]{2,1,0:T(8,128)(2,1)S(1)}, u32[]{:S(2)}, u32[]{:S(2)}) collective-permute-start(bf16[4,16,512]{2,1,0:T(8,128)(2,1)} %get-tuple-element.21.refs_0_), channel_id=1, source_target_pairs={{0,2},{1,3},{2,0},{3,1},{4,6},{5,7},{6,4},{7,5},{8,10},{9,11},{10,... | collective-permute-start | bytes 196616 | tf_op jit(solution)/shard_map/ppermute | solution.py:222
  24.7 9.0 %collective-permute-start.7 = (bf16[4,16,512]{2,1,0:T(8,128)(2,1)}, bf16[4,16,512]{2,1,0:T(8,128)(2,1)S(1)}, u32[]{:S(2)}, u32[]{:S(2)}) collective-permute-start(bf16[4,16,512]{2,1,0:T(8,128)(2,1)} %get-tuple-element.21.refs_0_), channel_id=1, source_target_pairs={{0,3},{1,2},{2,1},{3,0},{4,7},{5,6},{6,5},{7,4},{8,11},{9,10},{10,... | collective-permute-start | bytes 196616 | tf_op jit(solution)/shard_map/ppermute | solution.py:222
  28.7 1.0 %copy-start.1 = (f32[3,8,512]{2,1,0:T(8,128)}, f32[3,8,512]{2,1,0:T(8,128)S(1)}, u32[]{:S(2)}) copy-start(f32[3,8,512]{2,1,0:T(8,128)S(1)} %add.8.sums_ref) | copy-start | bytes 147460
  28.7 1.0 %copy-start.6 = (bf16[4,16,512]{2,1,0:T(8,128)(2,1)}, bf16[4,16,512]{2,1,0:T(8,128)(2,1)S(1)}, u32[]{:S(2)}) copy-start(bf16[4,16,512]{2,1,0:T(8,128)(2,1)S(1)} %collective-permute-done.2.refs_1_) | copy-start | bytes 196612
  28.8 9.3 %collective-permute-start.9 = (f32[3,8,512]{2,1,0:T(8,128)S(1)}, f32[3,8,512]{2,1,0:T(8,128)S(1)}, u32[]{:S(2)}, u32[]{:S(2)}) collective-permute-start(f32[3,8,512]{2,1,0:T(8,128)S(1)} %add.8.sums_ref), channel_id=1, source_target_pairs={{0,2},{1,3},{2,0},{3,1},{4,6},{5,7},{6,4},{7,5},{8,10},{9,11},{10,... | collective-permute-start | bytes 147464 | tf_op jit(solution)/shard_map/ppermute | solution.py:257
  29.7 0.6 %copy-start.8 = (bf16[4,16,512]{2,1,0:T(8,128)(2,1)}, bf16[4,16,512]{2,1,0:T(8,128)(2,1)S(1)}, u32[]{:S(2)}) copy-start(bf16[4,16,512]{2,1,0:T(8,128)(2,1)S(1)} %collective-permute-done.4.refs_3_) | copy-start | bytes 196612
  33.7 0.6 %copy-start.4 = (bf16[4,16,512]{2,1,0:T(8,128)(2,1)}, bf16[4,16,512]{2,1,0:T(8,128)(2,1)S(1)}, u32[]{:S(2)}) copy-start(bf16[4,16,512]{2,1,0:T(8,128)(2,1)S(1)} %collective-permute-done.5.refs_1_) | copy-start | bytes 196612
  33.7 0.6 %copy-start.5 = (bf16[4,16,512]{2,1,0:T(8,128)(2,1)}, bf16[4,16,512]{2,1,0:T(8,128)(2,1)S(1)}, u32[]{:S(2)}) copy-start(bf16[4,16,512]{2,1,0:T(8,128)(2,1)S(1)} %collective-permute-done.6.refs_2_) | copy-start | bytes 196612
  33.7 0.6 %copy-start.7 = (bf16[4,16,512]{2,1,0:T(8,128)(2,1)}, bf16[4,16,512]{2,1,0:T(8,128)(2,1)S(1)}, u32[]{:S(2)}) copy-start(bf16[4,16,512]{2,1,0:T(8,128)(2,1)S(1)} %collective-permute-done.7.refs_3_) | copy-start | bytes 196612
  38.0 0.6 %copy-start.11 = (f32[3,8,512]{2,1,0:T(8,128)}, f32[3,8,512]{2,1,0:T(8,128)S(1)}, u32[]{:S(2)}) copy-start(f32[3,8,512]{2,1,0:T(8,128)S(1)} %collective-permute-done.9.more_ref) | copy-start | bytes 147460

commit v2 on v1

--- a/solution.py
+++ b/solution.py
@@ -80,7 +80,7 @@
         adv_ref[b] = base - COURANT * radial(q, vr_ref[b], none, none)
         return carry
 
-    lax.fori_loop(0, bins, one_bin, 0)
+    lax.fori_loop(0, bins, one_bin, 0, unroll=True)
     for n in range(rows - 2 * HALO):
         low_ref[n] = adv_ref[:, HALO + n, :].astype(BF16)
 
@@ -107,7 +107,7 @@
         return (sums[0] + weight * vr, sums[1] + weight * va_ref[b], sums[2] + weight)
 
     zero = jnp.zeros(shape, F32)
-    sums = lax.fori_loop(0, bins, one_bin, (zero, zero, zero))
+    sums = lax.fori_loop(0, bins, one_bin, (zero, zero, zero), unroll=True)
     for n in range(3):
         sums_ref[n] = sums[n]
     for n, r in enumerate(edge_rows(rows)):
@@ -182,14 +182,16 @@
     return jax.ShapeDtypeStruct(shape, dtype)
 
 
-def call(kernel, outs, specs, *args, scratch=()):
+def call(kernel, outs, *args, scratch=(), scalars=0):
+    specs = [SMEM] * scalars + [VMEM] * (len(args) - scalars)
+    placed = [x if n < scalars else pltpu.with_memory_space_constraint(x, pltpu.VMEM) for n, x in enumerate(args)]
     return pl.pallas_call(
         kernel,
         out_shape=outs,
         in_specs=specs,
-        out_specs=jax.tree.map(lambda _: VMEM, outs),
+        out_specs=jax.tree.map(lambda _: VMEM, outs, is_leaf=lambda x: hasattr(x, "dtype")),
         scratch_shapes=scratch,
-    )(*args)
+    )(*placed)
 
 
 def xor_pairs(axis, bit):
@@ -230,46 +232,41 @@
     rate = 1.0 / stop_time
     scal = jnp.stack([rate / (1.0 + rate), rate, 1.0 / (1.0 + rate)])
     coef_rows = jnp.transpose(coef, (1, 0, 2)).reshape(total * bins, total)
-    field = struct(rho.shape)
-
-    halo = struct((3, bins, cells), BF16)
-    to_a, to_b = call(edge_kernel, (halo, halo), [VMEM] * 2, rho, vr)
+    field, kept = struct(rho.shape), pltpu.VMEM(rho.shape, F32)
+    inner_low = pltpu.VMEM((inner_rows, bins, cells), BF16)
+    outer_low = pltpu.VMEM((outer_rows, bins, cells), BF16)
+
+    halo = pltpu.VMEM((3, bins, cells), BF16)
+    to_a, to_b = call(edge_kernel, (halo, halo), rho, vr)
     from_b = lax.ppermute(to_b, "tile", odd_pairs("tile"))
     from_a = lax.ppermute(to_a, "tile", even_pairs("tile"))
 
-    base, low_in = call(
-        inner_kernel, (field, struct((inner_rows, bins, cells), BF16)), [VMEM] * 3, rho, vr, va,
-        scratch=[pltpu.VMEM(rho.shape, F32)],
-    )
+    base, low_in = call(inner_kernel, (kept, inner_low), rho, vr, va, scratch=[pltpu.VMEM(rho.shape, F32)])
     parts_in = gather_bins(low_in)
 
     adv, low_out, sums = call(
-        outer_kernel, (field, struct((outer_rows, bins, cells), BF16), struct((3, rows, cells))),
-        [SMEM] + [VMEM] * 6, scal, rho, vr, va, base, from_a, from_b,
-        scratch=[pltpu.VMEM((3, bins, cells), F32)] * 2,
+        outer_kernel, (kept, outer_low, pltpu.VMEM((3, rows, cells), F32)), scal, rho, vr, va, base, from_a, from_b,
+        scratch=[pltpu.VMEM((3, bins, cells), F32)] * 2, scalars=1,
     )
     parts_out = gather_direct(low_out)
 
-    bit = lax.axis_size("bin") // 2
-    others = None
-    step = 1
-    while True:
+    step, last = 1, lax.axis_size("bin") // 2
+    others = lax.ppermute(sums, "bin", xor_pairs("bin", step))
+    while step < last:
+        step *= 2
+        sums = sums + others
         others = lax.ppermute(sums, "bin", xor_pairs("bin", step))
-        step *= 2
-        if step > bit:
-            break
-        sums = sums + others
     vr_out, va_out, gvr_out, gva_out = call(
-        drag_kernel, (field, field, struct(gas.shape), struct(gas.shape)), [SMEM] + [VMEM] * 7,
-        scal, sums, others, gas, gvr, gva, vr, va,
+        drag_kernel, (field, field, struct(gas.shape), struct(gas.shape)),
+        scal, sums, others, gas, gvr, gva, vr, va, scalars=1,
     )
 
     gain_in = call(
-        inner_gain_kernel, struct((inner_rows, bins, cells)), [VMEM] * (1 + len(parts_in)), coef_rows, *parts_in,
+        inner_gain_kernel, pltpu.VMEM((inner_rows, bins, cells), F32), coef_rows, *parts_in,
         scratch=[pltpu.VMEM((inner_rows, total, cells), BF16)],
     )
     density_out = call(
-        outer_gain_kernel, field, [VMEM] * (3 + len(parts_out)), coef_rows, adv, gain_in, *parts_out,
+        outer_gain_kernel, field, coef_rows, adv, gain_in, *parts_out,
         scratch=[pltpu.VMEM((outer_rows, total, cells), BF16), pltpu.VMEM((outer_rows, bins, cells), F32)],
     )
     return density_out, vr_out, va_out, gvr_out, gva_out

time: 40.9 us -> 30.1 us (0.74)
  Pallas kernels: 20.4 us -> 8.83 us
  waiting for transfers between devices: 0.14 us -> 2.07 us
  local copies, waits for them, and re-layouts: 3.38 us -> 2.1 us
  starting transfers between devices: 14.6 us -> 15.5 us
  other arithmetic: 1.43 us -> 0.62 us
    pallas_call x6, Pallas kernels: 20.4 us -> 8.83 us  [call(): pl.pallas_call(kernel, out_shape=outs, in_specs=specs, out_specs=jax.tree...]
    ppermute x3, waiting for transfers between devices: 0.01 us -> 2.06 us  [gather_direct(): lax.ppermute(x, 'bin', xor_pairs('bin', at))]
    add x1, other arithmetic: 0.81 us -> 0.01 us  [body(): sums = sums + others]
    transpose x1, local copies, waits for them, and re-layouts: 0.88 us -> 0.17 us  [body(): coef_rows = jnp.transpose(coef, (1, 0, 2)).reshape(total * bins, total)]
    ppermute x2, starting transfers between devices: 1.65 us -> 2.33 us  [body(): others = lax.ppermute(sums, 'bin', xor_pairs('bin', step))]
    unnamed x26 -> x18, local copies, waits for them, and re-layouts: 2.5 us -> 1.93 us
  transfers between devices with their start and end apart: 10 -> 10, of which waited for: 1 -> 1; matrix products, arithmetic and copies ran while one was open for 6% -> 3% of each run, Pallas kernels for 41% -> 24%
where the time goes in v2:
time: 30.1 us; the launch traced here: 29.9 us
  starting transfers between devices  15.5 us (51%)
  Pallas kernels  8.83 us (29%)
  local copies, waits for them, and re-layouts  2.1 us (7%)
  waiting for transfers between devices  2.07 us (7%)
  between operations  0.76 us (3%)
  other arithmetic  0.62 us (2%)
    pallas_call x6, Pallas kernels, call(): pl.pallas_call(kernel, out_shape=outs, in_specs=specs, out_specs=jax.tree...  8.83 us
    ppermute x3, starting transfers between devices, gather_bins(): lax.ppermute(part, 'bin', xor_pairs('bin', bit))  4.68 us
    ppermute x3, starting transfers between devices, gather_direct(): lax.ppermute(x, 'bin', xor_pairs('bin', at))  4.39 us
    ppermute x1, starting transfers between devices, body(): from_b = lax.ppermute(to_b, 'tile', odd_pairs('tile'))  3.54 us
    ppermute x2, starting transfers between devices, body(): others = lax.ppermute(sums, 'bin', xor_pairs('bin', step))  2.33 us
    ppermute x3, waiting for transfers between devices, gather_direct(): lax.ppermute(x, 'bin', xor_pairs('bin', at))  2.06 us
    unnamed x18, local copies, waits for them, and re-layouts  1.93 us
    another operation x3, other arithmetic, body(): scal = jnp.stack([rate / (1.0 + rate), rate, 1.0 / (1.0 + rate)])  0.61 us
  transfers between devices with their start and end apart: 10, of which 1 were waited for; matrix products, arithmetic and copies ran while one was open for 3% of the time, Pallas kernels for 24%

profile of v2, /device:TPU:0, one launch (start us, length us, event | category | flops | bytes accessed | tf_op | source)
XLA Modules:
  0.0 29.9 jit_solution(6513539738718849853)
XLA Ops:
  0.6 0.0 copy-start
  0.6 0.9 %copy-done = f32[16,8,512]{2,1,0:T(8,128)S(1)} copy-done((f32[16,8,512]{2,1,0:T(8,128)S(1)}, f32[16,8,512]{2,1,0:T(8,128)}, u32[]{:S(2)}) %copy-start) | copy-done | bytes 262168
  1.6 0.9 %copy-done.2 = f32[16,8,512]{2,1,0:T(8,128)S(1)} copy-done((f32[16,8,512]{2,1,0:T(8,128)S(1)}, f32[16,8,512]{2,1,0:T(8,128)}, u32[]{:S(2)}) %copy-start.2) | copy-done | bytes 262168
  2.5 0.3 shard_map.120
  2.8 0.6 %collective-permute-start = (bf16[3,16,512]{2,1,0:T(8,128)(2,1)S(1)}, bf16[3,16,512]{2,1,0:T(8,128)(2,1)S(1)}, u32[]{:S(2)}, u32[]{:S(2)}) collective-permute-start(bf16[3,16,512]{2,1,0:T(8,128)(2,1)S(1)} %get-tuple-element.17), channel_id=1, source_target_pairs={{0,4},{4,0},{8,12},{12,8},{16,20},{20,16},{24,28},{28,24},{1,5},{5... | collective-permute-start | bytes 147464 | tf_op jit(solution)/shard_map/ppermute | solution.py:242
  3.4 3.5 %collective-permute-start.1 = (bf16[3,16,512]{2,1,0:T(8,128)(2,1)S(1)}, bf16[3,16,512]{2,1,0:T(8,128)(2,1)S(1)}, u32[]{:S(2)}, u32[]{:S(2)}) collective-permute-start(bf16[3,16,512]{2,1,0:T(8,128)(2,1)S(1)} %get-tuple-element.18), channel_id=1, source_target_pairs={{0,28},{28,0},{4,8},{8,4},{12,16},{16,12},{20,24},{24,20},{1,29},{... | collective-permute-start | bytes 147464 | tf_op jit(solution)/shard_map/ppermute | solution.py:241
  6.9 1.2 %shard_map.119 = (f32[16,8,512]{2,1,0:T(8,128)S(1)}, bf16[4,16,512]{2,1,0:T(8,128)(2,1)S(1)}) custom-call(f32[16,8,512]{2,1,0:T(8,128)S(1)} %copy-done.2, f32[16,8,512]{2,1,0:T(8,128)S(1)} %copy-done, f32[16,8,512]{2,1,0:T(8,128)S(1)} %copy-done.3), custom_call_target="tpu_custom_call" | custom-call | tf_op jit(solution)/shard_map/pallas_call | solution.py:188
  8.1 0.0 copy-start.8
  8.2 2.7 %collective-permute-start.3 = (bf16[4,16,512]{2,1,0:T(8,128)(2,1)S(1)}, bf16[4,16,512]{2,1,0:T(8,128)(2,1)S(1)}, u32[]{:S(2)}, u32[]{:S(2)}) collective-permute-start(bf16[4,16,512]{2,1,0:T(8,128)(2,1)S(1)} %get-tuple-element.20.refs_0_), channel_id=1, source_target_pairs={{0,2},{1,3},{2,0},{3,1},{4,6},{5,7},{6,4},{7,5},{8,10},{9,11},{10,... | collective-permute-start | bytes 196616 | tf_op jit(solution)/shard_map/ppermute | solution.py:217
  10.8 0.6 %pad_maximum_fusion.scal_ref = f32[3,16]{1,0:T(4,128)} fusion(f32[1,16]{1,0:T(1,128)S(1)} %divide_bitcast_fusion, f32[1,16]{1,0:T(1,128)S(1)} %bitcast.10, f32[1,16]{1,0:T(1,128)S(1)} %get-tuple-element.27), kind=kLoop, calls=%fused_computation | loop fusion | flops 96 | bytes 384 | tf_op jit(solution)/shard_map/stack | solution.py:233
  11.4 0.0 collective-permute-done.from_a_ref
  11.4 0.0 collective-permute-done.1.from_b_ref
  11.4 1.6 %shard_map.121 = (f32[16,8,512]{2,1,0:T(8,128)S(1)}, bf16[4,16,512]{2,1,0:T(8,128)(2,1)S(1)}, f32[3,8,512]{2,1,0:T(8,128)S(1)}) custom-call(f32[3,16]{1,0:T(4,128)} %pad_maximum_fusion.scal_ref, f32[16,8,512]{2,1,0:T(8,128)S(1)} %copy-done.2, f32[16,8,512]{2,1,0:T(8,128)S(1)} %copy-done, f32[16,8,512]{2,1,0:T(8,128)S(1)} %copy-done.3, ...), custom_call_target="tpu_custom_call" | custom-call | tf_op jit(solution)/shard_map/pallas_call | solution.py:188
  13.0 1.6 %collective-permute-start.8 = (f32[3,8,512]{2,1,0:T(8,128)S(1)}, f32[3,8,512]{2,1,0:T(8,128)S(1)}, u32[]{:S(2)}, u32[]{:S(2)}) collective-permute-start(f32[3,8,512]{2,1,0:T(8,128)S(1)} %get-tuple-element.22), channel_id=1, source_target_pairs={{0,1},{1,0},{2,3},{3,2},{4,5},{5,4},{6,7},{7,6},{8,9},{9,8},{10,11... | collective-permute-start | bytes 147464 | tf_op jit(solution)/shard_map/ppermute | solution.py:254
  14.7 0.4 %collective-permute-start.2 = (bf16[4,16,512]{2,1,0:T(8,128)(2,1)S(1)}, bf16[4,16,512]{2,1,0:T(8,128)(2,1)S(1)}, u32[]{:S(2)}, u32[]{:S(2)}) collective-permute-start(bf16[4,16,512]{2,1,0:T(8,128)(2,1)S(1)} %get-tuple-element.20.refs_0_), channel_id=1, source_target_pairs={{0,1},{1,0},{2,3},{3,2},{4,5},{5,4},{6,7},{7,6},{8,9},{9,8},{10,11... | collective-permute-start | bytes 196616 | tf_op jit(solution)/shard_map/ppermute | solution.py:217
  15.1 0.0 collective-permute-done.3.refs_2_
  15.1 1.6 %collective-permute-start.4 = (bf16[4,16,512]{2,1,0:T(8,128)(2,1)S(1)}, bf16[4,16,512]{2,1,0:T(8,128)(2,1)S(1)}, u32[]{:S(2)}, u32[]{:S(2)}) collective-permute-start(bf16[4,16,512]{2,1,0:T(8,128)(2,1)S(1)} %collective-permute-done.3.refs_2_), channel_id=1, source_target_pairs={{0,1},{1,0},{2,3},{3,2},{4,5},{5,4},{6,7},{7,6},{8,9},{9,8},{10,11... | collective-permute-start | bytes 196616 | tf_op jit(solution)/shard_map/ppermute | solution.py:217
  16.7 0.4 %collective-permute-start.5 = (bf16[4,16,512]{2,1,0:T(8,128)(2,1)S(1)}, bf16[4,16,512]{2,1,0:T(8,128)(2,1)S(1)}, u32[]{:S(2)}, u32[]{:S(2)}) collective-permute-start(bf16[4,16,512]{2,1,0:T(8,128)(2,1)S(1)} %get-tuple-element.21.refs_0_), channel_id=1, source_target_pairs={{0,1},{1,0},{2,3},{3,2},{4,5},{5,4},{6,7},{7,6},{8,9},{9,8},{10,11... | collective-permute-start | bytes 196616 | tf_op jit(solution)/shard_map/ppermute | solution.py:224
  17.2 1.1 %collective-permute-start.6 = (bf16[4,16,512]{2,1,0:T(8,128)(2,1)S(1)}, bf16[4,16,512]{2,1,0:T(8,128)(2,1)S(1)}, u32[]{:S(2)}, u32[]{:S(2)}) collective-permute-start(bf16[4,16,512]{2,1,0:T(8,128)(2,1)S(1)} %get-tuple-element.21.refs_0_), channel_id=1, source_target_pairs={{0,2},{1,3},{2,0},{3,1},{4,6},{5,7},{6,4},{7,5},{8,10},{9,11},{10,... | collective-permute-start | bytes 196616 | tf_op jit(solution)/shard_map/ppermute | solution.py:224
  18.3 0.0 collective-permute-done.8
  18.3 2.8 %collective-permute-start.7 = (bf16[4,16,512]{2,1,0:T(8,128)(2,1)S(1)}, bf16[4,16,512]{2,1,0:T(8,128)(2,1)S(1)}, u32[]{:S(2)}, u32[]{:S(2)}) collective-permute-start(bf16[4,16,512]{2,1,0:T(8,128)(2,1)S(1)} %get-tuple-element.21.refs_0_), channel_id=1, source_target_pairs={{0,3},{1,2},{2,1},{3,0},{4,7},{5,6},{6,5},{7,4},{8,11},{9,10},{10,... | collective-permute-start | bytes 196616 | tf_op jit(solution)/shard_map/ppermute | solution.py:224
  21.1 0.0 collective-permute-done.2.refs_1_
  21.1 0.7 %collective-permute-start.9 = (f32[3,8,512]{2,1,0:T(8,128)S(1)}, f32[3,8,512]{2,1,0:T(8,128)S(1)}, u32[]{:S(2)}, u32[]{:S(2)}) collective-permute-start(f32[3,8,512]{2,1,0:T(8,128)S(1)} %add.8.sums_ref), channel_id=1, source_target_pairs={{0,2},{1,3},{2,0},{3,1},{4,6},{5,7},{6,4},{7,5},{8,10},{9,11},{10,... | collective-permute-start | bytes 147464 | tf_op jit(solution)/shard_map/ppermute | solution.py:258
  21.8 0.2 copy.13
  22.0 0.0 collective-permute-done.4.refs_3_
  22.0 1.7 %shard_map.122.inner_ref = f32[4,16,512]{2,1,0:T(8,128)S(1)} custom-call(bf16[1024,64]{1,0:T(8,128)(2,1)S(1)} %bitcast.7, bf16[4,16,512]{2,1,0:T(8,128)(2,1)S(1)} %get-tuple-element.20.refs_0_, bf16[4,16,512]{2,1,0:T(8,128)(2,1)S(1)} %collective-permute-done.2.refs_1_, bf16[4,16,512]{2,1,0:T(8,128)(2,1)S(1)} %collective-permute-done.3.refs_2_, ...), custom_call_target="tpu_custom_call" | custom-call | tf_op jit(solution)/shard_map/pallas_call | solution.py:188
  23.7 0.0 collective-permute-done.5.refs_1_
  23.7 2.0 %collective-permute-done.6.refs_2_ = bf16[4,16,512]{2,1,0:T(8,128)(2,1)S(1)} collective-permute-done((bf16[4,16,512]{2,1,0:T(8,128)(2,1)S(1)}, bf16[4,16,512]{2,1,0:T(8,128)(2,1)S(1)}, u32[]{:S(2)}, u32[]{:S(2)}) %collective-permute-start.6) | collective-permute-done | bytes 65568 | tf_op jit(solution)/shard_map/ppermute | solution.py:224
  25.8 0.0 collective-permute-done.7.refs_3_
  25.8 0.0 copy-start.6
  25.8 2.5 %shard_map.123 = f32[16,8,512]{2,1,0:T(8,128)} custom-call(bf16[1024,64]{1,0:T(8,128)(2,1)S(1)} %bitcast.8, f32[16,8,512]{2,1,0:T(8,128)S(1)} %get-tuple-element.19.adv_ref, f32[4,16,512]{2,1,0:T(8,128)S(1)} %shard_map.122.inner_ref, bf16[4,16,512]{2,1,0:T(8,128)(2,1)S(1)} %get-tuple-element.21.refs_0_, ...), custom_call_target="tpu_custom_call" | custom-call | tf_op jit(solution)/shard_map/pallas_call | solution.py:188
  28.4 1.5 %shard_map.124 = (f32[16,8,512]{2,1,0:T(8,128)}, f32[16,8,512]{2,1,0:T(8,128)}, f32[8,512]{1,0:T(8,128)}, f32[8,512]{1,0:T(8,128)}) custom-call(f32[3,16]{1,0:T(4,128)} %pad_maximum_fusion.scal_ref, f32[3,8,512]{2,1,0:T(8,128)S(1)} %add.8.sums_ref, f32[3,8,512]{2,1,0:T(8,128)S(1)} %collective-permute-done.9.more_ref, f32[8,512]{1,0:T(8,128)S(1)} %copy-done.4, ...), custom_call_target="tpu_custom_call" | custom-call | tf_op jit(solution)/shard_map/pallas_call | solution.py:188
  (17 shorter events, 0.0 us)
Async XLA Ops:
  0.6 1.0 %copy-start = (f32[16,8,512]{2,1,0:T(8,128)S(1)}, f32[16,8,512]{2,1,0:T(8,128)}, u32[]{:S(2)}) copy-start(f32[16,8,512]{2,1,0:T(8,128)} %vr_ref.7) | copy-start | bytes 786436
  1.6 0.9 %copy-start.2 = (f32[16,8,512]{2,1,0:T(8,128)S(1)}, f32[16,8,512]{2,1,0:T(8,128)}, u32[]{:S(2)}) copy-start(f32[16,8,512]{2,1,0:T(8,128)} %rho_ref.5) | copy-start | bytes 786436
  2.5 4.4 %copy-start.3 = (f32[16,8,512]{2,1,0:T(8,128)S(1)}, f32[16,8,512]{2,1,0:T(8,128)}, u32[]{:S(2)}) copy-start(f32[16,8,512]{2,1,0:T(8,128)} %va_ref.5) | copy-start | bytes 786436
  2.8 8.6 %collective-permute-start = (bf16[3,16,512]{2,1,0:T(8,128)(2,1)S(1)}, bf16[3,16,512]{2,1,0:T(8,128)(2,1)S(1)}, u32[]{:S(2)}, u32[]{:S(2)}) collective-permute-start(bf16[3,16,512]{2,1,0:T(8,128)(2,1)S(1)} %get-tuple-element.17), channel_id=1, source_target_pairs={{0,4},{4,0},{8,12},{12,8},{16,20},{20,16},{24,28},{28,24},{1,5},{5... | collective-permute-start | bytes 147464 | tf_op jit(solution)/shard_map/ppermute | solution.py:242
  3.4 8.1 %collective-permute-start.1 = (bf16[3,16,512]{2,1,0:T(8,128)(2,1)S(1)}, bf16[3,16,512]{2,1,0:T(8,128)(2,1)S(1)}, u32[]{:S(2)}, u32[]{:S(2)}) collective-permute-start(bf16[3,16,512]{2,1,0:T(8,128)(2,1)S(1)} %get-tuple-element.18), channel_id=1, source_target_pairs={{0,28},{28,0},{4,8},{8,4},{12,16},{16,12},{20,24},{24,20},{1,29},{... | collective-permute-start | bytes 147464 | tf_op jit(solution)/shard_map/ppermute | solution.py:241
  8.1 2.7 %copy-start.8 = (f32[16]{0:T(128)S(1)}, f32[16]{0:T(128)}, u32[]{:S(2)}) copy-start(f32[16]{0:T(128)} %param.14) | copy-start | bytes 196
  8.2 7.0 %collective-permute-start.3 = (bf16[4,16,512]{2,1,0:T(8,128)(2,1)S(1)}, bf16[4,16,512]{2,1,0:T(8,128)(2,1)S(1)}, u32[]{:S(2)}, u32[]{:S(2)}) collective-permute-start(bf16[4,16,512]{2,1,0:T(8,128)(2,1)S(1)} %get-tuple-element.20.refs_0_), channel_id=1, source_target_pairs={{0,2},{1,3},{2,0},{3,1},{4,6},{5,7},{6,4},{7,5},{8,10},{9,11},{10,... | collective-permute-start | bytes 196616 | tf_op jit(solution)/shard_map/ppermute | solution.py:217
  11.4 10.4 %copy-start.7 = (bf16[16,64,64]{2,1,0:T(8,128)(2,1)S(1)}, bf16[16,64,64]{2,1,0:T(8,128)(2,1)}, u32[]{:S(2)}) copy-start(bf16[16,64,64]{2,1,0:T(8,128)(2,1)} %param.15) | copy-start | bytes 393220
  13.0 5.2 %collective-permute-start.8 = (f32[3,8,512]{2,1,0:T(8,128)S(1)}, f32[3,8,512]{2,1,0:T(8,128)S(1)}, u32[]{:S(2)}, u32[]{:S(2)}) collective-permute-start(f32[3,8,512]{2,1,0:T(8,128)S(1)} %get-tuple-element.22), channel_id=1, source_target_pairs={{0,1},{1,0},{2,3},{3,2},{4,5},{5,4},{6,7},{7,6},{8,9},{9,8},{10,11... | collective-permute-start | bytes 147464 | tf_op jit(solution)/shard_map/ppermute | solution.py:254
  14.7 6.4 %collective-permute-start.2 = (bf16[4,16,512]{2,1,0:T(8,128)(2,1)S(1)}, bf16[4,16,512]{2,1,0:T(8,128)(2,1)S(1)}, u32[]{:S(2)}, u32[]{:S(2)}) collective-permute-start(bf16[4,16,512]{2,1,0:T(8,128)(2,1)S(1)} %get-tuple-element.20.refs_0_), channel_id=1, source_target_pairs={{0,1},{1,0},{2,3},{3,2},{4,5},{5,4},{6,7},{7,6},{8,9},{9,8},{10,11... | collective-permute-start | bytes 196616 | tf_op jit(solution)/shard_map/ppermute | solution.py:217
  15.1 6.9 %collective-permute-start.4 = (bf16[4,16,512]{2,1,0:T(8,128)(2,1)S(1)}, bf16[4,16,512]{2,1,0:T(8,128)(2,1)S(1)}, u32[]{:S(2)}, u32[]{:S(2)}) collective-permute-start(bf16[4,16,512]{2,1,0:T(8,128)(2,1)S(1)} %collective-permute-done.3.refs_2_), channel_id=1, source_target_pairs={{0,1},{1,0},{2,3},{3,2},{4,5},{5,4},{6,7},{7,6},{8,9},{9,8},{10,11... | collective-permute-start | bytes 196616 | tf_op jit(solution)/shard_map/ppermute | solution.py:217
  16.7 7.0 %collective-permute-start.5 = (bf16[4,16,512]{2,1,0:T(8,128)(2,1)S(1)}, bf16[4,16,512]{2,1,0:T(8,128)(2,1)S(1)}, u32[]{:S(2)}, u32[]{:S(2)}) collective-permute-start(bf16[4,16,512]{2,1,0:T(8,128)(2,1)S(1)} %get-tuple-element.21.refs_0_), channel_id=1, source_target_pairs={{0,1},{1,0},{2,3},{3,2},{4,5},{5,4},{6,7},{7,6},{8,9},{9,8},{10,11... | collective-permute-start | bytes 196616 | tf_op jit(solution)/shard_map/ppermute | solution.py:224
  17.2 8.6 %collective-permute-start.6 = (bf16[4,16,512]{2,1,0:T(8,128)(2,1)S(1)}, bf16[4,16,512]{2,1,0:T(8,128)(2,1)S(1)}, u32[]{:S(2)}, u32[]{:S(2)}) collective-permute-start(bf16[4,16,512]{2,1,0:T(8,128)(2,1)S(1)} %get-tuple-element.21.refs_0_), channel_id=1, source_target_pairs={{0,2},{1,3},{2,0},{3,1},{4,6},{5,7},{6,4},{7,5},{8,10},{9,11},{10,... | collective-permute-start | bytes 196616 | tf_op jit(solution)/shard_map/ppermute | solution.py:224
  18.3 7.5 %collective-permute-start.7 = (bf16[4,16,512]{2,1,0:T(8,128)(2,1)S(1)}, bf16[4,16,512]{2,1,0:T(8,128)(2,1)S(1)}, u32[]{:S(2)}, u32[]{:S(2)}) collective-permute-start(bf16[4,16,512]{2,1,0:T(8,128)(2,1)S(1)} %get-tuple-element.21.refs_0_), channel_id=1, source_target_pairs={{0,3},{1,2},{2,1},{3,0},{4,7},{5,6},{6,5},{7,4},{8,11},{9,10},{10,... | collective-permute-start | bytes 196616 | tf_op jit(solution)/shard_map/ppermute | solution.py:224
  21.1 7.2 %collective-permute-start.9 = (f32[3,8,512]{2,1,0:T(8,128)S(1)}, f32[3,8,512]{2,1,0:T(8,128)S(1)}, u32[]{:S(2)}, u32[]{:S(2)}) collective-permute-start(f32[3,8,512]{2,1,0:T(8,128)S(1)} %add.8.sums_ref), channel_id=1, source_target_pairs={{0,2},{1,3},{2,0},{3,1},{4,6},{5,7},{6,4},{7,5},{8,10},{9,11},{10,... | collective-permute-start | bytes 147464 | tf_op jit(solution)/shard_map/ppermute | solution.py:258
  25.8 2.6 %copy-start.1 = (f32[16,8,512]{2,1,0:T(8,128)S(1)}, f32[16,8,512]{2,1,0:T(8,128)}, u32[]{:S(2)}) copy-start(f32[16,8,512]{2,1,0:T(8,128)} %vr_ref.7) | copy-start | bytes 786436
  25.8 2.6 %copy-start.4 = (f32[8,512]{1,0:T(8,128)S(1)}, f32[8,512]{1,0:T(8,128)}, u32[]{:S(2)}) copy-start(f32[8,512]{1,0:T(8,128)} %gas_ref.1) | copy-start | bytes 49156
  25.8 2.6 %copy-start.5 = (f32[8,512]{1,0:T(8,128)S(1)}, f32[8,512]{1,0:T(8,128)}, u32[]{:S(2)}) copy-start(f32[8,512]{1,0:T(8,128)} %gvr_ref.1) | copy-start | bytes 49156
  25.8 2.6 %copy-start.6 = (f32[8,512]{1,0:T(8,128)S(1)}, f32[8,512]{1,0:T(8,128)}, u32[]{:S(2)}) copy-start(f32[8,512]{1,0:T(8,128)} %gva_ref.1) | copy-start | bytes 49156

commit v3 on v2

v3 whole, which is shorter than its diff:
```python
import functools

import jax
import jax.numpy as jnp
from jax import lax
from jax.experimental import pallas as pl
from jax.experimental.pallas import tpu as pltpu
from jax.sharding import PartitionSpec as P

COURANT = 0.2
COAGULATION = 0.5
HALO = 2
F32 = jnp.float32
BF16 = jnp.bfloat16

VMEM = pl.BlockSpec(memory_space=pltpu.VMEM)
ANY = pl.BlockSpec(memory_space=pl.ANY)


def minmod(a, b):
    return jnp.maximum(jnp.minimum(a, b), 0.0) + jnp.minimum(jnp.maximum(a, b), 0.0)


def face_flux(low, low_slope, high, high_slope, u):
    cu = COURANT * u
    left = low + (0.5 - 0.5 * cu) * low_slope
    right = high - (0.5 + 0.5 * cu) * high_slope
    return jnp.maximum(u, 0.0) * left + jnp.minimum(u, 0.0) * right


def shift(x, by, axis):
    return pltpu.roll(x, by % x.shape[axis], axis)


def load_kernel(rho_in, vr_in, va_in, stop_in, to_a_ref, to_b_ref, rho_ref, vr_ref, va_ref, table_ref, stop_ref, stop_sem, sems):
    bins, rows, cells = rho_ref.shape
    pieces = sems.shape[1]
    part = bins // pieces
    stop_copy = pltpu.make_async_copy(stop_in, stop_ref, stop_sem)
    stop_copy.start()
    copies = []
    for f, (source, target) in enumerate(((rho_in, rho_ref), (vr_in, vr_ref), (va_in, va_ref))):
        for p in range(pieces):
            at = pl.ds(p * part, part)
            copies.append(pltpu.make_async_copy(source.at[at], target.at[at], sems.at[f, p]))
    for copy in copies:
        copy.start()
    stop_copy.wait()
    square = (bins, bins)
    own = lax.broadcasted_iota(jnp.int32, square, 0) == lax.broadcasted_iota(jnp.int32, square, 1)
    stop = jnp.sum(jnp.where(own, jnp.broadcast_to(stop_ref[...], square), 0.0), axis=1, keepdims=True)
    rate = 1.0 / stop
    scale = 1.0 / (1.0 + rate)
    table_ref[0] = jnp.broadcast_to(rate * scale, (bins, cells))
    table_ref[1] = jnp.broadcast_to(scale, (bins, cells))
    for copy in copies[:2 * pieces]:
        copy.wait()
    even = lax.axis_index("tile") % 2 == 0
    up = (rho_ref[:, 0, :], rho_ref[:, 1, :], vr_ref[:, 0, :])
    down = (rho_ref[:, rows - 1, :], rho_ref[:, rows - 2, :], vr_ref[:, rows - 1, :])
    for n in range(3):
        to_a_ref[n] = jnp.where(even, down[n], up[n]).astype(BF16)
        to_b_ref[n] = jnp.where(even, up[n], down[n]).astype(BF16)
    for copy in copies[2 * pieces:]:
        copy.wait()


def radial(q, v, top, bottom):
    rows = q.shape[0]
    row = lax.broadcasted_iota(jnp.int32, q.shape, 0)
    first, last = row == 0, row == rows - 1
    q_next = jnp.where(last, bottom[0], shift(q, -1, 0))
    q_prev = jnp.where(first, top[0], shift(q, 1, 0))
    v_next = jnp.where(last, bottom[2], shift(v, -1, 0))
    v_prev = jnp.where(first, top[2], shift(v, 1, 0))
    d_next = q_next - q
    d_prev = q - q_prev
    s = minmod(d_prev, d_next)
    s_top = minmod(top[0] - top[1], d_prev)
    s_bottom = minmod(d_next, bottom[1] - bottom[0])
    s_prev = jnp.where(first, s_top, shift(s, 1, 0))
    s_next = jnp.where(last, s_bottom, shift(s, -1, 0))
    out = face_flux(q, s, q_next, s_next, 0.5 * (v + v_next))
    into = face_flux(q_prev, s_prev, q, s, 0.5 * (v_prev + v))
    return out - into


def azimuthal(q, v):
    q_next = shift(q, -1, 1)
    d = q_next - q
    s = minmod(shift(d, 1, 1), d)
    flux = face_flux(q, s, q_next, shift(s, -1, 1), 0.5 * (v + shift(v, -1, 1)))
    return flux - shift(flux, 1, 1)


def inner_rows(rows):
    return list(range(HALO, rows - HALO))


def outer_rows(rows):
    return list(range(HALO)) + list(range(rows - HALO, rows))


def lines_of(bins, picked):
    return (bins + 6) * len(picked)


def write_message(ref, start, picked, adv_ref, sums, halves_ref):
    bins, count = adv_ref.shape[0], len(picked)
    for n, r in enumerate(picked):
        ref[start + n * bins:start + (n + 1) * bins, :] = adv_ref[:, r, :].astype(BF16)
    for n in range(3):
        high = sums[n].astype(BF16).astype(F32)
        for half, value in enumerate((high, sums[n] - high)):
            for m, r in enumerate(picked):
                at = (2 * n + half) * count + m
                halves_ref[at:at + 1, :] = value[r:r + 1, :]
    ref[start + count * bins:start + lines_of(bins, picked), :] = halves_ref[...].astype(BF16)


def read_sums(ref, start, picked, bins, halves_ref, sums_ref):
    count = len(picked)
    halves_ref[...] = ref[start + count * bins:start + lines_of(bins, picked), :].astype(F32)
    for n in range(3):
        for m, r in enumerate(picked):
            high, low = 2 * n * count + m, (2 * n + 1) * count + m
            sums_ref[n, r:r + 1, :] = halves_ref[high:high + 1, :] + halves_ref[low:low + 1, :]


def weighed(sums, adv, vr, va, coupling):
    weight = adv * coupling
    return (sums[0] + weight * vr, sums[1] + weight * va, sums[2] + weight)


def inner_kernel(table_ref, rho_ref, vr_ref, va_ref, base_ref, message_ref, adv_ref, halves_ref):
    bins, rows, cells = rho_ref.shape
    zero = jnp.zeros((rows, cells), F32)
    none = (zero, zero, zero)
    sums = none
    for b in range(bins):
        q, vr, va = rho_ref[b], vr_ref[b], va_ref[b]
        base = q - COURANT * azimuthal(q, va)
        base_ref[b] = base
        adv = base - COURANT * radial(q, vr, none, none)
        adv_ref[b] = adv
        sums = weighed(sums, adv, vr, va, jnp.broadcast_to(table_ref[0, b:b + 1, :], q.shape))
    write_message(message_ref, 0, inner_rows(rows), adv_ref, sums, halves_ref)


def outer_kernel(table_ref, rho_ref, vr_ref, va_ref, base_ref, from_a_ref, from_b_ref, inner_ref, adv_ref, message_ref, both_ref, top_ref, bottom_ref, halves_ref):
    bins, rows, cells = rho_ref.shape
    tile, tiles = lax.axis_index("tile"), lax.axis_size("tile")
    even = tile % 2 == 0
    has_top = jnp.where(tile > 0, 1.0, 0.0)
    has_bottom = jnp.where(tile < tiles - 1, 1.0, 0.0)
    for n in range(3):
        a, b = from_a_ref[n].astype(F32), from_b_ref[n].astype(F32)
        top_ref[n] = jnp.where(even, b, a) * has_top
        bottom_ref[n] = jnp.where(even, a, b) * has_bottom
    shape = (rows, cells)
    zero = jnp.zeros(shape, F32)
    sums = (zero, zero, zero)
    for b in range(bins):
        top = tuple(jnp.broadcast_to(top_ref[n, b:b + 1, :], shape) for n in range(3))
        bottom = tuple(jnp.broadcast_to(bottom_ref[n, b:b + 1, :], shape) for n in range(3))
        vr = vr_ref[b]
        adv = base_ref[b] - COURANT * radial(rho_ref[b], vr, top, bottom)
        adv_ref[b] = adv
        sums = weighed(sums, adv, vr, va_ref[b], jnp.broadcast_to(table_ref[0, b:b + 1, :], shape))
    write_message(message_ref, 0, outer_rows(rows), adv_ref, sums, halves_ref)
    split = inner_ref.shape[0]
    both_ref[:split, :] = inner_ref[...]
    both_ref[split:, :] = message_ref[...]


def total_sums(at, offset, bit):
    if bit == 0:
        return at(offset)
    return total_sums(at, offset, bit // 2) + total_sums(at, offset ^ bit, bit // 2)


def drag_kernel(layout, table_ref, gas_ref, gvr_ref, gva_ref, vr_ref, va_ref, *refs):
    bins, rows, _ = vr_ref.shape
    count = len(layout[0])
    messages, (vr_out, va_out, gvr_out, gva_out, sums_ref, halves_in_ref, halves_out_ref) = refs[:-7], refs[-7:]
    for offset in range(count):
        for places, picked, halves_ref in ((layout[0], inner_rows(rows), halves_in_ref), (layout[1], outer_rows(rows), halves_out_ref)):
            which, start = places[offset]
            read_sums(messages[which], start, picked, bins, halves_ref, sums_ref.at[offset])
    sums = [total_sums(lambda o, n=n: sums_ref[o, n], 0, count // 2) for n in range(3)]
    gas = gas_ref[...]
    denom = gas + sums[2]
    new_r = (gas * gvr_ref[...] + sums[0]) / denom
    new_a = (gas * gva_ref[...] + sums[1]) / denom
    gvr_out[...] = new_r
    gva_out[...] = new_a
    for b in range(bins):
        coupling = jnp.broadcast_to(table_ref[0, b:b + 1, :], gas.shape)
        scale = jnp.broadcast_to(table_ref[1, b:b + 1, :], gas.shape)
        vr_out[b] = vr_ref[b] * scale + coupling * new_r
        va_out[b] = va_ref[b] * scale + coupling * new_a


def gather_low(places, messages, dens_ref, bins):
    here = lax.axis_index("bin")
    for offset, (which, start) in enumerate(places):
        at = pl.multiple_of((here ^ offset) * bins, bins)
        for n in range(dens_ref.shape[0]):
            dens_ref[n, pl.ds(at, bins), :] = messages[which][start + n * bins:start + (n + 1) * bins, :]


def gain_rows(coef_ref, dens_ref, gain_ref, bins, n_rows):
    total = dens_ref.shape[1]
    group = 8

    def one_row(n, carry):
        low = dens_ref[n]
        wide = low.astype(F32)
        acc = jnp.zeros((bins, low.shape[1]), F32)
        for i in range(0, total, group):
            inner = jnp.dot(coef_ref[i * bins:(i + group) * bins, :], low, preferred_element_type=F32)
            for g in range(group):
                acc = acc + inner[g * bins:(g + 1) * bins] * wide[i + g:i + g + 1]
        gain_ref[n] = acc
        return carry

    lax.fori_loop(0, n_rows, one_row, 0)


def inner_gain_kernel(places, coef_ref, *refs):
    messages, (gain_ref, dens_ref) = refs[:-2], refs[-2:]
    n_rows, bins, _ = gain_ref.shape
    gather_low(places, messages, dens_ref, bins)
    gain_rows(coef_ref, dens_ref, gain_ref, bins, n_rows)


def outer_gain_kernel(places, after_ref, coef_ref, adv_ref, inner_ref, *refs):
    del after_ref
    messages, (out_ref, dens_ref, gain_ref) = refs[:-3], refs[-3:]
    bins, rows, _ = adv_ref.shape
    picked = outer_rows(rows)
    gather_low(places, messages, dens_ref, bins)
    gain_rows(coef_ref, dens_ref, gain_ref, bins, len(picked))
    for n, r in enumerate(picked):
        out_ref[:, r, :] = adv_ref[:, r, :] + COAGULATION * gain_ref[n]
    for n, r in enumerate(inner_rows(rows)):
        out_ref[:, r, :] = adv_ref[:, r, :] + COAGULATION * inner_ref[n]


def struct(shape, dtype=F32):
    return jax.ShapeDtypeStruct(shape, dtype)


def call(kernel, outs, *args, scratch=(), remote=()):
    specs = [ANY if n in remote else VMEM for n in range(len(args))]
    placed = [x if n in remote else pltpu.with_memory_space_constraint(x, pltpu.VMEM) for n, x in enumerate(args)]
    return pl.pallas_call(
        kernel,
        out_shape=outs,
        in_specs=specs,
        out_specs=jax.tree.map(lambda _: VMEM, outs, is_leaf=lambda x: hasattr(x, "dtype")),
        scratch_shapes=scratch,
    )(*placed)


def xor_pairs(axis, bit):
    return [(i, i ^ bit) for i in range(lax.axis_size(axis))]


def even_pairs(axis):
    return xor_pairs(axis, 1)


def odd_pairs(axis):
    count = lax.axis_size(axis)
    pairs = [(0, count - 1), (count - 1, 0)]
    for i in range(1, count - 1, 2):
        pairs += [(i, i + 1), (i + 1, i)]
    return pairs


def body(rho, vr, va, gas, gvr, gva, stop_time, coef):
    bins, rows, cells = rho.shape
    total = coef.shape[1]
    inner, outer = inner_rows(rows), outer_rows(rows)
    coef_rows = jnp.transpose(coef, (1, 0, 2)).reshape(total * bins, total)
    field, kept = struct(rho.shape), pltpu.VMEM(rho.shape, F32)
    flat = struct(gas.shape)
    halo = pltpu.VMEM((3, bins, cells), BF16)
    inner_lines, outer_lines = lines_of(bins, inner), lines_of(bins, outer)
    halves_in, halves_out = (pltpu.VMEM((6 * len(picked), cells), F32) for picked in (inner, outer))

    pieces = 2
    to_a, to_b, rho, vr, va, table = call(
        load_kernel, (halo, halo, kept, kept, kept, pltpu.VMEM((2, bins, cells), F32)), rho, vr, va, stop_time[None],
        scratch=[pltpu.VMEM((1, bins), F32), pltpu.SemaphoreType.DMA, pltpu.SemaphoreType.DMA((3, pieces))],
        remote=(0, 1, 2, 3),
    )
    from_b = lax.ppermute(to_b, "tile", odd_pairs("tile"))
    from_a = lax.ppermute(to_a, "tile", even_pairs("tile"))

    groups = lax.axis_size("bin")
    half = groups // 2
    base, low_in = call(
        inner_kernel, (kept, pltpu.VMEM((inner_lines, cells), BF16)), table, rho, vr, va, scratch=[kept, halves_in],
    )
    far_in = lax.ppermute(low_in, "bin", xor_pairs("bin", half))

    adv, low_out, low_all = call(
        outer_kernel, (kept, pltpu.VMEM((outer_lines, cells), BF16), pltpu.VMEM((inner_lines + outer_lines, cells), BF16)),
        table, rho, vr, va, base, from_a, from_b, low_in,
        scratch=[pltpu.VMEM((3, bins, cells), F32)] * 2 + [halves_out],
    )
    far_out = [lax.ppermute(low_out, "bin", xor_pairs("bin", at)) for at in range(groups - 1, half - 1, -1)][::-1]
    near_all = [lax.ppermute(low_all, "bin", xor_pairs("bin", at)) for at in range(1, half)]
    passed_in = [lax.ppermute(far_in, "bin", xor_pairs("bin", at)) for at in range(1, half)]

    in_messages = [low_in] + near_all + [far_in] + passed_in
    in_places = [(n, 0) for n in range(groups)]
    out_messages = [low_out] + near_all + far_out
    out_places = [(n, inner_lines if 0 < n < half else 0) for n in range(groups)]
    drag_out = [(n if 0 < n < half else groups + (n - half + 1 if n else 0), start) for n, start in out_places]
    drag_messages = in_messages + [low_out] + far_out

    gain_in = call(
        functools.partial(inner_gain_kernel, in_places), pltpu.VMEM((len(inner), bins, cells), F32), coef_rows, *in_messages,
        scratch=[pltpu.VMEM((len(inner), total, cells), BF16)],
    )
    vr_out, va_out, gvr_out, gva_out = call(
        functools.partial(drag_kernel, (in_places, drag_out)), (field, field, flat, flat),
        table, gas, gvr, gva, vr, va, *drag_messages,
        scratch=[pltpu.VMEM((groups, 3, rows, cells), F32), halves_in, halves_out],
    )
    density_out = call(
        functools.partial(outer_gain_kernel, out_places), field, gvr_out, coef_rows, adv, gain_in, *out_messages,
        scratch=[pltpu.VMEM((len(outer), total, cells), BF16), pltpu.VMEM((len(outer), bins, cells), F32)],
        remote=(0,),
    )
    return density_out, vr_out, va_out, gvr_out, gva_out


def solution(mesh):
    field, flat = P("bin", "tile", None), P("tile", None)
    return jax.shard_map(
        body,
        mesh=mesh,
        in_specs=(field, field, field, flat, flat, flat, P("bin"), P("bin", None, None)),
        out_specs=(field, field, field, flat, flat),
        check_vma=False,
    )
```

time: 30.1 us -> 28.1 us (0.934)
  waiting for transfers between devices: 2.07 us -> 5.08 us
  starting transfers between devices: 15.5 us -> 13.3 us
  local copies, waits for them, and re-layouts: 2.1 us -> 0.19 us
  other arithmetic: 0.62 us -> 0 us
    ppermute x8 -> x5, waiting for transfers between devices: 2.07 us -> 5.08 us  [the longest x2 2.68 us: body(): lax.ppermute(low_out, 'bin', xor_pairs('bin', at))]
    ppermute x8 -> x5, starting transfers between devices: 11.4 us -> 9.2 us  [the longest x2 3.19 us: body(): lax.ppermute(low_out, 'bin', xor_pairs('bin', at))]
    unnamed x18 -> x8, local copies, waits for them, and re-layouts: 1.93 us -> 0.01 us
    another operation x3 -> x0, other arithmetic: 0.61 us -> none  [body(): scal = jnp.stack([rate / (1.0 + rate), rate, 1.0 / (1.0 + rate)])]
  transfers between devices with their start and end apart: 10 -> 7, of which waited for: 1 -> 4; matrix products, arithmetic and copies ran while one was open for 3% -> 1% of each run, Pallas kernels for 24% -> 14%
where the time goes in v3:
time: 28.1 us; the launch traced here: 27.9 us
  starting transfers between devices  13.3 us (47%)
  Pallas kernels  8.69 us (31%)
  waiting for transfers between devices  5.08 us (18%)
  between operations  0.68 us (2%)
    pallas_call x6, Pallas kernels, call(): pl.pallas_call(kernel, out_shape=outs, in_specs=specs, out_specs=jax.tree...  8.69 us
    ppermute x1, starting transfers between devices, body(): from_b = lax.ppermute(to_b, 'tile', odd_pairs('tile'))  3.54 us
    ppermute x2, starting transfers between devices, body(): lax.ppermute(low_out, 'bin', xor_pairs('bin', at))  3.19 us
    ppermute x2, waiting for transfers between devices, body(): lax.ppermute(low_out, 'bin', xor_pairs('bin', at))  2.68 us
    ppermute x1, starting transfers between devices, body(): far_in = lax.ppermute(low_in, 'bin', xor_pairs('bin', half))  2.65 us
    ppermute x1, waiting for transfers between devices, body(): lax.ppermute(far_in, 'bin', xor_pairs('bin', at))  1.85 us
    ppermute x1, starting transfers between devices, body(): lax.ppermute(far_in, 'bin', xor_pairs('bin', at))  1.71 us
    ppermute x1, starting transfers between devices, body(): lax.ppermute(low_all, 'bin', xor_pairs('bin', at))  1.64 us
  transfers between devices with their start and end apart: 7, of which 4 were waited for; matrix products, arithmetic and copies ran while one was open for 1% of the time, Pallas kernels for 14%

profile of v3, /device:TPU:0, one launch (start us, length us, event | category | flops | bytes accessed | tf_op | source)
XLA Modules:
  0.0 27.9 jit_solution(16077497025520110163)
XLA Ops:
  0.6 1.4 %shard_map.119 = (bf16[3,16,512]{2,1,0:T(8,128)(2,1)S(1)}, bf16[3,16,512]{2,1,0:T(8,128)(2,1)S(1)}, f32[16,8,512]{2,1,0:T(8,128)S(1)}, f32[16,8,512]{2,1,0:T(8,1...) custom-call(f32[16,8,512]{2,1,0:T(8,128)} %rho_in.1, f32[16,8,512]{2,1,0:T(8,128)} %vr_in.1, ...), custom_call_target="tpu_custom_call" | custom-call | tf_op jit(solution)/shard_map/pallas_call | solution.py:257
  2.1 0.6 %collective-permute-start = (bf16[3,16,512]{2,1,0:T(8,128)(2,1)S(1)}, bf16[3,16,512]{2,1,0:T(8,128)(2,1)S(1)}, u32[]{:S(2)}, u32[]{:S(2)}) collective-permute-start(bf16[3,16,512]{2,1,0:T(8,128)(2,1)S(1)} %get-tuple-element.26), channel_id=1, source_target_pairs={{0,4},{4,0},{8,12},{12,8},{16,20},{20,16},{24,28},{28,24},{1,5},{5... | collective-permute-start | bytes 147464 | tf_op jit(solution)/shard_map/ppermute | solution.py:300
  2.6 3.5 %collective-permute-start.1 = (bf16[3,16,512]{2,1,0:T(8,128)(2,1)S(1)}, bf16[3,16,512]{2,1,0:T(8,128)(2,1)S(1)}, u32[]{:S(2)}, u32[]{:S(2)}) collective-permute-start(bf16[3,16,512]{2,1,0:T(8,128)(2,1)S(1)} %get-tuple-element.27), channel_id=1, source_target_pairs={{0,28},{28,0},{4,8},{8,4},{12,16},{16,12},{20,24},{24,20},{1,29},{... | collective-permute-start | bytes 147464 | tf_op jit(solution)/shard_map/ppermute | solution.py:299
  6.2 1.3 %shard_map.120 = (f32[16,8,512]{2,1,0:T(8,128)S(1)}, bf16[88,512]{1,0:T(8,128)(2,1)S(1)}) custom-call(f32[2,16,512]{2,1,0:T(8,128)S(1)} %get-tuple-element.20.table_ref, f32[16,8,512]{2,1,0:T(8,128)S(1)} %get-tuple-element.23.rho_ref, f32[16,8,512]{2,1,0:T(8,128)S(1)} %get-tuple-element.21.vr_ref, f32[16,8,512]{2,1,0:T(8,128)S(1)} %get-tuple-element.22.va_ref), custom_call_target="tpu_custom_call" | custom-call | tf_op jit(solution)/shard_map/pallas_call | solution.py:257
  7.5 2.7 %collective-permute-start.3 = (bf16[88,512]{1,0:T(8,128)(2,1)S(1)}, bf16[88,512]{1,0:T(8,128)(2,1)S(1)}, u32[]{:S(2)}, u32[]{:S(2)}) collective-permute-start(bf16[88,512]{1,0:T(8,128)(2,1)S(1)} %get-tuple-element.24.inner_ref.refs_0_), channel_id=1, source_target_pairs={{0,2},{1,3},{2,0},{3,1},{4,6},{5,7},{6,4},{7,5},{8,10},{9,11},{10,... | collective-permute-start | bytes 270344 | tf_op jit(solution)/shard_map/ppermute | solution.py:307
  10.1 0.0 collective-permute-done.from_a_ref
  10.1 0.0 collective-permute-done.1.from_b_ref
  10.1 0.0 copy-start.3
  10.1 0.8 %shard_map.121 = (f32[16,8,512]{2,1,0:T(8,128)S(1)}, bf16[88,512]{1,0:T(8,128)(2,1)S(1)}, bf16[176,512]{1,0:T(8,128)(2,1)S(1)}) custom-call(f32[2,16,512]{2,1,0:T(8,128)S(1)} %get-tuple-element.20.table_ref, f32[16,8,512]{2,1,0:T(8,128)S(1)} %get-tuple-element.23.rho_ref, f32[16,8,512]{2,1,0:T(8,128)S(1)} %get-tuple-element.21.vr_ref, ...), custom_call_target="tpu_custom_call" | custom-call | tf_op jit(solution)/shard_map/pallas_call | solution.py:257
  11.0 1.6 %collective-permute-start.2 = (bf16[176,512]{1,0:T(8,128)(2,1)S(1)}, bf16[176,512]{1,0:T(8,128)(2,1)S(1)}, u32[]{:S(2)}, u32[]{:S(2)}) collective-permute-start(bf16[176,512]{1,0:T(8,128)(2,1)S(1)} %get-tuple-element.28), channel_id=1, source_target_pairs={{0,1},{1,0},{2,3},{3,2},{4,5},{5,4},{6,7},{7,6},{8,9},{9,8},{10,11... | collective-permute-start | bytes 540680 | tf_op jit(solution)/shard_map/ppermute | solution.py:315
  12.6 0.5 %collective-permute-done.3.refs_2_ = bf16[88,512]{1,0:T(8,128)(2,1)S(1)} collective-permute-done((bf16[88,512]{1,0:T(8,128)(2,1)S(1)}, bf16[88,512]{1,0:T(8,128)(2,1)S(1)}, u32[]{:S(2)}, u32[]{:S(2)}) %collective-permute-start.3) | collective-permute-done | bytes 90144 | tf_op jit(solution)/shard_map/ppermute | solution.py:307
  13.1 1.7 %collective-permute-start.4 = (bf16[88,512]{1,0:T(8,128)(2,1)S(1)}, bf16[88,512]{1,0:T(8,128)(2,1)S(1)}, u32[]{:S(2)}, u32[]{:S(2)}) collective-permute-start(bf16[88,512]{1,0:T(8,128)(2,1)S(1)} %collective-permute-done.3.refs_2_), channel_id=1, source_target_pairs={{0,1},{1,0},{2,3},{3,2},{4,5},{5,4},{6,7},{7,6},{8,9},{9,8},{10,11... | collective-permute-start | bytes 270344 | tf_op jit(solution)/shard_map/ppermute | solution.py:316
  14.9 3.2 %collective-permute-start.5 = (bf16[88,512]{1,0:T(8,128)(2,1)S(1)}, bf16[88,512]{1,0:T(8,128)(2,1)S(1)}, u32[]{:S(2)}, u32[]{:S(2)}) collective-permute-start(bf16[88,512]{1,0:T(8,128)(2,1)S(1)} %get-tuple-element.29.refs_4_.refs_0_), channel_id=1, source_target_pairs={{0,2},{1,3},{2,0},{3,1},{4,6},{5,7},{6,4},{7,5},{8,10},{9,11},{10,... | collective-permute-start | bytes 270344 | tf_op jit(solution)/shard_map/ppermute | solution.py:314
  18.1 0.0 collective-permute-start.6
  18.1 0.0 copy-done.3
  18.1 0.2 copy.13
  18.2 1.9 %collective-permute-done.4.refs_3_ = bf16[88,512]{1,0:T(8,128)(2,1)S(1)} collective-permute-done((bf16[88,512]{1,0:T(8,128)(2,1)S(1)}, bf16[88,512]{1,0:T(8,128)(2,1)S(1)}, u32[]{:S(2)}, u32[]{:S(2)}) %collective-permute-start.4) | collective-permute-done | bytes 90144 | tf_op jit(solution)/shard_map/ppermute | solution.py:316
  20.1 0.0 collective-permute-done.2.refs_1_
  20.1 0.0 copy-start
  20.1 0.0 copy-start.1
  20.1 0.0 copy-start.2
  20.1 1.7 %shard_map.123.inner_ref = f32[4,16,512]{2,1,0:T(8,128)S(1)} custom-call(bf16[1024,64]{1,0:T(8,128)(2,1)S(1)} %bitcast.3, bf16[88,512]{1,0:T(8,128)(2,1)S(1)} %get-tuple-element.24.inner_ref.refs_0_, bf16[176,512]{1,0:T(8,128)(2,1)S(1)} %collective-permute-done.2.refs_1_, bf16[88,512]{1,0:T(8,128)(2,1)S(1)} %collective-permute-done.3.refs_2_, ...), custom_call_target="tpu_custom_call" | custom-call | tf_op jit(solution)/shard_map/pallas_call | solution.py:257
  21.8 1.1 %collective-permute-done.5.refs_5_.refs_2_ = bf16[88,512]{1,0:T(8,128)(2,1)S(1)} collective-permute-done((bf16[88,512]{1,0:T(8,128)(2,1)S(1)}, bf16[88,512]{1,0:T(8,128)(2,1)S(1)}, u32[]{:S(2)}, u32[]{:S(2)}) %collective-permute-start.5) | collective-permute-done | bytes 90144 | tf_op jit(solution)/shard_map/ppermute | solution.py:314
  22.9 1.6 %collective-permute-done.6.refs_6_.refs_3_ = bf16[88,512]{1,0:T(8,128)(2,1)S(1)} collective-permute-done((bf16[88,512]{1,0:T(8,128)(2,1)S(1)}, bf16[88,512]{1,0:T(8,128)(2,1)S(1)}, u32[]{:S(2)}, u32[]{:S(2)}) %collective-permute-start.6) | collective-permute-done | bytes 90144 | tf_op jit(solution)/shard_map/ppermute | solution.py:314
  24.5 0.0 copy-done
  24.5 0.0 copy-done.1
  24.5 0.0 copy-done.2
  24.5 0.9 %shard_map.122 = (f32[16,8,512]{2,1,0:T(8,128)}, f32[16,8,512]{2,1,0:T(8,128)}, f32[8,512]{1,0:T(8,128)}, f32[8,512]{1,0:T(8,128)}) custom-call(f32[2,16,512]{2,1,0:T(8,128)S(1)} %get-tuple-element.20.table_ref, f32[8,512]{1,0:T(8,128)S(1)} %copy-done, f32[8,512]{1,0:T(8,128)S(1)} %copy-done.1, f32[8,512]{1,0:T(8,128)S(1)} %copy-done.2, ...), custom_call_target="tpu_custom_call" | custom-call | tf_op jit(solution)/shard_map/pallas_call | solution.py:257
  25.4 2.5 %shard_map.124 = f32[16,8,512]{2,1,0:T(8,128)} custom-call(f32[8,512]{1,0:T(8,128)} %get-tuple-element.18.after_ref, bf16[1024,64]{1,0:T(8,128)(2,1)S(1)} %bitcast.4, f32[16,8,512]{2,1,0:T(8,128)S(1)} %get-tuple-element.31.adv_ref, f32[4,16,512]{2,1,0:T(8,128)S(1)} %shard_map.123.inner_ref, bf16[88,512]{1,0:T(8,128)(2,1)S(1)} %get-tuple-element.29.refs_4_.refs_0_, ...), custom_call_target="tpu_custom_call" | custom-call | tf_op jit(solution)/shard_map/pallas_call | solution.py:257
Async XLA Ops:
  2.1 8.0 %collective-permute-start = (bf16[3,16,512]{2,1,0:T(8,128)(2,1)S(1)}, bf16[3,16,512]{2,1,0:T(8,128)(2,1)S(1)}, u32[]{:S(2)}, u32[]{:S(2)}) collective-permute-start(bf16[3,16,512]{2,1,0:T(8,128)(2,1)S(1)} %get-tuple-element.26), channel_id=1, source_target_pairs={{0,4},{4,0},{8,12},{12,8},{16,20},{20,16},{24,28},{28,24},{1,5},{5... | collective-permute-start | bytes 147464 | tf_op jit(solution)/shard_map/ppermute | solution.py:300
  2.6 7.5 %collective-permute-start.1 = (bf16[3,16,512]{2,1,0:T(8,128)(2,1)S(1)}, bf16[3,16,512]{2,1,0:T(8,128)(2,1)S(1)}, u32[]{:S(2)}, u32[]{:S(2)}) collective-permute-start(bf16[3,16,512]{2,1,0:T(8,128)(2,1)S(1)} %get-tuple-element.27), channel_id=1, source_target_pairs={{0,28},{28,0},{4,8},{8,4},{12,16},{16,12},{20,24},{24,20},{1,29},{... | collective-permute-start | bytes 147464 | tf_op jit(solution)/shard_map/ppermute | solution.py:299
  7.5 5.7 %collective-permute-start.3 = (bf16[88,512]{1,0:T(8,128)(2,1)S(1)}, bf16[88,512]{1,0:T(8,128)(2,1)S(1)}, u32[]{:S(2)}, u32[]{:S(2)}) collective-permute-start(bf16[88,512]{1,0:T(8,128)(2,1)S(1)} %get-tuple-element.24.inner_ref.refs_0_), channel_id=1, source_target_pairs={{0,2},{1,3},{2,0},{3,1},{4,6},{5,7},{6,4},{7,5},{8,10},{9,11},{10,... | collective-permute-start | bytes 270344 | tf_op jit(solution)/shard_map/ppermute | solution.py:307
  10.1 7.9 %copy-start.3 = (bf16[16,64,64]{2,1,0:T(8,128)(2,1)S(1)}, bf16[16,64,64]{2,1,0:T(8,128)(2,1)}, u32[]{:S(2)}) copy-start(bf16[16,64,64]{2,1,0:T(8,128)(2,1)} %param.15) | copy-start | bytes 393220
  11.0 9.1 %collective-permute-start.2 = (bf16[176,512]{1,0:T(8,128)(2,1)S(1)}, bf16[176,512]{1,0:T(8,128)(2,1)S(1)}, u32[]{:S(2)}, u32[]{:S(2)}) collective-permute-start(bf16[176,512]{1,0:T(8,128)(2,1)S(1)} %get-tuple-element.28), channel_id=1, source_target_pairs={{0,1},{1,0},{2,3},{3,2},{4,5},{5,4},{6,7},{7,6},{8,9},{9,8},{10,11... | collective-permute-start | bytes 540680 | tf_op jit(solution)/shard_map/ppermute | solution.py:315
  13.1 6.9 %collective-permute-start.4 = (bf16[88,512]{1,0:T(8,128)(2,1)S(1)}, bf16[88,512]{1,0:T(8,128)(2,1)S(1)}, u32[]{:S(2)}, u32[]{:S(2)}) collective-permute-start(bf16[88,512]{1,0:T(8,128)(2,1)S(1)} %collective-permute-done.3.refs_2_), channel_id=1, source_target_pairs={{0,1},{1,0},{2,3},{3,2},{4,5},{5,4},{6,7},{7,6},{8,9},{9,8},{10,11... | collective-permute-start | bytes 270344 | tf_op jit(solution)/shard_map/ppermute | solution.py:316
  14.9 8.0 %collective-permute-start.5 = (bf16[88,512]{1,0:T(8,128)(2,1)S(1)}, bf16[88,512]{1,0:T(8,128)(2,1)S(1)}, u32[]{:S(2)}, u32[]{:S(2)}) collective-permute-start(bf16[88,512]{1,0:T(8,128)(2,1)S(1)} %get-tuple-element.29.refs_4_.refs_0_), channel_id=1, source_target_pairs={{0,2},{1,3},{2,0},{3,1},{4,6},{5,7},{6,4},{7,5},{8,10},{9,11},{10,... | collective-permute-start | bytes 270344 | tf_op jit(solution)/shard_map/ppermute | solution.py:314
  18.1 6.4 %collective-permute-start.6 = (bf16[88,512]{1,0:T(8,128)(2,1)S(1)}, bf16[88,512]{1,0:T(8,128)(2,1)S(1)}, u32[]{:S(2)}, u32[]{:S(2)}) collective-permute-start(bf16[88,512]{1,0:T(8,128)(2,1)S(1)} %get-tuple-element.29.refs_4_.refs_0_), channel_id=1, source_target_pairs={{0,3},{1,2},{2,1},{3,0},{4,7},{5,6},{6,5},{7,4},{8,11},{9,10},{10,... | collective-permute-start | bytes 270344 | tf_op jit(solution)/shard_map/ppermute | solution.py:314
  20.1 4.4 %copy-start = (f32[8,512]{1,0:T(8,128)S(1)}, f32[8,512]{1,0:T(8,128)}, u32[]{:S(2)}) copy-start(f32[8,512]{1,0:T(8,128)} %gas_ref.1) | copy-start | bytes 49156
  20.1 4.4 %copy-start.1 = (f32[8,512]{1,0:T(8,128)S(1)}, f32[8,512]{1,0:T(8,128)}, u32[]{:S(2)}) copy-start(f32[8,512]{1,0:T(8,128)} %gvr_ref.1) | copy-start | bytes 49156
  20.1 4.4 %copy-start.2 = (f32[8,512]{1,0:T(8,128)S(1)}, f32[8,512]{1,0:T(8,128)}, u32[]{:S(2)}) copy-start(f32[8,512]{1,0:T(8,128)} %gva_ref.1) | copy-start | bytes 49156

commit v4 on v3

--- a/solution.py
+++ b/solution.py
@@ -7,9 +7,11 @@
 from jax.experimental.pallas import tpu as pltpu
 from jax.sharding import PartitionSpec as P
 
+
 COURANT = 0.2
 COAGULATION = 0.5
 HALO = 2
+SMALL_BYTES = 2**19
 F32 = jnp.float32
 BF16 = jnp.bfloat16
 
@@ -179,10 +181,9 @@
     return total_sums(at, offset, bit // 2) + total_sums(at, offset ^ bit, bit // 2)
 
 
-def drag_kernel(layout, table_ref, gas_ref, gvr_ref, gva_ref, vr_ref, va_ref, *refs):
+def drag(layout, table_ref, gas_ref, gvr_ref, gva_ref, vr_ref, va_ref, messages, vr_out, va_out, gvr_out, gva_out, sums_ref, halves_in_ref, halves_out_ref):
     bins, rows, _ = vr_ref.shape
     count = len(layout[0])
-    messages, (vr_out, va_out, gvr_out, gva_out, sums_ref, halves_in_ref, halves_out_ref) = refs[:-7], refs[-7:]
     for offset in range(count):
         for places, picked, halves_ref in ((layout[0], inner_rows(rows), halves_in_ref), (layout[1], outer_rows(rows), halves_out_ref)):
             which, start = places[offset]
@@ -201,64 +202,101 @@
         va_out[b] = va_ref[b] * scale + coupling * new_a
 
 
-def gather_low(places, messages, dens_ref, bins):
+def weights_kernel(rows_ref, swapped_ref, out_ref):
+    lines, total = rows_ref.shape
+    bins = lines // total
     here = lax.axis_index("bin")
-    for offset, (which, start) in enumerate(places):
-        at = pl.multiple_of((here ^ offset) * bins, bins)
-        for n in range(dens_ref.shape[0]):
-            dens_ref[n, pl.ds(at, bins), :] = messages[which][start + n * bins:start + (n + 1) * bins, :]
-
-
-def gain_rows(coef_ref, dens_ref, gain_ref, bins, n_rows):
-    total = dens_ref.shape[1]
+    shift_of = (bins - 1).bit_length()
+    taker = lax.shift_right_logical(lax.broadcasted_iota(jnp.int32, (lines, total), 0), 2 * shift_of) ^ here
+    giver = lax.shift_right_logical(lax.broadcasted_iota(jnp.int32, (lines, total), 1), shift_of) ^ here
+    one = rows_ref[...].astype(F32)
+    both = one + swapped_ref[...].astype(F32)
+    high = both.astype(BF16).astype(F32)
+    earlier = giver < taker
+    zero = jnp.zeros_like(one)
+    out_ref[:, :total] = jnp.where(giver == taker, one, jnp.where(earlier, high, zero)).astype(BF16)
+    out_ref[:, total:] = jnp.where(earlier, both - high, zero).astype(BF16)
+
+
+def block_start(offset, bins):
+    return pl.multiple_of((lax.axis_index("bin") ^ offset) * bins, bins)
+
+
+def add_blocks(weights_ref, messages, places, first, last, dens_ref, gain_ref, old_ref):
+    n_rows, bins, cells = gain_ref.shape
+    total = dens_ref.shape[1] // 2
     group = 8
-
-    def one_row(n, carry):
-        low = dens_ref[n]
-        wide = low.astype(F32)
-        acc = jnp.zeros((bins, low.shape[1]), F32)
-        for i in range(0, total, group):
-            inner = jnp.dot(coef_ref[i * bins:(i + group) * bins, :], low, preferred_element_type=F32)
-            for g in range(group):
-                acc = acc + inner[g * bins:(g + 1) * bins] * wide[i + g:i + g + 1]
+    for offset in range(len(places)):
+        at = block_start(offset, bins)
+        for n in range(n_rows):
+            if offset < last:
+                which, start = places[offset]
+                low = messages[which][start + n * bins:start + (n + 1) * bins, :]
+            else:
+                low = jnp.zeros((bins, cells), BF16)
+            dens_ref[n, pl.ds(at, bins), :] = low
+            dens_ref[n, pl.ds(total + at, bins), :] = low
+    for n in range(n_rows):
+        both = dens_ref[n]
+        acc = jnp.zeros((bins, cells), F32) if old_ref is None else old_ref[n]
+        for offset in range(first, last):
+            which, start = places[offset]
+            wide = messages[which][start + n * bins:start + (n + 1) * bins, :].astype(F32)
+            at = block_start(offset, bins) * bins
+            for i in range(0, bins, group):
+                lines = pl.ds(pl.multiple_of(at + i * bins, group * bins), group * bins)
+                inner = jnp.dot(weights_ref[lines, :], both, preferred_element_type=F32)
+                for g in range(group):
+                    acc = acc + inner[g * bins:(g + 1) * bins] * wide[i + g:i + g + 1]
         gain_ref[n] = acc
-        return carry
-
-    lax.fori_loop(0, n_rows, one_row, 0)
-
-
-def inner_gain_kernel(places, coef_ref, *refs):
-    messages, (gain_ref, dens_ref) = refs[:-2], refs[-2:]
-    n_rows, bins, _ = gain_ref.shape
-    gather_low(places, messages, dens_ref, bins)
-    gain_rows(coef_ref, dens_ref, gain_ref, bins, n_rows)
-
-
-def outer_gain_kernel(places, after_ref, coef_ref, adv_ref, inner_ref, *refs):
-    del after_ref
-    messages, (out_ref, dens_ref, gain_ref) = refs[:-3], refs[-3:]
-    bins, rows, _ = adv_ref.shape
-    picked = outer_rows(rows)
-    gather_low(places, messages, dens_ref, bins)
-    gain_rows(coef_ref, dens_ref, gain_ref, bins, len(picked))
-    for n, r in enumerate(picked):
-        out_ref[:, r, :] = adv_ref[:, r, :] + COAGULATION * gain_ref[n]
+
+
+def first_gain_kernel(in_places, out_places, weights_ref, *refs):
+    messages, (gain_in_ref, gain_out_ref, dens_in_ref, dens_out_ref) = refs[:-4], refs[-4:]
+    half = len(in_places) // 2
+    add_blocks(weights_ref, messages, out_places, 0, half, dens_out_ref, gain_out_ref, None)
+    add_blocks(weights_ref, messages, in_places, 0, half + 1, dens_in_ref, gain_in_ref, None)
+
+
+def last_kernel(
+    in_places, out_places, table_ref, gas_ref, gvr_ref, gva_ref, vr_ref, va_ref, weights_ref, adv_ref, gain_in_ref, gain_out_ref, *refs
+):
+    messages, refs = refs[:-18], refs[-18:]
+    outs, kept, refs = refs[:5], refs[5:10], refs[10:]
+    new_in_ref, new_out_ref, dens_in_ref, dens_out_ref, sums_ref, halves_in_ref, halves_out_ref, sems = refs
+    _, rows, _ = adv_ref.shape
+    count = len(in_places)
+    copies = [pltpu.make_async_copy(kept[n], outs[n], sems.at[n]) for n in range(5)]
+    density_ref, vr_out, va_out, gvr_out, gva_out = kept
+    drag(
+        (in_places, out_places), table_ref, gas_ref, gvr_ref, gva_ref, vr_ref, va_ref, messages,
+        vr_out, va_out, gvr_out, gva_out, sums_ref, halves_in_ref, halves_out_ref,
+    )
+    for copy in copies[1:]:
+        copy.start()
+    add_blocks(weights_ref, messages, in_places, count // 2 + 1, count, dens_in_ref, new_in_ref, gain_in_ref)
     for n, r in enumerate(inner_rows(rows)):
-        out_ref[:, r, :] = adv_ref[:, r, :] + COAGULATION * inner_ref[n]
+        density_ref[:, r, :] = adv_ref[:, r, :] + COAGULATION * new_in_ref[n]
+    add_blocks(weights_ref, messages, out_places, count // 2, count, dens_out_ref, new_out_ref, gain_out_ref)
+    for n, r in enumerate(outer_rows(rows)):
+        density_ref[:, r, :] = adv_ref[:, r, :] + COAGULATION * new_out_ref[n]
+    copies[0].start()
+    for copy in copies:
+        copy.wait()
 
 
 def struct(shape, dtype=F32):
     return jax.ShapeDtypeStruct(shape, dtype)
 
 
-def call(kernel, outs, *args, scratch=(), remote=()):
+def call(kernel, outs, *args, scratch=(), remote=(), loose=(), spec=VMEM):
     specs = [ANY if n in remote else VMEM for n in range(len(args))]
-    placed = [x if n in remote else pltpu.with_memory_space_constraint(x, pltpu.VMEM) for n, x in enumerate(args)]
+    placed = [x if n in remote or n in loose else pltpu.with_memory_space_constraint(x, pltpu.VMEM) for n, x in enumerate(args)]
     return pl.pallas_call(
         kernel,
         out_shape=outs,
         in_specs=specs,
-        out_specs=jax.tree.map(lambda _: VMEM, outs, is_leaf=lambda x: hasattr(x, "dtype")),
+        out_specs=jax.tree.map(lambda _: spec, outs, is_leaf=lambda x: hasattr(x, "dtype")),
         scratch_shapes=scratch,
     )(*placed)
 
@@ -283,7 +321,12 @@
     bins, rows, cells = rho.shape
     total = coef.shape[1]
     inner, outer = inner_rows(rows), outer_rows(rows)
-    coef_rows = jnp.transpose(coef, (1, 0, 2)).reshape(total * bins, total)
+    weights_size = (total * bins, 2 * total)
+    small = 2 * weights_size[0] * weights_size[1] <= SMALL_BYTES
+    weights = call(
+        weights_kernel, (pltpu.VMEM if small else struct)(weights_size, BF16),
+        jnp.transpose(coef, (1, 0, 2)).reshape(total * bins, total), jnp.transpose(coef, (2, 0, 1)).reshape(total * bins, total),
+    )
     field, kept = struct(rho.shape), pltpu.VMEM(rho.shape, F32)
     flat = struct(gas.shape)
     halo = pltpu.VMEM((3, bins, cells), BF16)
@@ -302,7 +345,8 @@
     groups = lax.axis_size("bin")
     half = groups // 2
     base, low_in = call(
-        inner_kernel, (kept, pltpu.VMEM((inner_lines, cells), BF16)), table, rho, vr, va, scratch=[kept, halves_in],
+        inner_kernel, (kept, pltpu.VMEM((inner_lines, cells), BF16)), table, rho, vr, va,
+        scratch=[kept, halves_in],
     )
     far_in = lax.ppermute(low_in, "bin", xor_pairs("bin", half))
 
@@ -315,28 +359,25 @@
     near_all = [lax.ppermute(low_all, "bin", xor_pairs("bin", at)) for at in range(1, half)]
     passed_in = [lax.ppermute(far_in, "bin", xor_pairs("bin", at)) for at in range(1, half)]
 
-    in_messages = [low_in] + near_all + [far_in] + passed_in
+    messages = [low_in] + near_all + [far_in] + passed_in + [low_out] + far_out
     in_places = [(n, 0) for n in range(groups)]
-    out_messages = [low_out] + near_all + far_out
-    out_places = [(n, inner_lines if 0 < n < half else 0) for n in range(groups)]
-    drag_out = [(n if 0 < n < half else groups + (n - half + 1 if n else 0), start) for n, start in out_places]
-    drag_messages = in_messages + [low_out] + far_out
-
-    gain_in = call(
-        functools.partial(inner_gain_kernel, in_places), pltpu.VMEM((len(inner), bins, cells), F32), coef_rows, *in_messages,
-        scratch=[pltpu.VMEM((len(inner), total, cells), BF16)],
-    )
-    vr_out, va_out, gvr_out, gva_out = call(
-        functools.partial(drag_kernel, (in_places, drag_out)), (field, field, flat, flat),
-        table, gas, gvr, gva, vr, va, *drag_messages,
-        scratch=[pltpu.VMEM((groups, 3, rows, cells), F32), halves_in, halves_out],
-    )
-    density_out = call(
-        functools.partial(outer_gain_kernel, out_places), field, gvr_out, coef_rows, adv, gain_in, *out_messages,
-        scratch=[pltpu.VMEM((len(outer), total, cells), BF16), pltpu.VMEM((len(outer), bins, cells), F32)],
-        remote=(0,),
-    )
-    return density_out, vr_out, va_out, gvr_out, gva_out
+    out_places = [(n, inner_lines) if 0 < n < half else (groups + (n - half + 1 if n else 0), 0) for n in range(groups)]
+
+    ready = half + 1
+    gains = [pltpu.VMEM((len(picked), bins, cells), F32) for picked in (inner, outer)]
+    dens = [pltpu.VMEM((len(picked), 2 * total, cells), BF16) for picked in (inner, outer)]
+    early = messages[:ready] + [low_out]
+    early_out = [(n, inner_lines) if n else (ready, 0) for n in range(half)] + [None] * (groups - half)
+    gain_in, gain_out = call(
+        functools.partial(first_gain_kernel, in_places, early_out), tuple(gains), weights, *early, scratch=dens, loose=() if small else (0,),
+    )
+    return call(
+        functools.partial(last_kernel, in_places, out_places), (field, field, field, flat, flat),
+        table, gas, gvr, gva, vr, va, weights, adv, gain_in, gain_out, *messages,
+        scratch=[kept] * 3 + [pltpu.VMEM(gas.shape, F32)] * 2 + gains + dens
+        + [pltpu.VMEM((groups, 3, rows, cells), F32), halves_in, halves_out, pltpu.SemaphoreType.DMA((5,))],
+        loose=() if small else (6,), spec=ANY,
+    )
 
 
 def solution(mesh):

time: 28.1 us -> 27.9 us (level)
  Pallas kernels: 8.69 us -> 7.52 us
  starting transfers between devices: 13.3 us -> 14.4 us
  waiting for transfers between devices: 5.08 us -> 4.63 us
    ppermute x1, starting transfers between devices: 1.71 us -> 4.03 us  [body(): lax.ppermute(far_in, 'bin', xor_pairs('bin', at))]
    ppermute x1, waiting for transfers between devices: 0.55 us -> 2.42 us  [body(): far_in = lax.ppermute(low_in, 'bin', xor_pairs('bin', half))]
    ppermute x1, waiting for transfers between devices: 1.85 us -> 0.01 us  [body(): lax.ppermute(far_in, 'bin', xor_pairs('bin', at))]
    ppermute x2, starting transfers between devices: 3.19 us -> 1.91 us  [body(): lax.ppermute(low_out, 'bin', xor_pairs('bin', at))]
    pallas_call x6, Pallas kernels: 8.69 us -> 7.52 us  [call(): pl.pallas_call(kernel, out_shape=outs, in_specs=specs, out_specs=jax.tree...]
    ppermute x2, waiting for transfers between devices: 2.68 us -> 1.73 us  [body(): lax.ppermute(low_out, 'bin', xor_pairs('bin', at))]
    ppermute x1, waiting for transfers between devices: 0.01 us -> 0.47 us  [body(): from_b = lax.ppermute(to_b, 'tile', odd_pairs('tile'))]
  transfers between devices with their start and end apart: 7 -> 7, of which waited for: 4 -> 3; matrix products, arithmetic and copies ran while one was open for 1% -> 2% of each run, Pallas kernels for 14% -> 12%
where the time goes in v4:
time: 27.9 us; the launch traced here: 27.7 us
  starting transfers between devices  14.4 us (52%)
  Pallas kernels  7.52 us (27%)
  waiting for transfers between devices  4.63 us (17%)
  between operations  0.72 us (3%)
  local copies, waits for them, and re-layouts  0.45 us (2%)
    pallas_call x6, Pallas kernels, call(): pl.pallas_call(kernel, out_shape=outs, in_specs=specs, out_specs=jax.tree...  7.52 us
    ppermute x1, starting transfers between devices, body(): lax.ppermute(far_in, 'bin', xor_pairs('bin', at))  4.03 us
    ppermute x1, starting transfers between devices, body(): from_b = lax.ppermute(to_b, 'tile', odd_pairs('tile'))  3.54 us
    ppermute x1, starting transfers between devices, body(): far_in = lax.ppermute(low_in, 'bin', xor_pairs('bin', half))  2.59 us
    ppermute x1, waiting for transfers between devices, body(): far_in = lax.ppermute(low_in, 'bin', xor_pairs('bin', half))  2.42 us
    ppermute x2, starting transfers between devices, body(): lax.ppermute(low_out, 'bin', xor_pairs('bin', at))  1.91 us
    ppermute x1, starting transfers between devices, body(): lax.ppermute(low_all, 'bin', xor_pairs('bin', at))  1.8 us
    ppermute x2, waiting for transfers between devices, body(): lax.ppermute(low_out, 'bin', xor_pairs('bin', at))  1.73 us
  transfers between devices with their start and end apart: 7, of which 3 were waited for; matrix products, arithmetic and copies ran while one was open for 2% of the time, Pallas kernels for 12%

profile of v4, /device:TPU:0, one launch (start us, length us, event | category | flops | bytes accessed | tf_op | source)
XLA Modules:
  0.0 27.7 jit_solution(4042125755393414310)
XLA Ops:
  0.6 1.4 %shard_map.119 = (bf16[3,16,512]{2,1,0:T(8,128)(2,1)S(1)}, bf16[3,16,512]{2,1,0:T(8,128)(2,1)S(1)}, f32[16,8,512]{2,1,0:T(8,128)S(1)}, f32[16,8,512]{2,1,0:T(8,1...) custom-call(f32[16,8,512]{2,1,0:T(8,128)} %rho_in.1, f32[16,8,512]{2,1,0:T(8,128)} %vr_in.1, ...), custom_call_target="tpu_custom_call" | custom-call | tf_op jit(solution)/shard_map/pallas_call | solution.py:295
  2.1 0.6 %collective-permute-start = (bf16[3,16,512]{2,1,0:T(8,128)(2,1)S(1)}, bf16[3,16,512]{2,1,0:T(8,128)(2,1)S(1)}, u32[]{:S(2)}, u32[]{:S(2)}) collective-permute-start(bf16[3,16,512]{2,1,0:T(8,128)(2,1)S(1)} %get-tuple-element.23), channel_id=1, source_target_pairs={{0,4},{4,0},{8,12},{12,8},{16,20},{20,16},{24,28},{28,24},{1,5},{5... | collective-permute-start | bytes 147464 | tf_op jit(solution)/shard_map/ppermute | solution.py:343
  2.6 3.5 %collective-permute-start.1 = (bf16[3,16,512]{2,1,0:T(8,128)(2,1)S(1)}, bf16[3,16,512]{2,1,0:T(8,128)(2,1)S(1)}, u32[]{:S(2)}, u32[]{:S(2)}) collective-permute-start(bf16[3,16,512]{2,1,0:T(8,128)(2,1)S(1)} %get-tuple-element.24), channel_id=1, source_target_pairs={{0,28},{28,0},{4,8},{8,4},{12,16},{16,12},{20,24},{24,20},{1,29},{... | collective-permute-start | bytes 147464 | tf_op jit(solution)/shard_map/ppermute | solution.py:342
  6.2 1.3 %shard_map.121 = (f32[16,8,512]{2,1,0:T(8,128)S(1)}, bf16[88,512]{1,0:T(8,128)(2,1)S(1)}) custom-call(f32[2,16,512]{2,1,0:T(8,128)S(1)} %get-tuple-element.18.table_ref, f32[16,8,512]{2,1,0:T(8,128)S(1)} %get-tuple-element.21.rho_ref, f32[16,8,512]{2,1,0:T(8,128)S(1)} %get-tuple-element.19.vr_ref, f32[16,8,512]{2,1,0:T(8,128)S(1)} %get-tuple-element.20.va_ref), custom_call_target="tpu_custom_call" | custom-call | tf_op jit(solution)/shard_map/pallas_call | solution.py:295
  7.5 0.0 collective-permute-done.from_a_ref
  7.5 0.5 %collective-permute-done.1.from_b_ref = bf16[3,16,512]{2,1,0:T(8,128)(2,1)S(1)} collective-permute-done((bf16[3,16,512]{2,1,0:T(8,128)(2,1)S(1)}, bf16[3,16,512]{2,1,0:T(8,128)(2,1)S(1)}, u32[]{:S(2)}, u32[]{:S(2)}) %collective-permute-start.1) | collective-permute-done | bytes 49184 | tf_op jit(solution)/shard_map/ppermute | solution.py:342
  7.9 0.0 copy-start.3
  7.9 0.9 %shard_map.122 = (f32[16,8,512]{2,1,0:T(8,128)S(1)}, bf16[88,512]{1,0:T(8,128)(2,1)S(1)}, bf16[176,512]{1,0:T(8,128)(2,1)S(1)}) custom-call(f32[2,16,512]{2,1,0:T(8,128)S(1)} %get-tuple-element.18.table_ref, f32[16,8,512]{2,1,0:T(8,128)S(1)} %get-tuple-element.21.rho_ref, f32[16,8,512]{2,1,0:T(8,128)S(1)} %get-tuple-element.19.vr_ref, ...), custom_call_target="tpu_custom_call" | custom-call | tf_op jit(solution)/shard_map/pallas_call | solution.py:295
  8.8 1.8 %collective-permute-start.2 = (bf16[176,512]{1,0:T(8,128)(2,1)S(1)}, bf16[176,512]{1,0:T(8,128)(2,1)S(1)}, u32[]{:S(2)}, u32[]{:S(2)}) collective-permute-start(bf16[176,512]{1,0:T(8,128)(2,1)S(1)} %get-tuple-element.27), channel_id=1, source_target_pairs={{0,1},{1,0},{2,3},{3,2},{4,5},{5,4},{6,7},{7,6},{8,9},{9,8},{10,11... | collective-permute-start | bytes 540680 | tf_op jit(solution)/shard_map/ppermute | solution.py:359
  10.6 2.6 %collective-permute-start.3 = (bf16[88,512]{1,0:T(8,128)(2,1)S(1)}, bf16[88,512]{1,0:T(8,128)(2,1)S(1)}, u32[]{:S(2)}, u32[]{:S(2)}) collective-permute-start(bf16[88,512]{1,0:T(8,128)(2,1)S(1)} %get-tuple-element.25.inner_ref.refs_0_), channel_id=1, source_target_pairs={{0,2},{1,3},{2,0},{3,1},{4,6},{5,7},{6,4},{7,5},{8,10},{9,11},{10,... | collective-permute-start | bytes 270344 | tf_op jit(solution)/shard_map/ppermute | solution.py:351
  13.2 0.1 collective-permute-start.6
  13.2 1.8 %collective-permute-start.5 = (bf16[88,512]{1,0:T(8,128)(2,1)S(1)}, bf16[88,512]{1,0:T(8,128)(2,1)S(1)}, u32[]{:S(2)}, u32[]{:S(2)}) collective-permute-start(bf16[88,512]{1,0:T(8,128)(2,1)S(1)} %get-tuple-element.28.refs_3_.refs_4_), channel_id=1, source_target_pairs={{0,2},{1,3},{2,0},{3,1},{4,6},{5,7},{6,4},{7,5},{8,10},{9,11},{10,... | collective-permute-start | bytes 270344 | tf_op jit(solution)/shard_map/ppermute | solution.py:358
  15.1 2.4 %collective-permute-done.3.refs_2_ = bf16[88,512]{1,0:T(8,128)(2,1)S(1)} collective-permute-done((bf16[88,512]{1,0:T(8,128)(2,1)S(1)}, bf16[88,512]{1,0:T(8,128)(2,1)S(1)}, u32[]{:S(2)}, u32[]{:S(2)}) %collective-permute-start.3) | collective-permute-done | bytes 90144 | tf_op jit(solution)/shard_map/ppermute | solution.py:351
  17.5 4.0 %collective-permute-start.4 = (bf16[88,512]{1,0:T(8,128)(2,1)S(1)}, bf16[88,512]{1,0:T(8,128)(2,1)S(1)}, u32[]{:S(2)}, u32[]{:S(2)}) collective-permute-start(bf16[88,512]{1,0:T(8,128)(2,1)S(1)} %collective-permute-done.3.refs_2_), channel_id=1, source_target_pairs={{0,1},{1,0},{2,3},{3,2},{4,5},{5,4},{6,7},{7,6},{8,9},{9,8},{10,11... | collective-permute-start | bytes 270344 | tf_op jit(solution)/shard_map/ppermute | solution.py:360
  21.5 0.0 copy-done.3
  21.5 0.2 copy.13
  21.7 0.3 copy.14
  22.0 0.3 %shard_map.120.weights_ref = bf16[1024,128]{1,0:T(8,128)(2,1)S(1)} custom-call(bf16[1024,64]{1,0:T(8,128)(2,1)S(1)} %bitcast.5, bf16[1024,64]{1,0:T(8,128)(2,1)S(1)} %bitcast.6), custom_call_target="tpu_custom_call" | custom-call | tf_op jit(solution)/shard_map/pallas_call | solution.py:295
  22.3 0.0 collective-permute-done.2.refs_1_
  22.3 0.0 copy-start
  22.3 0.0 copy-start.1
  22.4 0.0 copy-start.2
  22.4 1.6 %shard_map.123 = (f32[4,16,512]{2,1,0:T(8,128)S(1)}, f32[4,16,512]{2,1,0:T(8,128)S(1)}) custom-call(bf16[1024,128]{1,0:T(8,128)(2,1)S(1)} %shard_map.120.weights_ref, bf16[88,512]{1,0:T(8,128)(2,1)S(1)} %get-tuple-element.25.inner_ref.refs_0_, bf16[176,512]{1,0:T(8,128)(2,1)S(1)} %collective-permute-done.2.refs_1_, ...), custom_call_target="tpu_custom_call" | custom-call | tf_op jit(solution)/shard_map/pallas_call | solution.py:295
  23.9 0.0 collective-permute-done.6.refs_6_
  24.0 1.7 %collective-permute-done.5.refs_5_ = bf16[88,512]{1,0:T(8,128)(2,1)S(1)} collective-permute-done((bf16[88,512]{1,0:T(8,128)(2,1)S(1)}, bf16[88,512]{1,0:T(8,128)(2,1)S(1)}, u32[]{:S(2)}, u32[]{:S(2)}) %collective-permute-start.5) | collective-permute-done | bytes 90144 | tf_op jit(solution)/shard_map/ppermute | solution.py:358
  25.7 0.0 collective-permute-done.4.refs_3_
  25.7 0.0 copy-done
  25.7 0.0 copy-done.1
  25.7 0.0 copy-done.2
  25.7 2.0 %shard_map.124 = (f32[16,8,512]{2,1,0:T(8,128)}, f32[16,8,512]{2,1,0:T(8,128)}, f32[16,8,512]{2,1,0:T(8,128)}, f32[8,512]{1,0:T(8,128)}, f32[8,512]{1,0:T(8,128)}) custom-call(f32[2,16,512]{2,1,0:T(8,128)S(1)} %get-tuple-element.18.table_ref, f32[8,512]{1,0:T(8,128)S(1)} %copy-done, f32[8,512]{1,0:T(8,128)S(1)} %copy-done.1, f32[8,512]{1,0:T(8,128)S(1)} %copy-done.2, ...), custom_call_target="tpu_custom_call" | custom-call | tf_op jit(solution)/shard_map/pallas_call | solution.py:295
Async XLA Ops:
  2.1 5.4 %collective-permute-start = (bf16[3,16,512]{2,1,0:T(8,128)(2,1)S(1)}, bf16[3,16,512]{2,1,0:T(8,128)(2,1)S(1)}, u32[]{:S(2)}, u32[]{:S(2)}) collective-permute-start(bf16[3,16,512]{2,1,0:T(8,128)(2,1)S(1)} %get-tuple-element.23), channel_id=1, source_target_pairs={{0,4},{4,0},{8,12},{12,8},{16,20},{20,16},{24,28},{28,24},{1,5},{5... | collective-permute-start | bytes 147464 | tf_op jit(solution)/shard_map/ppermute | solution.py:343
  2.6 5.3 %collective-permute-start.1 = (bf16[3,16,512]{2,1,0:T(8,128)(2,1)S(1)}, bf16[3,16,512]{2,1,0:T(8,128)(2,1)S(1)}, u32[]{:S(2)}, u32[]{:S(2)}) collective-permute-start(bf16[3,16,512]{2,1,0:T(8,128)(2,1)S(1)} %get-tuple-element.24), channel_id=1, source_target_pairs={{0,28},{28,0},{4,8},{8,4},{12,16},{16,12},{20,24},{24,20},{1,29},{... | collective-permute-start | bytes 147464 | tf_op jit(solution)/shard_map/ppermute | solution.py:342
  7.9 13.6 %copy-start.3 = (bf16[16,64,64]{2,1,0:T(8,128)(2,1)S(1)}, bf16[16,64,64]{2,1,0:T(8,128)(2,1)}, u32[]{:S(2)}) copy-start(bf16[16,64,64]{2,1,0:T(8,128)(2,1)} %param.15) | copy-start | bytes 393220
  8.8 13.5 %collective-permute-start.2 = (bf16[176,512]{1,0:T(8,128)(2,1)S(1)}, bf16[176,512]{1,0:T(8,128)(2,1)S(1)}, u32[]{:S(2)}, u32[]{:S(2)}) collective-permute-start(bf16[176,512]{1,0:T(8,128)(2,1)S(1)} %get-tuple-element.27), channel_id=1, source_target_pairs={{0,1},{1,0},{2,3},{3,2},{4,5},{5,4},{6,7},{7,6},{8,9},{9,8},{10,11... | collective-permute-start | bytes 540680 | tf_op jit(solution)/shard_map/ppermute | solution.py:359
  10.6 6.9 %collective-permute-start.3 = (bf16[88,512]{1,0:T(8,128)(2,1)S(1)}, bf16[88,512]{1,0:T(8,128)(2,1)S(1)}, u32[]{:S(2)}, u32[]{:S(2)}) collective-permute-start(bf16[88,512]{1,0:T(8,128)(2,1)S(1)} %get-tuple-element.25.inner_ref.refs_0_), channel_id=1, source_target_pairs={{0,2},{1,3},{2,0},{3,1},{4,6},{5,7},{6,4},{7,5},{8,10},{9,11},{10,... | collective-permute-start | bytes 270344 | tf_op jit(solution)/shard_map/ppermute | solution.py:351
  13.2 10.8 %collective-permute-start.6 = (bf16[88,512]{1,0:T(8,128)(2,1)S(1)}, bf16[88,512]{1,0:T(8,128)(2,1)S(1)}, u32[]{:S(2)}, u32[]{:S(2)}) collective-permute-start(bf16[88,512]{1,0:T(8,128)(2,1)S(1)} %get-tuple-element.28.refs_3_.refs_4_), channel_id=1, source_target_pairs={{0,3},{1,2},{2,1},{3,0},{4,7},{5,6},{6,5},{7,4},{8,11},{9,10},{10,... | collective-permute-start | bytes 270344 | tf_op jit(solution)/shard_map/ppermute | solution.py:358
  13.2 12.4 %collective-permute-start.5 = (bf16[88,512]{1,0:T(8,128)(2,1)S(1)}, bf16[88,512]{1,0:T(8,128)(2,1)S(1)}, u32[]{:S(2)}, u32[]{:S(2)}) collective-permute-start(bf16[88,512]{1,0:T(8,128)(2,1)S(1)} %get-tuple-element.28.refs_3_.refs_4_), channel_id=1, source_target_pairs={{0,2},{1,3},{2,0},{3,1},{4,6},{5,7},{6,4},{7,5},{8,10},{9,11},{10,... | collective-permute-start | bytes 270344 | tf_op jit(solution)/shard_map/ppermute | solution.py:358
  17.5 8.2 %collective-permute-start.4 = (bf16[88,512]{1,0:T(8,128)(2,1)S(1)}, bf16[88,512]{1,0:T(8,128)(2,1)S(1)}, u32[]{:S(2)}, u32[]{:S(2)}) collective-permute-start(bf16[88,512]{1,0:T(8,128)(2,1)S(1)} %collective-permute-done.3.refs_2_), channel_id=1, source_target_pairs={{0,1},{1,0},{2,3},{3,2},{4,5},{5,4},{6,7},{7,6},{8,9},{9,8},{10,11... | collective-permute-start | bytes 270344 | tf_op jit(solution)/shard_map/ppermute | solution.py:360
  22.3 3.4 %copy-start = (f32[8,512]{1,0:T(8,128)S(1)}, f32[8,512]{1,0:T(8,128)}, u32[]{:S(2)}) copy-start(f32[8,512]{1,0:T(8,128)} %gas_ref.1) | copy-start | bytes 49156
  22.3 3.3 %copy-start.1 = (f32[8,512]{1,0:T(8,128)S(1)}, f32[8,512]{1,0:T(8,128)}, u32[]{:S(2)}) copy-start(f32[8,512]{1,0:T(8,128)} %gvr_ref.1) | copy-start | bytes 49156
  22.4 3.3 %copy-start.2 = (f32[8,512]{1,0:T(8,128)S(1)}, f32[8,512]{1,0:T(8,128)}, u32[]{:S(2)}) copy-start(f32[8,512]{1,0:T(8,128)} %gva_ref.1) | copy-start | bytes 49156

commit v5 on v4

v5 whole, which is shorter than its diff:
```python
import functools

import jax
import jax.numpy as jnp
from jax import lax
from jax.experimental import pallas as pl
from jax.experimental.pallas import tpu as pltpu
from jax.sharding import PartitionSpec as P


COURANT = 0.2
COAGULATION = 0.5
HALO = 2
SMALL_BYTES = 2**19
F32 = jnp.float32
BF16 = jnp.bfloat16

VMEM = pl.BlockSpec(memory_space=pltpu.VMEM)
ANY = pl.BlockSpec(memory_space=pl.ANY)


def minmod(a, b):
    return jnp.maximum(jnp.minimum(a, b), 0.0) + jnp.minimum(jnp.maximum(a, b), 0.0)


def face_flux(low, low_slope, high, high_slope, u):
    cu = COURANT * u
    left = low + (0.5 - 0.5 * cu) * low_slope
    right = high - (0.5 + 0.5 * cu) * high_slope
    return jnp.maximum(u, 0.0) * left + jnp.minimum(u, 0.0) * right


def shift(x, by, axis):
    return pltpu.roll(x, by % x.shape[axis], axis)


def edge_rows(rows, width):
    return list(range(width)) + list(range(rows - width, rows))


def load_kernel(rho_in, vr_in, va_in, stop_in, to_a_ref, to_b_ref, rho_ref, vr_ref, va_ref, table_ref, stop_ref, stop_sem, sems):
    _, bins, cells = rho_ref.shape
    rows = rho_in.shape[1]
    stop_copy = pltpu.make_async_copy(stop_in, stop_ref, stop_sem)
    copies = []
    for source, target in ((rho_in, rho_ref), (vr_in, vr_ref), (va_in, va_ref)):
        for n, r in enumerate(edge_rows(rows, target.shape[0] // 2)):
            copies.append(pltpu.make_async_copy(source.at[:, r, :], target.at[n], sems.at[len(copies)]))
    for copy in copies:
        copy.start()
    stop_copy.start()
    stop_copy.wait()
    square = (bins, bins)
    own = lax.broadcasted_iota(jnp.int32, square, 0) == lax.broadcasted_iota(jnp.int32, square, 1)
    stop = jnp.sum(jnp.where(own, jnp.broadcast_to(stop_ref[...], square), 0.0), axis=1, keepdims=True)
    rate = 1.0 / stop
    scale = 1.0 / (1.0 + rate)
    table_ref[0] = jnp.broadcast_to(rate * scale, (bins, cells))
    table_ref[1] = jnp.broadcast_to(scale, (bins, cells))
    for copy in copies:
        copy.wait()
    even = lax.axis_index("tile") % 2 == 0
    up = (rho_ref[0], rho_ref[1], vr_ref[0])
    last, last_v = rho_ref.shape[0] - 1, vr_ref.shape[0] - 1
    down = (rho_ref[last], rho_ref[last - 1], vr_ref[last_v])
    for n in range(3):
        to_a_ref[n] = jnp.where(even, down[n], up[n]).astype(BF16)
        to_b_ref[n] = jnp.where(even, up[n], down[n]).astype(BF16)


def radial_inside(q, v):
    rows = q.shape[0]
    row = lax.broadcasted_iota(jnp.int32, q.shape, 0)
    q_next = shift(q, -1, 0)
    d = q_next - q
    s = minmod(shift(d, 1, 0), d)
    flux = face_flux(q, s, q_next, shift(s, -1, 0), 0.5 * (v + shift(v, -1, 0)))
    flux = jnp.where((row >= HALO - 1) & (row < rows - HALO), flux, 0.0)
    return flux - shift(flux, 1, 0)


def azimuthal(q, v):
    q_next = shift(q, -1, 1)
    d = q_next - q
    s = minmod(shift(d, 1, 1), d)
    flux = face_flux(q, s, q_next, shift(s, -1, 1), 0.5 * (v + shift(v, -1, 1)))
    return flux - shift(flux, 1, 1)


def inner_rows(rows):
    return list(range(HALO, rows - HALO))


def outer_rows(rows):
    return edge_rows(rows, HALO)


def lines_of(bins, picked):
    return (bins + 6) * len(picked)


def write_message(ref, densities, sums, halves_ref):
    bins, count = densities[0].shape[0], len(densities)
    for m in range(count):
        ref[m * bins:(m + 1) * bins, :] = densities[m].astype(BF16)
        for n in range(3):
            high = sums[n][m].astype(BF16).astype(F32)
            for half, value in enumerate((high, sums[n][m] - high)):
                at = (2 * n + half) * count + m
                halves_ref[at:at + 1, :] = value
    ref[count * bins:, :] = halves_ref[...].astype(BF16)


def read_sums(ref, picked, bins, halves_ref, sums_ref):
    count = len(picked)
    halves_ref[...] = ref[count * bins:, :].astype(F32)
    for n in range(3):
        for m, r in enumerate(picked):
            high, low = 2 * n * count + m, (2 * n + 1) * count + m
            sums_ref[n, r:r + 1, :] = halves_ref[high:high + 1, :] + halves_ref[low:low + 1, :]


def weighed(sums, adv, vr, va, coupling):
    weight = adv * coupling
    return (sums[0] + weight * vr, sums[1] + weight * va, sums[2] + weight)


def inner_kernel(table_ref, rho_ref, vr_ref, va_ref, message_ref, adv_ref, part_ref, all_ref, halves_ref):
    bins, rows, cells = rho_ref.shape
    zero = jnp.zeros((rows, cells), F32)
    sums = (zero, zero, zero)
    for b in range(bins):
        q, vr, va = rho_ref[b], vr_ref[b], va_ref[b]
        adv = q - COURANT * (azimuthal(q, va) + radial_inside(q, vr))
        all_ref[b] = adv
        sums = weighed(sums, adv, vr, va, jnp.broadcast_to(table_ref[0, b:b + 1, :], q.shape))
    picked = inner_rows(rows)
    densities = [all_ref[:, r, :] for r in picked]
    for n, density in enumerate(densities):
        adv_ref[n] = density
    write_message(message_ref, densities, [[x[r:r + 1] for r in picked] for x in sums], halves_ref)
    for n, r in enumerate(outer_rows(rows)):
        part_ref[n] = all_ref[:, r, :]


def outer_kernel(table_ref, rho_ref, vr_ref, va_ref, part_ref, from_a_ref, from_b_ref, adv_ref, message_ref, halves_ref):
    tile, tiles = lax.axis_index("tile"), lax.axis_size("tile")
    even = tile % 2 == 0
    has_top = jnp.where(tile > 0, 1.0, 0.0)
    has_bottom = jnp.where(tile < tiles - 1, 1.0, 0.0)
    top, bottom = [], []
    for n in range(3):
        a, b = from_a_ref[n].astype(F32), from_b_ref[n].astype(F32)
        top.append(jnp.where(even, b, a) * has_top)
        bottom.append(jnp.where(even, a, b) * has_bottom)

    def edge(nearest, nearest_part, v, sign, halo):
        q = [halo[1], halo[0]] + nearest
        d = [sign * (q[n] - q[n + 1]) for n in range(4)]
        s = [minmod(d[n], d[n + 1]) for n in range(3)]
        speed = [0.5 * (halo[2] + v[0]), 0.5 * (v[0] + v[1])]
        flux = []
        for n in range(2):
            low, high = (n, n + 1) if sign < 0 else (n + 1, n)
            flux.append(face_flux(q[low + 1], s[low], q[high + 1], s[high], speed[n]))
        outermost = nearest_part[0] - COURANT * sign * (flux[0] - flux[1])
        return outermost, nearest_part[1] - COURANT * sign * flux[1]

    row = [rho_ref[n] for n in range(rho_ref.shape[0])]
    speed = [vr_ref[n] for n in range(vr_ref.shape[0])]
    part = [part_ref[n] for n in range(part_ref.shape[0])]
    first, second = edge(row[:3], part[:2], speed[:2], -1.0, top)
    last, before = edge(row[:2:-1], part[:1:-1], speed[:1:-1], 1.0, bottom)
    densities = [first, second, before, last]
    sums = [[], [], []]
    for n, density in enumerate(densities):
        adv_ref[n] = density
        weight = density * table_ref[0]
        for kind, value in enumerate((weight * speed[n], weight * va_ref[n], weight)):
            sums[kind].append(jnp.sum(value, axis=0, keepdims=True))
    write_message(message_ref, densities, sums, halves_ref)


def total_sums(at, offset, bit):
    if bit == 0:
        return at(offset)
    return total_sums(at, offset, bit // 2) + total_sums(at, offset ^ bit, bit // 2)


def drag(count, table_ref, gas_ref, gvr_ref, gva_ref, vr_ref, va_ref, messages, vr_out, va_out, gvr_out, gva_out, sums_ref, halves_in_ref, halves_out_ref):
    bins, rows, _ = vr_ref.shape
    for offset in range(count):
        read_sums(messages[offset], inner_rows(rows), bins, halves_in_ref, sums_ref.at[offset])
        read_sums(messages[count + offset], outer_rows(rows), bins, halves_out_ref, sums_ref.at[offset])
    sums = [total_sums(lambda o, n=n: sums_ref[o, n], 0, count // 2) for n in range(3)]
    gas = gas_ref[...]
    denom = gas + sums[2]
    new_r = (gas * gvr_ref[...] + sums[0]) / denom
    new_a = (gas * gva_ref[...] + sums[1]) / denom
    gvr_out[...] = new_r
    gva_out[...] = new_a
    for b in range(bins):
        coupling = jnp.broadcast_to(table_ref[0, b:b + 1, :], gas.shape)
        scale = jnp.broadcast_to(table_ref[1, b:b + 1, :], gas.shape)
        vr_out[b] = vr_ref[b] * scale + coupling * new_r
        va_out[b] = va_ref[b] * scale + coupling * new_a


def weights_kernel(rows_ref, swapped_ref, out_ref):
    lines, total = rows_ref.shape
    bins = lines // total
    here = lax.axis_index("bin")
    shift_of = (bins - 1).bit_length()
    taker = lax.shift_right_logical(lax.broadcasted_iota(jnp.int32, (lines, total), 0), 2 * shift_of) ^ here
    giver = lax.shift_right_logical(lax.broadcasted_iota(jnp.int32, (lines, total), 1), shift_of) ^ here
    one = rows_ref[...].astype(F32)
    both = one + swapped_ref[...].astype(F32)
    high = both.astype(BF16).astype(F32)
    earlier = giver < taker
    zero = jnp.zeros_like(one)
    out_ref[:, :total] = jnp.where(giver == taker, one, jnp.where(earlier, high, zero)).astype(BF16)
    out_ref[:, total:] = jnp.where(earlier, both - high, zero).astype(BF16)


def block_start(offset, bins):
    return pl.multiple_of((lax.axis_index("bin") ^ offset) * bins, bins)


def add_blocks(weights_ref, messages, count, first, last, dens_ref, gain_ref, old_ref):
    n_rows, bins, cells = gain_ref.shape
    total = dens_ref.shape[1] // 2
    group = 8
    for offset in range(count):
        at = block_start(offset, bins)
        for n in range(n_rows):
            if offset < last:
                low = messages[offset][n * bins:(n + 1) * bins, :]
            else:
                low = jnp.zeros((bins, cells), BF16)
            dens_ref[n, pl.ds(at, bins), :] = low
            dens_ref[n, pl.ds(total + at, bins), :] = low
    for n in range(n_rows):
        both = dens_ref[n]
        acc = jnp.zeros((bins, cells), F32) if old_ref is None else old_ref[n]
        for offset in range(first, last):
            wide = messages[offset][n * bins:(n + 1) * bins, :].astype(F32)
            at = block_start(offset, bins) * bins
            for i in range(0, bins, group):
                lines = pl.ds(pl.multiple_of(at + i * bins, group * bins), group * bins)
                inner = jnp.dot(weights_ref[lines, :], both, preferred_element_type=F32)
                for g in range(group):
                    acc = acc + inner[g * bins:(g + 1) * bins] * wide[i + g:i + g + 1]
        gain_ref[n] = acc


def first_gain_kernel(count, weights_ref, *refs):
    messages, (gain_in_ref, gain_out_ref, dens_in_ref, dens_out_ref) = refs[:-4], refs[-4:]
    half = count // 2
    add_blocks(weights_ref, messages[half + 1:], count, 0, half, dens_out_ref, gain_out_ref, None)
    add_blocks(weights_ref, messages[:half + 1], count, 0, half + 1, dens_in_ref, gain_in_ref, None)


def second_gain_kernel(weights_ref, old_ref, *refs):
    messages, (gain_ref, dens_ref) = refs[:-2], refs[-2:]
    count = len(messages)
    add_blocks(weights_ref, messages, count, count // 2, count, dens_ref, gain_ref, old_ref)


def last_kernel(
    count, table_ref, gas_ref, gvr_ref, gva_ref, vr_ref, va_ref, weights_ref, adv_in_ref, adv_out_ref, gain_in_ref, gain_out_ref, *refs
):
    messages, refs = refs[:-16], refs[-16:]
    outs, kept, refs = refs[:5], refs[5:10], refs[10:]
    new_in_ref, dens_in_ref, sums_ref, halves_in_ref, halves_out_ref, sems = refs
    rows = vr_ref.shape[1]
    copies = [pltpu.make_async_copy(kept[n], outs[n], sems.at[n]) for n in range(5)]
    density_ref, vr_out, va_out, gvr_out, gva_out = kept
    drag(
        count, table_ref, gas_ref, gvr_ref, gva_ref, vr_ref, va_ref, messages,
        vr_out, va_out, gvr_out, gva_out, sums_ref, halves_in_ref, halves_out_ref,
    )
    for copy in copies[1:]:
        copy.start()
    add_blocks(weights_ref, messages[:count], count, count // 2 + 1, count, dens_in_ref, new_in_ref, gain_in_ref)
    for n, r in enumerate(inner_rows(rows)):
        density_ref[:, r, :] = adv_in_ref[n] + COAGULATION * new_in_ref[n]
    for n, r in enumerate(outer_rows(rows)):
        density_ref[:, r, :] = adv_out_ref[n] + COAGULATION * gain_out_ref[n]
    copies[0].start()
    for copy in copies:
        copy.wait()


def struct(shape, dtype=F32):
    return jax.ShapeDtypeStruct(shape, dtype)


def call(kernel, outs, *args, scratch=(), remote=(), loose=(), spec=VMEM):
    specs = [ANY if n in remote else VMEM for n in range(len(args))]
    placed = [x if n in remote or n in loose else pltpu.with_memory_space_constraint(x, pltpu.VMEM) for n, x in enumerate(args)]
    return pl.pallas_call(
        kernel,
        out_shape=outs,
        in_specs=specs,
        out_specs=jax.tree.map(lambda _: spec, outs, is_leaf=lambda x: hasattr(x, "dtype")),
        scratch_shapes=scratch,
    )(*placed)


def xor_pairs(axis, bit):
    return [(i, i ^ bit) for i in range(lax.axis_size(axis))]


def even_pairs(axis):
    return xor_pairs(axis, 1)


def odd_pairs(axis):
    count = lax.axis_size(axis)
    pairs = [(0, count - 1), (count - 1, 0)]
    for i in range(1, count - 1, 2):
        pairs += [(i, i + 1), (i + 1, i)]
    return pairs


def body(rho, vr, va, gas, gvr, gva, stop_time, coef):
    bins, rows, cells = rho.shape
    total = coef.shape[1]
    inner, outer = inner_rows(rows), outer_rows(rows)
    weights_size = (total * bins, 2 * total)
    small = 2 * weights_size[0] * weights_size[1] <= SMALL_BYTES
    weights = call(
        weights_kernel, (pltpu.VMEM if small else struct)(weights_size, BF16),
        jnp.transpose(coef, (1, 0, 2)).reshape(total * bins, total), jnp.transpose(coef, (2, 0, 1)).reshape(total * bins, total),
    )
    field, kept = struct(rho.shape), pltpu.VMEM(rho.shape, F32)
    flat = struct(gas.shape)
    halo = pltpu.VMEM((3, bins, cells), BF16)
    inner_lines, outer_lines = lines_of(bins, inner), lines_of(bins, outer)
    halves_in, halves_out = (pltpu.VMEM((6 * len(picked), cells), F32) for picked in (inner, outer))

    edges = [pltpu.VMEM((2 * width, bins, cells), F32) for width in (HALO + 1, HALO, HALO)]
    to_a, to_b, rho_edge, vr_edge, va_edge, table = call(
        load_kernel, (halo, halo, *edges, pltpu.VMEM((2, bins, cells), F32)), rho, vr, va, stop_time[None],
        scratch=[pltpu.VMEM((1, bins), F32), pltpu.SemaphoreType.DMA, pltpu.SemaphoreType.DMA((6 * HALO + 2,))],
        remote=(0, 1, 2, 3),
    )
    from_b = lax.ppermute(to_b, "tile", odd_pairs("tile"))
    from_a = lax.ppermute(to_a, "tile", even_pairs("tile"))

    groups = lax.axis_size("bin")
    half = groups // 2
    dense = [pltpu.VMEM((len(picked), bins, cells), F32) for picked in (inner, outer)]
    low_in, adv_in, part_out = call(
        inner_kernel, (pltpu.VMEM((inner_lines, cells), BF16), *dense), table, rho, vr, va,
        scratch=[kept, halves_in],
    )
    near_in = [lax.ppermute(low_in, "bin", xor_pairs("bin", at)) for at in range(1, half)]
    far_in = lax.ppermute(low_in, "bin", xor_pairs("bin", half))

    adv_out, low_out = call(
        outer_kernel, (dense[1], pltpu.VMEM((outer_lines, cells), BF16)),
        table, rho_edge, vr_edge, va_edge, part_out, from_a, from_b, scratch=[halves_out],
    )
    near_out = [lax.ppermute(low_out, "bin", xor_pairs("bin", at)) for at in range(1, half)]
    far_out = [lax.ppermute(low_out, "bin", xor_pairs("bin", at)) for at in range(half, groups)]
    passed_in = [lax.ppermute(far_in, "bin", xor_pairs("bin", at)) for at in range(1, half)]

    in_messages = [low_in] + near_in + [far_in] + passed_in
    out_messages = [low_out] + near_out + far_out

    dens = [pltpu.VMEM((len(picked), 2 * total, cells), BF16) for picked in (inner, outer)]
    gain_in, gain_out = call(
        functools.partial(first_gain_kernel, groups), tuple(dense), weights, *in_messages[:half + 1], *out_messages[:half],
        scratch=dens, loose=() if small else (0,),
    )
    gain_out = call(
        second_gain_kernel, dense[1], weights, gain_out, *out_messages, scratch=dens[1:], loose=() if small else (0,),
    )
    return call(
        functools.partial(last_kernel, groups), (field, field, field, flat, flat),
        table, gas, gvr, gva, vr, va, weights, adv_in, adv_out, gain_in, gain_out, *in_messages, *out_messages,
        scratch=[kept] * 3 + [pltpu.VMEM(gas.shape, F32)] * 2 + dense[:1] + dens[:1]
        + [pltpu.VMEM((groups, 3, rows, cells), F32), halves_in, halves_out, pltpu.SemaphoreType.DMA((5,))],
        loose=() if small else (6,), spec=ANY,
    )


def solution(mesh):
    field, flat = P("bin", "tile", None), P("tile", None)
    return jax.shard_map(
        body,
        mesh=mesh,
        in_specs=(field, field, field, flat, flat, flat, P("bin"), P("bin", None, None)),
        out_specs=(field, field, field, flat, flat),
        check_vma=False,
    )
```

time: 27.9 us -> 26.3 us (0.943)
  waiting for transfers between devices: 4.63 us -> 3.61 us
  Pallas kernels: 7.52 us -> 6.85 us
    ppermute x1, waiting for transfers between devices: 2.42 us -> 0.01 us  [body(): far_in = lax.ppermute(low_in, 'bin', xor_pairs('bin', half))]
    ppermute x2 -> x3, starting transfers between devices: 1.91 us -> 3.55 us  [body(): lax.ppermute(low_out, 'bin', xor_pairs('bin', at))]
    ppermute x2 -> x3, waiting for transfers between devices: 1.73 us -> 3.33 us  [body(): lax.ppermute(low_out, 'bin', xor_pairs('bin', at))]
    ppermute x1, starting transfers between devices: 4.03 us -> 2.48 us  [body(): lax.ppermute(far_in, 'bin', xor_pairs('bin', at))]
    ppermute x1, starting transfers between devices: 2.59 us -> 4.13 us  [body(): far_in = lax.ppermute(low_in, 'bin', xor_pairs('bin', half))]
    ppermute x1, starting transfers between devices: 3.54 us -> 2.56 us  [body(): from_b = lax.ppermute(to_b, 'tile', odd_pairs('tile'))]
    pallas_call x6 -> x7, Pallas kernels: 7.52 us -> 6.85 us  [call(): pl.pallas_call(kernel, out_shape=outs, in_specs=specs, out_specs=jax.tree...]
    ppermute x1, starting transfers between devices: 0.56 us -> 0.01 us  [body(): from_a = lax.ppermute(to_a, 'tile', even_pairs('tile'))]
  transfers between devices with their start and end apart: 7 -> 8, of which waited for: 3 -> 3; matrix products, arithmetic and copies ran while one was open for 2% -> 2% of each run, Pallas kernels for 12% -> 11%
where the time goes in v5:
time: 26.3 us; the launch traced here: 26 us
  starting transfers between devices  14.3 us (54%)
  Pallas kernels  6.85 us (26%)
  waiting for transfers between devices  3.61 us (14%)
  between operations  0.76 us (3%)
  local copies, waits for them, and re-layouts  0.51 us (2%)
    pallas_call x7, Pallas kernels, call(): pl.pallas_call(kernel, out_shape=outs, in_specs=specs, out_specs=jax.tree...  6.85 us
    ppermute x1, starting transfers between devices, body(): far_in = lax.ppermute(low_in, 'bin', xor_pairs('bin', half))  4.13 us
    ppermute x3, starting transfers between devices, body(): lax.ppermute(low_out, 'bin', xor_pairs('bin', at))  3.55 us
    ppermute x3, waiting for transfers between devices, body(): lax.ppermute(low_out, 'bin', xor_pairs('bin', at))  3.33 us
    ppermute x1, starting transfers between devices, body(): from_b = lax.ppermute(to_b, 'tile', odd_pairs('tile'))  2.56 us
    ppermute x1, starting transfers between devices, body(): lax.ppermute(far_in, 'bin', xor_pairs('bin', at))  2.48 us
    ppermute x1, starting transfers between devices, body(): lax.ppermute(low_in, 'bin', xor_pairs('bin', at))  1.58 us
  transfers between devices with their start and end apart: 8, of which 3 were waited for; matrix products, arithmetic and copies ran while one was open for 2% of the time, Pallas kernels for 11%

profile of v5, /device:TPU:0, one launch (start us, length us, event | category | flops | bytes accessed | tf_op | source)
XLA Modules:
  0.0 26.0 jit_solution(3766232731840140113)
XLA Ops:
  0.6 0.0 copy-start
  0.6 0.0 copy-start.1
  0.7 0.0 copy-start.2
  0.7 1.3 %shard_map.119 = (bf16[3,16,512]{2,1,0:T(8,128)(2,1)S(1)}, bf16[3,16,512]{2,1,0:T(8,128)(2,1)S(1)}, f32[6,16,512]{2,1,0:T(8,128)S(1)}, f32[4,16,512]{2,1,0:T(8,1...) custom-call(f32[16,8,512]{2,1,0:T(8,128)} %rho_ref.1, f32[16,8,512]{2,1,0:T(8,128)} %vr_ref.3, ...), custom_call_target="tpu_custom_call" | custom-call | tf_op jit(solution)/shard_map/pallas_call | solution.py:301
  1.9 0.0 copy-done
  2.0 0.0 copy-done.1
  2.0 0.1 copy-done.2
  2.0 1.1 %shard_map.121 = (bf16[88,512]{1,0:T(8,128)(2,1)S(1)}, f32[4,16,512]{2,1,0:T(8,128)S(1)}, f32[4,16,512]{2,1,0:T(8,128)S(1)}) custom-call(f32[2,16,512]{2,1,0:T(8,128)S(1)} %get-tuple-element.18.table_ref, f32[16,8,512]{2,1,0:T(8,128)S(1)} %copy-done.2, f32[16,8,512]{2,1,0:T(8,128)S(1)} %copy-done, f32[16,8,512]{2,1,0:T(8,128)S(1)} %copy-done.1), custom_call_target="tpu_custom_call" | custom-call | tf_op jit(solution)/shard_map/pallas_call | solution.py:301
  3.2 4.1 %collective-permute-start.3 = (bf16[88,512]{1,0:T(8,128)(2,1)S(1)}, bf16[88,512]{1,0:T(8,128)(2,1)S(1)}, u32[]{:S(2)}, u32[]{:S(2)}) collective-permute-start(bf16[88,512]{1,0:T(8,128)(2,1)S(1)} %get-tuple-element.27.refs_0_), channel_id=1, source_target_pairs={{0,2},{1,3},{2,0},{3,1},{4,6},{5,7},{6,4},{7,5},{8,10},{9,11},{10,... | collective-permute-start | bytes 270344 | tf_op jit(solution)/shard_map/ppermute | solution.py:359
  7.3 0.0 collective-permute-start
  7.3 2.6 %collective-permute-start.1 = (bf16[3,16,512]{2,1,0:T(8,128)(2,1)S(1)}, bf16[3,16,512]{2,1,0:T(8,128)(2,1)S(1)}, u32[]{:S(2)}, u32[]{:S(2)}) collective-permute-start(bf16[3,16,512]{2,1,0:T(8,128)(2,1)S(1)} %get-tuple-element.25), channel_id=1, source_target_pairs={{0,28},{28,0},{4,8},{8,4},{12,16},{16,12},{20,24},{24,20},{1,29},{... | collective-permute-start | bytes 147464 | tf_op jit(solution)/shard_map/ppermute | solution.py:348
  9.8 1.6 %collective-permute-start.2 = (bf16[88,512]{1,0:T(8,128)(2,1)S(1)}, bf16[88,512]{1,0:T(8,128)(2,1)S(1)}, u32[]{:S(2)}, u32[]{:S(2)}) collective-permute-start(bf16[88,512]{1,0:T(8,128)(2,1)S(1)} %get-tuple-element.27.refs_0_), channel_id=1, source_target_pairs={{0,1},{1,0},{2,3},{3,2},{4,5},{5,4},{6,7},{7,6},{8,9},{9,8},{10,11... | collective-permute-start | bytes 270344 | tf_op jit(solution)/shard_map/ppermute | solution.py:358
  11.4 0.0 collective-permute-done.from_a_ref
  11.4 0.3 %collective-permute-done.1.from_b_ref = bf16[3,16,512]{2,1,0:T(8,128)(2,1)S(1)} collective-permute-done((bf16[3,16,512]{2,1,0:T(8,128)(2,1)S(1)}, bf16[3,16,512]{2,1,0:T(8,128)(2,1)S(1)}, u32[]{:S(2)}, u32[]{:S(2)}) %collective-permute-start.1) | collective-permute-done | bytes 49184 | tf_op jit(solution)/shard_map/ppermute | solution.py:348
  11.7 0.3 %shard_map.122 = (f32[4,16,512]{2,1,0:T(8,128)S(1)}, bf16[88,512]{1,0:T(8,128)(2,1)S(1)}) custom-call(f32[2,16,512]{2,1,0:T(8,128)S(1)} %get-tuple-element.18.table_ref, f32[6,16,512]{2,1,0:T(8,128)S(1)} %get-tuple-element.20.rho_ref, f32[4,16,512]{2,1,0:T(8,128)S(1)} %get-tuple-element.21.vr_ref, f32[4,16,512]{2,1,0:T(8,128)S(1)} %get-tuple-element.22.va_ref, ...), custom_call_target="tpu_custom_call" | custom-call | tf_op jit(solution)/shard_map/pallas_call | solution.py:301
  12.0 1.6 %collective-permute-start.4 = (bf16[88,512]{1,0:T(8,128)(2,1)S(1)}, bf16[88,512]{1,0:T(8,128)(2,1)S(1)}, u32[]{:S(2)}, u32[]{:S(2)}) collective-permute-start(bf16[88,512]{1,0:T(8,128)(2,1)S(1)} %get-tuple-element.28.refs_3_.refs_0_.refs_4_), channel_id=1, source_target_pairs={{0,1},{1,0},{2,3},{3,2},{4,5},{5,4},{6,7},{7,6},{8,9},{9,8},{10,11... | collective-permute-start | bytes 270344 | tf_op jit(solution)/shard_map/ppermute | solution.py:365
  13.6 0.1 collective-permute-start.6
  13.8 1.8 %collective-permute-start.5 = (bf16[88,512]{1,0:T(8,128)(2,1)S(1)}, bf16[88,512]{1,0:T(8,128)(2,1)S(1)}, u32[]{:S(2)}, u32[]{:S(2)}) collective-permute-start(bf16[88,512]{1,0:T(8,128)(2,1)S(1)} %get-tuple-element.28.refs_3_.refs_0_.refs_4_), channel_id=1, source_target_pairs={{0,2},{1,3},{2,0},{3,1},{4,6},{5,7},{6,4},{7,5},{8,10},{9,11},{10,... | collective-permute-start | bytes 270344 | tf_op jit(solution)/shard_map/ppermute | solution.py:366
  15.5 0.0 collective-permute-done.3.refs_2_
  15.5 2.5 %collective-permute-start.7 = (bf16[88,512]{1,0:T(8,128)(2,1)S(1)}, bf16[88,512]{1,0:T(8,128)(2,1)S(1)}, u32[]{:S(2)}, u32[]{:S(2)}) collective-permute-start(bf16[88,512]{1,0:T(8,128)(2,1)S(1)} %collective-permute-done.3.refs_2_), channel_id=1, source_target_pairs={{0,1},{1,0},{2,3},{3,2},{4,5},{5,4},{6,7},{7,6},{8,9},{9,8},{10,11... | collective-permute-start | bytes 270344 | tf_op jit(solution)/shard_map/ppermute | solution.py:367
  18.0 0.0 copy-done.6
  18.0 0.2 copy.13
  18.2 0.3 copy.14
  18.5 0.3 %shard_map.120.weights_ref = bf16[1024,128]{1,0:T(8,128)(2,1)S(1)} custom-call(bf16[1024,64]{1,0:T(8,128)(2,1)S(1)} %bitcast.5, bf16[1024,64]{1,0:T(8,128)(2,1)S(1)} %bitcast.6), custom_call_target="tpu_custom_call" | custom-call | tf_op jit(solution)/shard_map/pallas_call | solution.py:301
  18.8 0.0 collective-permute-done.2.refs_1_
  18.8 0.0 collective-permute-done.4.refs_4_.refs_1_.refs_5_
  18.8 1.6 %shard_map.123 = (f32[4,16,512]{2,1,0:T(8,128)S(1)}, f32[4,16,512]{2,1,0:T(8,128)S(1)}) custom-call(bf16[1024,128]{1,0:T(8,128)(2,1)S(1)} %shard_map.120.weights_ref, bf16[88,512]{1,0:T(8,128)(2,1)S(1)} %get-tuple-element.27.refs_0_, bf16[88,512]{1,0:T(8,128)(2,1)S(1)} %collective-permute-done.2.refs_1_, bf16[88,512]{1,0:T(8,128)(2,1)S(1)} %collective-permute-done.3.refs_2_, ...), custom_call_target="tpu_custom_call" | custom-call | tf_op jit(solution)/shard_map/pallas_call | solution.py:301
  20.4 0.5 %collective-permute-done.6.refs_3_.refs_7_ = bf16[88,512]{1,0:T(8,128)(2,1)S(1)} collective-permute-done((bf16[88,512]{1,0:T(8,128)(2,1)S(1)}, bf16[88,512]{1,0:T(8,128)(2,1)S(1)}, u32[]{:S(2)}, u32[]{:S(2)}) %collective-permute-start.6) | collective-permute-done | bytes 90144 | tf_op jit(solution)/shard_map/ppermute | solution.py:366
  20.9 2.8 %collective-permute-done.5.refs_2_.refs_6_ = bf16[88,512]{1,0:T(8,128)(2,1)S(1)} collective-permute-done((bf16[88,512]{1,0:T(8,128)(2,1)S(1)}, bf16[88,512]{1,0:T(8,128)(2,1)S(1)}, u32[]{:S(2)}, u32[]{:S(2)}) %collective-permute-start.5) | collective-permute-done | bytes 90144 | tf_op jit(solution)/shard_map/ppermute | solution.py:366
  23.7 0.7 %shard_map.124.gain_out_ref = f32[4,16,512]{2,1,0:T(8,128)S(1)} custom-call(bf16[1024,128]{1,0:T(8,128)(2,1)S(1)} %shard_map.120.weights_ref, f32[4,16,512]{2,1,0:T(8,128)S(1)} %get-tuple-element.30.old_ref, bf16[88,512]{1,0:T(8,128)(2,1)S(1)} %get-tuple-element.28.refs_3_.refs_0_.refs_4_, ...), custom_call_target="tpu_custom_call" | custom-call | tf_op jit(solution)/shard_map/pallas_call | solution.py:301
  24.5 0.0 collective-permute-done.7.refs_3_
  24.5 1.5 %shard_map.125 = (f32[16,8,512]{2,1,0:T(8,128)}, f32[16,8,512]{2,1,0:T(8,128)}, f32[16,8,512]{2,1,0:T(8,128)}, f32[8,512]{1,0:T(8,128)}, f32[8,512]{1,0:T(8,128)}) custom-call(f32[2,16,512]{2,1,0:T(8,128)S(1)} %get-tuple-element.18.table_ref, f32[8,512]{1,0:T(8,128)S(1)} %copy-done.3, f32[8,512]{1,0:T(8,128)S(1)} %copy-done.4, f32[8,512]{1,0:T(8,128)S(1)} %copy-done.5, ...), custom_call_target="tpu_custom_call" | custom-call | tf_op jit(solution)/shard_map/pallas_call | solution.py:301
  (7 shorter events, 0.0 us)
Async XLA Ops:
  0.6 1.3 %copy-start = (f32[16,8,512]{2,1,0:T(8,128)S(1)}, f32[16,8,512]{2,1,0:T(8,128)}, u32[]{:S(2)}) copy-start(f32[16,8,512]{2,1,0:T(8,128)} %vr_ref.3) | copy-start | bytes 786436
  0.6 1.3 %copy-start.1 = (f32[16,8,512]{2,1,0:T(8,128)S(1)}, f32[16,8,512]{2,1,0:T(8,128)}, u32[]{:S(2)}) copy-start(f32[16,8,512]{2,1,0:T(8,128)} %va_ref.3) | copy-start | bytes 786436
  0.7 1.4 %copy-start.2 = (f32[16,8,512]{2,1,0:T(8,128)S(1)}, f32[16,8,512]{2,1,0:T(8,128)}, u32[]{:S(2)}) copy-start(f32[16,8,512]{2,1,0:T(8,128)} %rho_ref.1) | copy-start | bytes 786436
  3.2 12.4 %collective-permute-start.3 = (bf16[88,512]{1,0:T(8,128)(2,1)S(1)}, bf16[88,512]{1,0:T(8,128)(2,1)S(1)}, u32[]{:S(2)}, u32[]{:S(2)}) collective-permute-start(bf16[88,512]{1,0:T(8,128)(2,1)S(1)} %get-tuple-element.27.refs_0_), channel_id=1, source_target_pairs={{0,2},{1,3},{2,0},{3,1},{4,6},{5,7},{6,4},{7,5},{8,10},{9,11},{10,... | collective-permute-start | bytes 270344 | tf_op jit(solution)/shard_map/ppermute | solution.py:359
  7.3 4.1 %collective-permute-start = (bf16[3,16,512]{2,1,0:T(8,128)(2,1)S(1)}, bf16[3,16,512]{2,1,0:T(8,128)(2,1)S(1)}, u32[]{:S(2)}, u32[]{:S(2)}) collective-permute-start(bf16[3,16,512]{2,1,0:T(8,128)(2,1)S(1)} %get-tuple-element.24), channel_id=1, source_target_pairs={{0,4},{4,0},{8,12},{12,8},{16,20},{20,16},{24,28},{28,24},{1,5},{5... | collective-permute-start | bytes 147464 | tf_op jit(solution)/shard_map/ppermute | solution.py:349
  7.3 4.4 %collective-permute-start.1 = (bf16[3,16,512]{2,1,0:T(8,128)(2,1)S(1)}, bf16[3,16,512]{2,1,0:T(8,128)(2,1)S(1)}, u32[]{:S(2)}, u32[]{:S(2)}) collective-permute-start(bf16[3,16,512]{2,1,0:T(8,128)(2,1)S(1)} %get-tuple-element.25), channel_id=1, source_target_pairs={{0,28},{28,0},{4,8},{8,4},{12,16},{16,12},{20,24},{24,20},{1,29},{... | collective-permute-start | bytes 147464 | tf_op jit(solution)/shard_map/ppermute | solution.py:348
  9.8 9.0 %collective-permute-start.2 = (bf16[88,512]{1,0:T(8,128)(2,1)S(1)}, bf16[88,512]{1,0:T(8,128)(2,1)S(1)}, u32[]{:S(2)}, u32[]{:S(2)}) collective-permute-start(bf16[88,512]{1,0:T(8,128)(2,1)S(1)} %get-tuple-element.27.refs_0_), channel_id=1, source_target_pairs={{0,1},{1,0},{2,3},{3,2},{4,5},{5,4},{6,7},{7,6},{8,9},{9,8},{10,11... | collective-permute-start | bytes 270344 | tf_op jit(solution)/shard_map/ppermute | solution.py:358
  11.7 6.3 %copy-start.6 = (bf16[16,64,64]{2,1,0:T(8,128)(2,1)S(1)}, bf16[16,64,64]{2,1,0:T(8,128)(2,1)}, u32[]{:S(2)}) copy-start(bf16[16,64,64]{2,1,0:T(8,128)(2,1)} %param.15) | copy-start | bytes 393220
  12.0 6.8 %collective-permute-start.4 = (bf16[88,512]{1,0:T(8,128)(2,1)S(1)}, bf16[88,512]{1,0:T(8,128)(2,1)S(1)}, u32[]{:S(2)}, u32[]{:S(2)}) collective-permute-start(bf16[88,512]{1,0:T(8,128)(2,1)S(1)} %get-tuple-element.28.refs_3_.refs_0_.refs_4_), channel_id=1, source_target_pairs={{0,1},{1,0},{2,3},{3,2},{4,5},{5,4},{6,7},{7,6},{8,9},{9,8},{10,11... | collective-permute-start | bytes 270344 | tf_op jit(solution)/shard_map/ppermute | solution.py:365
  13.6 7.3 %collective-permute-start.6 = (bf16[88,512]{1,0:T(8,128)(2,1)S(1)}, bf16[88,512]{1,0:T(8,128)(2,1)S(1)}, u32[]{:S(2)}, u32[]{:S(2)}) collective-permute-start(bf16[88,512]{1,0:T(8,128)(2,1)S(1)} %get-tuple-element.28.refs_3_.refs_0_.refs_4_), channel_id=1, source_target_pairs={{0,3},{1,2},{2,1},{3,0},{4,7},{5,6},{6,5},{7,4},{8,11},{9,10},{10,... | collective-permute-start | bytes 270344 | tf_op jit(solution)/shard_map/ppermute | solution.py:366
  13.8 10.0 %collective-permute-start.5 = (bf16[88,512]{1,0:T(8,128)(2,1)S(1)}, bf16[88,512]{1,0:T(8,128)(2,1)S(1)}, u32[]{:S(2)}, u32[]{:S(2)}) collective-permute-start(bf16[88,512]{1,0:T(8,128)(2,1)S(1)} %get-tuple-element.28.refs_3_.refs_0_.refs_4_), channel_id=1, source_target_pairs={{0,2},{1,3},{2,0},{3,1},{4,6},{5,7},{6,4},{7,5},{8,10},{9,11},{10,... | collective-permute-start | bytes 270344 | tf_op jit(solution)/shard_map/ppermute | solution.py:366
  15.5 8.9 %collective-permute-start.7 = (bf16[88,512]{1,0:T(8,128)(2,1)S(1)}, bf16[88,512]{1,0:T(8,128)(2,1)S(1)}, u32[]{:S(2)}, u32[]{:S(2)}) collective-permute-start(bf16[88,512]{1,0:T(8,128)(2,1)S(1)} %collective-permute-done.3.refs_2_), channel_id=1, source_target_pairs={{0,1},{1,0},{2,3},{3,2},{4,5},{5,4},{6,7},{7,6},{8,9},{9,8},{10,11... | collective-permute-start | bytes 270344 | tf_op jit(solution)/shard_map/ppermute | solution.py:367
  23.7 0.8 %copy-start.3 = (f32[8,512]{1,0:T(8,128)S(1)}, f32[8,512]{1,0:T(8,128)}, u32[]{:S(2)}) copy-start(f32[8,512]{1,0:T(8,128)} %gas_ref.1) | copy-start | bytes 49156
  23.7 0.8 %copy-start.4 = (f32[8,512]{1,0:T(8,128)S(1)}, f32[8,512]{1,0:T(8,128)}, u32[]{:S(2)}) copy-start(f32[8,512]{1,0:T(8,128)} %gvr_ref.1) | copy-start | bytes 49156
  23.7 0.8 %copy-start.5 = (f32[8,512]{1,0:T(8,128)S(1)}, f32[8,512]{1,0:T(8,128)}, u32[]{:S(2)}) copy-start(f32[8,512]{1,0:T(8,128)} %gva_ref.1) | copy-start | bytes 49156

commit v6 on v5

--- a/solution.py
+++ b/solution.py
@@ -125,7 +125,7 @@
     return (sums[0] + weight * vr, sums[1] + weight * va, sums[2] + weight)
 
 
-def inner_kernel(table_ref, rho_ref, vr_ref, va_ref, message_ref, adv_ref, part_ref, all_ref, halves_ref):
+def inner_kernel(table_ref, rho_ref, vr_ref, va_ref, message_ref, plain_ref, adv_ref, part_ref, all_ref, halves_ref):
     bins, rows, cells = rho_ref.shape
     zero = jnp.zeros((rows, cells), F32)
     sums = (zero, zero, zero)
@@ -139,6 +139,7 @@
     for n, density in enumerate(densities):
         adv_ref[n] = density
     write_message(message_ref, densities, [[x[r:r + 1] for r in picked] for x in sums], halves_ref)
+    plain_ref[...] = message_ref[:plain_ref.shape[0], :]
     for n, r in enumerate(outer_rows(rows)):
         part_ref[n] = all_ref[:, r, :]
 
@@ -181,18 +182,40 @@
     write_message(message_ref, densities, sums, halves_ref)
 
 
+def pack_kernel(own_ref, far_ref, out_ref, a_ref, b_ref):
+    start = out_ref.shape[0] - a_ref.shape[0]
+    count = a_ref.shape[0] // 6
+    out_ref[:start, :] = far_ref[:start, :]
+    a_ref[...] = own_ref[start:, :].astype(F32)
+    b_ref[...] = far_ref[start:, :].astype(F32)
+    for n in range(3):
+        high, low = pl.ds(2 * n * count, count), pl.ds((2 * n + 1) * count, count)
+        both = (a_ref[high, :] + a_ref[low, :]) + (b_ref[high, :] + b_ref[low, :])
+        first = both.astype(BF16).astype(F32)
+        a_ref[high, :] = first
+        a_ref[low, :] = both - first
+    out_ref[start:, :] = a_ref[...].astype(BF16)
+
+
 def total_sums(at, offset, bit):
     if bit == 0:
         return at(offset)
     return total_sums(at, offset, bit // 2) + total_sums(at, offset ^ bit, bit // 2)
 
 
-def drag(count, table_ref, gas_ref, gvr_ref, gva_ref, vr_ref, va_ref, messages, vr_out, va_out, gvr_out, gva_out, sums_ref, halves_in_ref, halves_out_ref):
+def drag(count, passing_ref, table_ref, gas_ref, gvr_ref, gva_ref, vr_ref, va_ref, messages, vr_out, va_out, gvr_out, gva_out, sums_ref, halves_in_ref, halves_out_ref):
     bins, rows, _ = vr_ref.shape
+    half = count // 2
+    for offset in range(half):
+        passed = messages[half + offset] if offset else passing_ref
+        read_sums(passed, inner_rows(rows), bins, halves_in_ref, sums_ref.at[offset])
     for offset in range(count):
-        read_sums(messages[offset], inner_rows(rows), bins, halves_in_ref, sums_ref.at[offset])
-        read_sums(messages[count + offset], outer_rows(rows), bins, halves_out_ref, sums_ref.at[offset])
-    sums = [total_sums(lambda o, n=n: sums_ref[o, n], 0, count // 2) for n in range(3)]
+        read_sums(messages[count + offset], outer_rows(rows), bins, halves_out_ref, sums_ref.at[half + offset])
+    inner = [total_sums(lambda o, n=n: sums_ref[o, n], 0, half // 2) for n in range(3)]
+    outer = [total_sums(lambda o, n=n: sums_ref[half + o, n], 0, half) for n in range(3)]
+    row = lax.broadcasted_iota(jnp.int32, gas_ref.shape, 0)
+    inside = (row >= HALO) & (row < rows - HALO)
+    sums = [jnp.where(inside, inner[n], outer[n]) for n in range(3)]
     gas = gas_ref[...]
     denom = gas + sums[2]
     new_r = (gas * gvr_ref[...] + sums[0]) / denom
@@ -253,30 +276,22 @@
         gain_ref[n] = acc
 
 
-def first_gain_kernel(count, weights_ref, *refs):
-    messages, (gain_in_ref, gain_out_ref, dens_in_ref, dens_out_ref) = refs[:-4], refs[-4:]
-    half = count // 2
-    add_blocks(weights_ref, messages[half + 1:], count, 0, half, dens_out_ref, gain_out_ref, None)
-    add_blocks(weights_ref, messages[:half + 1], count, 0, half + 1, dens_in_ref, gain_in_ref, None)
-
-
-def second_gain_kernel(weights_ref, old_ref, *refs):
+def gain_kernel(count, weights_ref, *refs):
     messages, (gain_ref, dens_ref) = refs[:-2], refs[-2:]
-    count = len(messages)
-    add_blocks(weights_ref, messages, count, count // 2, count, dens_ref, gain_ref, old_ref)
+    add_blocks(weights_ref, messages, count, 0, len(messages), dens_ref, gain_ref, None)
 
 
 def last_kernel(
-    count, table_ref, gas_ref, gvr_ref, gva_ref, vr_ref, va_ref, weights_ref, adv_in_ref, adv_out_ref, gain_in_ref, gain_out_ref, *refs
+    count, passing_ref, table_ref, gas_ref, gvr_ref, gva_ref, vr_ref, va_ref, weights_ref, adv_in_ref, adv_out_ref, gain_in_ref, gain_out_ref, *refs
 ):
-    messages, refs = refs[:-16], refs[-16:]
+    messages, refs = refs[:-18], refs[-18:]
     outs, kept, refs = refs[:5], refs[5:10], refs[10:]
-    new_in_ref, dens_in_ref, sums_ref, halves_in_ref, halves_out_ref, sems = refs
+    new_in_ref, new_out_ref, dens_in_ref, dens_out_ref, sums_ref, halves_in_ref, halves_out_ref, sems = refs
     rows = vr_ref.shape[1]
     copies = [pltpu.make_async_copy(kept[n], outs[n], sems.at[n]) for n in range(5)]
     density_ref, vr_out, va_out, gvr_out, gva_out = kept
     drag(
-        count, table_ref, gas_ref, gvr_ref, gva_ref, vr_ref, va_ref, messages,
+        count, passing_ref, table_ref, gas_ref, gvr_ref, gva_ref, vr_ref, va_ref, messages,
         vr_out, va_out, gvr_out, gva_out, sums_ref, halves_in_ref, halves_out_ref,
     )
     for copy in copies[1:]:
@@ -284,8 +299,9 @@
     add_blocks(weights_ref, messages[:count], count, count // 2 + 1, count, dens_in_ref, new_in_ref, gain_in_ref)
     for n, r in enumerate(inner_rows(rows)):
         density_ref[:, r, :] = adv_in_ref[n] + COAGULATION * new_in_ref[n]
+    add_blocks(weights_ref, messages[count:], count, count - 1, count, dens_out_ref, new_out_ref, gain_out_ref)
     for n, r in enumerate(outer_rows(rows)):
-        density_ref[:, r, :] = adv_out_ref[n] + COAGULATION * gain_out_ref[n]
+        density_ref[:, r, :] = adv_out_ref[n] + COAGULATION * new_out_ref[n]
     copies[0].start()
     for copy in copies:
         copy.wait()
@@ -351,11 +367,12 @@
     groups = lax.axis_size("bin")
     half = groups // 2
     dense = [pltpu.VMEM((len(picked), bins, cells), F32) for picked in (inner, outer)]
-    low_in, adv_in, part_out = call(
-        inner_kernel, (pltpu.VMEM((inner_lines, cells), BF16), *dense), table, rho, vr, va,
+    low_in, plain_in, adv_in, part_out = call(
+        inner_kernel,
+        (pltpu.VMEM((inner_lines, cells), BF16), pltpu.VMEM((bins * len(inner), cells), BF16), *dense), table, rho, vr, va,
         scratch=[kept, halves_in],
     )
-    near_in = [lax.ppermute(low_in, "bin", xor_pairs("bin", at)) for at in range(1, half)]
+    near_in = [lax.ppermute(plain_in, "bin", xor_pairs("bin", at)) for at in range(1, half)]
     far_in = lax.ppermute(low_in, "bin", xor_pairs("bin", half))
 
     adv_out, low_out = call(
@@ -364,25 +381,24 @@
     )
     near_out = [lax.ppermute(low_out, "bin", xor_pairs("bin", at)) for at in range(1, half)]
     far_out = [lax.ppermute(low_out, "bin", xor_pairs("bin", at)) for at in range(half, groups)]
-    passed_in = [lax.ppermute(far_in, "bin", xor_pairs("bin", at)) for at in range(1, half)]
+    passing = call(pack_kernel, pltpu.VMEM((inner_lines, cells), BF16), low_in, far_in, scratch=[halves_in] * 2)
+    passed_in = [lax.ppermute(passing, "bin", xor_pairs("bin", at)) for at in range(1, half)]
 
     in_messages = [low_in] + near_in + [far_in] + passed_in
     out_messages = [low_out] + near_out + far_out
 
     dens = [pltpu.VMEM((len(picked), 2 * total, cells), BF16) for picked in (inner, outer)]
-    gain_in, gain_out = call(
-        functools.partial(first_gain_kernel, groups), tuple(dense), weights, *in_messages[:half + 1], *out_messages[:half],
-        scratch=dens, loose=() if small else (0,),
-    )
-    gain_out = call(
-        second_gain_kernel, dense[1], weights, gain_out, *out_messages, scratch=dens[1:], loose=() if small else (0,),
-    )
+    gains = []
+    for n, some in ((0, in_messages[:half + 1]), (1, out_messages[:-1])):
+        gains.append(call(
+            functools.partial(gain_kernel, groups), dense[n], weights, *some, scratch=dens[n:n + 1], loose=() if small else (0,),
+        ))
     return call(
         functools.partial(last_kernel, groups), (field, field, field, flat, flat),
-        table, gas, gvr, gva, vr, va, weights, adv_in, adv_out, gain_in, gain_out, *in_messages, *out_messages,
-        scratch=[kept] * 3 + [pltpu.VMEM(gas.shape, F32)] * 2 + dense[:1] + dens[:1]
-        + [pltpu.VMEM((groups, 3, rows, cells), F32), halves_in, halves_out, pltpu.SemaphoreType.DMA((5,))],
-        loose=() if small else (6,), spec=ANY,
+        passing, table, gas, gvr, gva, vr, va, weights, adv_in, adv_out, *gains, *in_messages, *out_messages,
+        scratch=[kept] * 3 + [pltpu.VMEM(gas.shape, F32)] * 2 + dense + dens
+        + [pltpu.VMEM((half + groups, 3, rows, cells), F32), halves_in, halves_out, pltpu.SemaphoreType.DMA((5,))],
+        loose=() if small else (7,), spec=ANY,
     )
 
 

time: 26.3 us -> 30 us (1.14)
  waiting for transfers between devices: 3.61 us -> 8.33 us
  starting transfers between devices: 14.3 us -> 13.2 us
    ppermute x2, waiting for transfers between devices: 0.01 us -> 6.47 us  [the longest x1 6.46 us: body(): lax.ppermute(plain_in, 'bin', xor_pairs('bin', at))]
    ppermute x3, waiting for transfers between devices: 3.33 us -> 0.01 us  [body(): lax.ppermute(low_out, 'bin', xor_pairs('bin', at))]
    ppermute x2, starting transfers between devices: 4.05 us -> 2.09 us  [the longest x1 1.35 us: body(): lax.ppermute(plain_in, 'bin', xor_pairs('bin', at))]
    ppermute x1, waiting for transfers between devices: 0.27 us -> 1.85 us  [body(): from_b = lax.ppermute(to_b, 'tile', odd_pairs('tile'))]
    ppermute x3, starting transfers between devices: 3.55 us -> 4.45 us  [body(): lax.ppermute(low_out, 'bin', xor_pairs('bin', at))]
    pallas_call x7 -> x8, Pallas kernels: 6.85 us -> 6.95 us  [call(): pl.pallas_call(kernel, out_shape=outs, in_specs=specs, out_specs=jax.tree...]
  transfers between devices with their start and end apart: 8 -> 8, of which waited for: 3 -> 2; matrix products, arithmetic and copies ran while one was open for 2% -> 1% of each run, Pallas kernels for 11% -> 9%
where the time goes in v6:
time: 30 us; the launch traced here: 29.8 us
  starting transfers between devices  13.2 us (44%)
  waiting for transfers between devices  8.33 us (28%)
  Pallas kernels  6.95 us (23%)
  between operations  0.81 us (3%)
  local copies, waits for them, and re-layouts  0.52 us (2%)
    pallas_call x8, Pallas kernels, call(): pl.pallas_call(kernel, out_shape=outs, in_specs=specs, out_specs=jax.tree...  6.95 us
    ppermute x1, waiting for transfers between devices, body(): lax.ppermute(plain_in, 'bin', xor_pairs('bin', at))  6.46 us
    ppermute x3, starting transfers between devices, body(): lax.ppermute(low_out, 'bin', xor_pairs('bin', at))  4.45 us
    ppermute x1, starting transfers between devices, body(): far_in = lax.ppermute(low_in, 'bin', xor_pairs('bin', half))  4.13 us
    ppermute x1, starting transfers between devices, body(): from_b = lax.ppermute(to_b, 'tile', odd_pairs('tile'))  2.56 us
    ppermute x1, waiting for transfers between devices, body(): from_b = lax.ppermute(to_b, 'tile', odd_pairs('tile'))  1.85 us
    ppermute x1, starting transfers between devices, body(): lax.ppermute(plain_in, 'bin', xor_pairs('bin', at))  1.35 us
    ppermute x1, starting transfers between devices, body(): lax.ppermute(passing, 'bin', xor_pairs('bin', at))  0.74 us
  transfers between devices with their start and end apart: 8, of which 2 were waited for; matrix products, arithmetic and copies ran while one was open for 1% of the time, Pallas kernels for 9%

profile of v6, /device:TPU:0, one launch (start us, length us, event | category | flops | bytes accessed | tf_op | source)
XLA Modules:
  0.0 29.8 jit_solution(9255134183129238129)
XLA Ops:
  0.7 1.3 %shard_map.119 = (bf16[3,16,512]{2,1,0:T(8,128)(2,1)S(1)}, bf16[3,16,512]{2,1,0:T(8,128)(2,1)S(1)}, f32[6,16,512]{2,1,0:T(8,128)S(1)}, f32[4,16,512]{2,1,0:T(8,1...) custom-call(f32[16,8,512]{2,1,0:T(8,128)} %rho_ref.1, f32[16,8,512]{2,1,0:T(8,128)} %vr_ref.3, ...), custom_call_target="tpu_custom_call" | custom-call | tf_op jit(solution)/shard_map/pallas_call | solution.py:317
  1.9 0.0 copy-done
  2.0 0.0 copy-done.1
  2.0 0.1 copy-done.2
  2.0 1.1 %shard_map.120 = (bf16[88,512]{1,0:T(8,128)(2,1)S(1)}, bf16[64,512]{1,0:T(8,128)(2,1)S(1)}, f32[4,16,512]{2,1,0:T(8,128)S(1)}, f32[4,16,512]{2,1,0:T(8,128)S(1)}) custom-call(f32[2,16,512]{2,1,0:T(8,128)S(1)} %get-tuple-element.17.table_ref, f32[16,8,512]{2,1,0:T(8,128)S(1)} %copy-done.2, f32[16,8,512]{2,1,0:T(8,128)S(1)} %copy-done, f32[16,8,512]{2,1,0:T(8,128)S(1)} %copy-done.1), custom_call_target="tpu_custom_call" | custom-call | tf_op jit(solution)/shard_map/pallas_call | solution.py:317
  3.2 4.1 %collective-permute-start = (bf16[88,512]{1,0:T(8,128)(2,1)S(1)}, bf16[88,512]{1,0:T(8,128)(2,1)S(1)}, u32[]{:S(2)}, u32[]{:S(2)}) collective-permute-start(bf16[88,512]{1,0:T(8,128)(2,1)S(1)} %get-tuple-element.18.own_ref.refs_0_), channel_id=1, source_target_pairs={{0,2},{1,3},{2,0},{3,1},{4,6},{5,7},{6,4},{7,5},{8,10},{9,11},{10,... | collective-permute-start | bytes 270344 | tf_op jit(solution)/shard_map/ppermute | solution.py:376
  7.3 0.0 collective-permute-start.1
  7.3 2.6 %collective-permute-start.2 = (bf16[3,16,512]{2,1,0:T(8,128)(2,1)S(1)}, bf16[3,16,512]{2,1,0:T(8,128)(2,1)S(1)}, u32[]{:S(2)}, u32[]{:S(2)}) collective-permute-start(bf16[3,16,512]{2,1,0:T(8,128)(2,1)S(1)} %get-tuple-element.25), channel_id=1, source_target_pairs={{0,28},{28,0},{4,8},{8,4},{12,16},{16,12},{20,24},{24,20},{1,29},{... | collective-permute-start | bytes 147464 | tf_op jit(solution)/shard_map/ppermute | solution.py:364
  9.8 0.0 collective-permute-done.1.from_a_ref
  9.9 1.9 %collective-permute-done.2.from_b_ref = bf16[3,16,512]{2,1,0:T(8,128)(2,1)S(1)} collective-permute-done((bf16[3,16,512]{2,1,0:T(8,128)(2,1)S(1)}, bf16[3,16,512]{2,1,0:T(8,128)(2,1)S(1)}, u32[]{:S(2)}, u32[]{:S(2)}) %collective-permute-start.2) | collective-permute-done | bytes 49184 | tf_op jit(solution)/shard_map/ppermute | solution.py:364
  11.7 0.3 shard_map.123
  12.0 0.0 copy-start.6
  12.0 1.4 %collective-permute-start.7 = (bf16[88,512]{1,0:T(8,128)(2,1)S(1)}, bf16[88,512]{1,0:T(8,128)(2,1)S(1)}, u32[]{:S(2)}, u32[]{:S(2)}) collective-permute-start(bf16[88,512]{1,0:T(8,128)(2,1)S(1)} %get-tuple-element.28.refs_0_.refs_4_), channel_id=1, source_target_pairs={{0,3},{1,2},{2,1},{3,0},{4,7},{5,6},{6,5},{7,4},{8,11},{9,10},{10,... | collective-permute-start | bytes 270344 | tf_op jit(solution)/shard_map/ppermute | solution.py:383
  13.4 1.7 %collective-permute-start.5 = (bf16[88,512]{1,0:T(8,128)(2,1)S(1)}, bf16[88,512]{1,0:T(8,128)(2,1)S(1)}, u32[]{:S(2)}, u32[]{:S(2)}) collective-permute-start(bf16[88,512]{1,0:T(8,128)(2,1)S(1)} %get-tuple-element.28.refs_0_.refs_4_), channel_id=1, source_target_pairs={{0,2},{1,3},{2,0},{3,1},{4,6},{5,7},{6,4},{7,5},{8,10},{9,11},{10,... | collective-permute-start | bytes 270344 | tf_op jit(solution)/shard_map/ppermute | solution.py:383
  15.1 1.3 %collective-permute-start.4 = (bf16[88,512]{1,0:T(8,128)(2,1)S(1)}, bf16[88,512]{1,0:T(8,128)(2,1)S(1)}, u32[]{:S(2)}, u32[]{:S(2)}) collective-permute-start(bf16[88,512]{1,0:T(8,128)(2,1)S(1)} %get-tuple-element.28.refs_0_.refs_4_), channel_id=1, source_target_pairs={{0,1},{1,0},{2,3},{3,2},{4,5},{5,4},{6,7},{7,6},{8,9},{9,8},{10,11... | collective-permute-start | bytes 270344 | tf_op jit(solution)/shard_map/ppermute | solution.py:382
  16.5 0.0 collective-permute-done.far_ref.refs_2_
  16.5 0.7 %collective-permute-start.6 = (bf16[88,512]{1,0:T(8,128)(2,1)S(1)}, bf16[88,512]{1,0:T(8,128)(2,1)S(1)}, u32[]{:S(2)}, u32[]{:S(2)}) collective-permute-start(bf16[88,512]{1,0:T(8,128)(2,1)S(1)} %shard_map.121.passing_ref), channel_id=1, source_target_pairs={{0,1},{1,0},{2,3},{3,2},{4,5},{5,4},{6,7},{7,6},{8,9},{9,8},{10,11... | collective-permute-start | bytes 270344 | tf_op jit(solution)/shard_map/ppermute | solution.py:385
  17.2 1.3 %collective-permute-start.3 = (bf16[64,512]{1,0:T(8,128)(2,1)S(1)}, bf16[64,512]{1,0:T(8,128)(2,1)S(1)}, u32[]{:S(2)}, u32[]{:S(2)}) collective-permute-start(bf16[64,512]{1,0:T(8,128)(2,1)S(1)} %get-tuple-element.27), channel_id=1, source_target_pairs={{0,1},{1,0},{2,3},{3,2},{4,5},{5,4},{6,7},{7,6},{8,9},{9,8},{10,11... | collective-permute-start | bytes 196616 | tf_op jit(solution)/shard_map/ppermute | solution.py:375
  18.6 0.2 copy.13
  18.8 0.3 copy.14
  19.0 0.3 %shard_map.122.weights_ref = bf16[1024,128]{1,0:T(8,128)(2,1)S(1)} custom-call(bf16[1024,64]{1,0:T(8,128)(2,1)S(1)} %bitcast.5, bf16[1024,64]{1,0:T(8,128)(2,1)S(1)} %bitcast.6), custom_call_target="tpu_custom_call" | custom-call | tf_op jit(solution)/shard_map/pallas_call | solution.py:317
  19.4 6.5 %collective-permute-done.3.refs_1_ = bf16[64,512]{1,0:T(8,128)(2,1)S(1)} collective-permute-done((bf16[64,512]{1,0:T(8,128)(2,1)S(1)}, bf16[64,512]{1,0:T(8,128)(2,1)S(1)}, u32[]{:S(2)}, u32[]{:S(2)}) %collective-permute-start.3) | collective-permute-done | bytes 65568 | tf_op jit(solution)/shard_map/ppermute | solution.py:375
  25.8 1.0 %shard_map.124.gain_in_ref = f32[4,16,512]{2,1,0:T(8,128)S(1)} custom-call(bf16[1024,128]{1,0:T(8,128)(2,1)S(1)} %shard_map.122.weights_ref, bf16[88,512]{1,0:T(8,128)(2,1)S(1)} %get-tuple-element.18.own_ref.refs_0_, bf16[64,512]{1,0:T(8,128)(2,1)S(1)} %collective-permute-done.3.refs_1_, bf16[88,512]{1,0:T(8,128)(2,1)S(1)} %collective-permute-done.far_ref.refs_2_), custom_call_target="tpu_custom_call" | custom-call | tf_op jit(solution)/shard_map/pallas_call | solution.py:317
  26.9 0.0 copy-start.3
  26.9 0.0 copy-start.4
  26.9 0.0 copy-start.5
  26.9 0.0 collective-permute-done.5.refs_2_.refs_6_
  26.9 0.0 collective-permute-done.4.refs_1_.refs_5_
  26.9 1.0 %shard_map.125.gain_out_ref = f32[4,16,512]{2,1,0:T(8,128)S(1)} custom-call(bf16[1024,128]{1,0:T(8,128)(2,1)S(1)} %shard_map.122.weights_ref, bf16[88,512]{1,0:T(8,128)(2,1)S(1)} %get-tuple-element.28.refs_0_.refs_4_, bf16[88,512]{1,0:T(8,128)(2,1)S(1)} %collective-permute-done.4.refs_1_.refs_5_, bf16[88,512]{1,0:T(8,128)(2,1)S(1)} %collective-permute-done.5.refs_2_.refs_6_), custom_call_target="tpu_custom_call" | custom-call | tf_op jit(solution)/shard_map/pallas_call | solution.py:317
  27.9 0.0 collective-permute-done.7.refs_7_
  27.9 0.0 collective-permute-done.6.refs_3_
  28.0 1.9 %shard_map.126 = (f32[16,8,512]{2,1,0:T(8,128)}, f32[16,8,512]{2,1,0:T(8,128)}, f32[16,8,512]{2,1,0:T(8,128)}, f32[8,512]{1,0:T(8,128)}, f32[8,512]{1,0:T(8,128)}) custom-call(bf16[88,512]{1,0:T(8,128)(2,1)S(1)} %shard_map.121.passing_ref, f32[2,16,512]{2,1,0:T(8,128)S(1)} %get-tuple-element.17.table_ref, f32[8,512]{1,0:T(8,128)S(1)} %copy-done.3, ...), custom_call_target="tpu_custom_call" | custom-call | tf_op jit(solution)/shard_map/pallas_call | solution.py:317
  (8 shorter events, 0.1 us)
Async XLA Ops:
  0.6 1.3 %copy-start = (f32[16,8,512]{2,1,0:T(8,128)S(1)}, f32[16,8,512]{2,1,0:T(8,128)}, u32[]{:S(2)}) copy-start(f32[16,8,512]{2,1,0:T(8,128)} %vr_ref.3) | copy-start | bytes 786436
  0.6 1.3 %copy-start.1 = (f32[16,8,512]{2,1,0:T(8,128)S(1)}, f32[16,8,512]{2,1,0:T(8,128)}, u32[]{:S(2)}) copy-start(f32[16,8,512]{2,1,0:T(8,128)} %va_ref.3) | copy-start | bytes 786436
  0.7 1.4 %copy-start.2 = (f32[16,8,512]{2,1,0:T(8,128)S(1)}, f32[16,8,512]{2,1,0:T(8,128)}, u32[]{:S(2)}) copy-start(f32[16,8,512]{2,1,0:T(8,128)} %rho_ref.1) | copy-start | bytes 786436
  3.2 13.3 %collective-permute-start = (bf16[88,512]{1,0:T(8,128)(2,1)S(1)}, bf16[88,512]{1,0:T(8,128)(2,1)S(1)}, u32[]{:S(2)}, u32[]{:S(2)}) collective-permute-start(bf16[88,512]{1,0:T(8,128)(2,1)S(1)} %get-tuple-element.18.own_ref.refs_0_), channel_id=1, source_target_pairs={{0,2},{1,3},{2,0},{3,1},{4,6},{5,7},{6,4},{7,5},{8,10},{9,11},{10,... | collective-permute-start | bytes 270344 | tf_op jit(solution)/shard_map/ppermute | solution.py:376
  7.3 2.6 %collective-permute-start.1 = (bf16[3,16,512]{2,1,0:T(8,128)(2,1)S(1)}, bf16[3,16,512]{2,1,0:T(8,128)(2,1)S(1)}, u32[]{:S(2)}, u32[]{:S(2)}) collective-permute-start(bf16[3,16,512]{2,1,0:T(8,128)(2,1)S(1)} %get-tuple-element.24), channel_id=1, source_target_pairs={{0,4},{4,0},{8,12},{12,8},{16,20},{20,16},{24,28},{28,24},{1,5},{5... | collective-permute-start | bytes 147464 | tf_op jit(solution)/shard_map/ppermute | solution.py:365
  7.3 4.4 %collective-permute-start.2 = (bf16[3,16,512]{2,1,0:T(8,128)(2,1)S(1)}, bf16[3,16,512]{2,1,0:T(8,128)(2,1)S(1)}, u32[]{:S(2)}, u32[]{:S(2)}) collective-permute-start(bf16[3,16,512]{2,1,0:T(8,128)(2,1)S(1)} %get-tuple-element.25), channel_id=1, source_target_pairs={{0,28},{28,0},{4,8},{8,4},{12,16},{16,12},{20,24},{24,20},{1,29},{... | collective-permute-start | bytes 147464 | tf_op jit(solution)/shard_map/ppermute | solution.py:364
  12.0 6.6 %copy-start.6 = (bf16[16,64,64]{2,1,0:T(8,128)(2,1)S(1)}, bf16[16,64,64]{2,1,0:T(8,128)(2,1)}, u32[]{:S(2)}) copy-start(bf16[16,64,64]{2,1,0:T(8,128)(2,1)} %param.15) | copy-start | bytes 393220
  12.0 15.9 %collective-permute-start.7 = (bf16[88,512]{1,0:T(8,128)(2,1)S(1)}, bf16[88,512]{1,0:T(8,128)(2,1)S(1)}, u32[]{:S(2)}, u32[]{:S(2)}) collective-permute-start(bf16[88,512]{1,0:T(8,128)(2,1)S(1)} %get-tuple-element.28.refs_0_.refs_4_), channel_id=1, source_target_pairs={{0,3},{1,2},{2,1},{3,0},{4,7},{5,6},{6,5},{7,4},{8,11},{9,10},{10,... | collective-permute-start | bytes 270344 | tf_op jit(solution)/shard_map/ppermute | solution.py:383
  13.4 13.5 %collective-permute-start.5 = (bf16[88,512]{1,0:T(8,128)(2,1)S(1)}, bf16[88,512]{1,0:T(8,128)(2,1)S(1)}, u32[]{:S(2)}, u32[]{:S(2)}) collective-permute-start(bf16[88,512]{1,0:T(8,128)(2,1)S(1)} %get-tuple-element.28.refs_0_.refs_4_), channel_id=1, source_target_pairs={{0,2},{1,3},{2,0},{3,1},{4,6},{5,7},{6,4},{7,5},{8,10},{9,11},{10,... | collective-permute-start | bytes 270344 | tf_op jit(solution)/shard_map/ppermute | solution.py:383
  15.1 11.8 %collective-permute-start.4 = (bf16[88,512]{1,0:T(8,128)(2,1)S(1)}, bf16[88,512]{1,0:T(8,128)(2,1)S(1)}, u32[]{:S(2)}, u32[]{:S(2)}) collective-permute-start(bf16[88,512]{1,0:T(8,128)(2,1)S(1)} %get-tuple-element.28.refs_0_.refs_4_), channel_id=1, source_target_pairs={{0,1},{1,0},{2,3},{3,2},{4,5},{5,4},{6,7},{7,6},{8,9},{9,8},{10,11... | collective-permute-start | bytes 270344 | tf_op jit(solution)/shard_map/ppermute | solution.py:382
  16.5 11.4 %collective-permute-start.6 = (bf16[88,512]{1,0:T(8,128)(2,1)S(1)}, bf16[88,512]{1,0:T(8,128)(2,1)S(1)}, u32[]{:S(2)}, u32[]{:S(2)}) collective-permute-start(bf16[88,512]{1,0:T(8,128)(2,1)S(1)} %shard_map.121.passing_ref), channel_id=1, source_target_pairs={{0,1},{1,0},{2,3},{3,2},{4,5},{5,4},{6,7},{7,6},{8,9},{9,8},{10,11... | collective-permute-start | bytes 270344 | tf_op jit(solution)/shard_map/ppermute | solution.py:385
  17.2 8.6 %collective-permute-start.3 = (bf16[64,512]{1,0:T(8,128)(2,1)S(1)}, bf16[64,512]{1,0:T(8,128)(2,1)S(1)}, u32[]{:S(2)}, u32[]{:S(2)}) collective-permute-start(bf16[64,512]{1,0:T(8,128)(2,1)S(1)} %get-tuple-element.27), channel_id=1, source_target_pairs={{0,1},{1,0},{2,3},{3,2},{4,5},{5,4},{6,7},{7,6},{8,9},{9,8},{10,11... | collective-permute-start | bytes 196616 | tf_op jit(solution)/shard_map/ppermute | solution.py:375
  26.9 1.1 %copy-start.3 = (f32[8,512]{1,0:T(8,128)S(1)}, f32[8,512]{1,0:T(8,128)}, u32[]{:S(2)}) copy-start(f32[8,512]{1,0:T(8,128)} %gas_ref.1) | copy-start | bytes 49156
  26.9 1.1 %copy-start.4 = (f32[8,512]{1,0:T(8,128)S(1)}, f32[8,512]{1,0:T(8,128)}, u32[]{:S(2)}) copy-start(f32[8,512]{1,0:T(8,128)} %gvr_ref.1) | copy-start | bytes 49156
  26.9 1.1 %copy-start.5 = (f32[8,512]{1,0:T(8,128)S(1)}, f32[8,512]{1,0:T(8,128)}, u32[]{:S(2)}) copy-start(f32[8,512]{1,0:T(8,128)} %gva_ref.1) | copy-start | bytes 49156

commit v7 on v6

--- a/solution.py
+++ b/solution.py
@@ -20,14 +20,13 @@
 
 
 def minmod(a, b):
-    return jnp.maximum(jnp.minimum(a, b), 0.0) + jnp.minimum(jnp.maximum(a, b), 0.0)
-
-
-def face_flux(low, low_slope, high, high_slope, u):
-    cu = COURANT * u
-    left = low + (0.5 - 0.5 * cu) * low_slope
-    right = high - (0.5 + 0.5 * cu) * high_slope
-    return jnp.maximum(u, 0.0) * left + jnp.minimum(u, 0.0) * right
+    return jnp.maximum(jnp.minimum(a, b), jnp.minimum(jnp.maximum(a, b), 0.0))
+
+
+def face_flux(low, low_slope, high, high_slope, low_speed, high_speed):
+    cu = low_speed + high_speed
+    reach = 0.5 - 0.5 * jnp.abs(cu)
+    return cu * jnp.where(cu > 0, low + reach * low_slope, high - reach * high_slope)
 
 
 def shift(x, by, axis):
@@ -74,7 +73,7 @@
     q_next = shift(q, -1, 0)
     d = q_next - q
     s = minmod(shift(d, 1, 0), d)
-    flux = face_flux(q, s, q_next, shift(s, -1, 0), 0.5 * (v + shift(v, -1, 0)))
+    flux = face_flux(q, s, q_next, shift(s, -1, 0), v, shift(v, -1, 0))
     flux = jnp.where((row >= HALO - 1) & (row < rows - HALO), flux, 0.0)
     return flux - shift(flux, 1, 0)
 
@@ -83,7 +82,7 @@
     q_next = shift(q, -1, 1)
     d = q_next - q
     s = minmod(shift(d, 1, 1), d)
-    flux = face_flux(q, s, q_next, shift(s, -1, 1), 0.5 * (v + shift(v, -1, 1)))
+    flux = face_flux(q, s, q_next, shift(s, -1, 1), v, shift(v, -1, 1))
     return flux - shift(flux, 1, 1)
 
 
@@ -131,7 +130,7 @@
     sums = (zero, zero, zero)
     for b in range(bins):
         q, vr, va = rho_ref[b], vr_ref[b], va_ref[b]
-        adv = q - COURANT * (azimuthal(q, va) + radial_inside(q, vr))
+        adv = q - (azimuthal(q, 0.5 * COURANT * va) + radial_inside(q, 0.5 * COURANT * vr))
         all_ref[b] = adv
         sums = weighed(sums, adv, vr, va, jnp.broadcast_to(table_ref[0, b:b + 1, :], q.shape))
     picked = inner_rows(rows)
@@ -159,13 +158,13 @@
         q = [halo[1], halo[0]] + nearest
         d = [sign * (q[n] - q[n + 1]) for n in range(4)]
         s = [minmod(d[n], d[n + 1]) for n in range(3)]
-        speed = [0.5 * (halo[2] + v[0]), 0.5 * (v[0] + v[1])]
+        speed = [0.5 * COURANT * x for x in (halo[2], v[0], v[1])]
         flux = []
         for n in range(2):
             low, high = (n, n + 1) if sign < 0 else (n + 1, n)
-            flux.append(face_flux(q[low + 1], s[low], q[high + 1], s[high], speed[n]))
-        outermost = nearest_part[0] - COURANT * sign * (flux[0] - flux[1])
-        return outermost, nearest_part[1] - COURANT * sign * flux[1]
+            flux.append(face_flux(q[low + 1], s[low], q[high + 1], s[high], speed[n], speed[n + 1]))
+        outermost = nearest_part[0] - sign * (flux[0] - flux[1])
+        return outermost, nearest_part[1] - sign * flux[1]
 
     row = [rho_ref[n] for n in range(rho_ref.shape[0])]
     speed = [vr_ref[n] for n in range(vr_ref.shape[0])]
@@ -281,12 +280,18 @@
     add_blocks(weights_ref, messages, count, 0, len(messages), dens_ref, gain_ref, None)
 
 
+def last_block_kernel(weights_ref, old_ref, *refs):
+    messages, (gain_ref, dens_ref) = refs[:-2], refs[-2:]
+    count = len(messages)
+    add_blocks(weights_ref, messages, count, count - 1, count, dens_ref, gain_ref, old_ref)
+
+
 def last_kernel(
     count, passing_ref, table_ref, gas_ref, gvr_ref, gva_ref, vr_ref, va_ref, weights_ref, adv_in_ref, adv_out_ref, gain_in_ref, gain_out_ref, *refs
 ):
-    messages, refs = refs[:-18], refs[-18:]
+    messages, refs = refs[:-16], refs[-16:]
     outs, kept, refs = refs[:5], refs[5:10], refs[10:]
-    new_in_ref, new_out_ref, dens_in_ref, dens_out_ref, sums_ref, halves_in_ref, halves_out_ref, sems = refs
+    new_in_ref, dens_in_ref, sums_ref, halves_in_ref, halves_out_ref, sems = refs
     rows = vr_ref.shape[1]
     copies = [pltpu.make_async_copy(kept[n], outs[n], sems.at[n]) for n in range(5)]
     density_ref, vr_out, va_out, gvr_out, gva_out = kept
@@ -299,9 +304,8 @@
     add_blocks(weights_ref, messages[:count], count, count // 2 + 1, count, dens_in_ref, new_in_ref, gain_in_ref)
     for n, r in enumerate(inner_rows(rows)):
         density_ref[:, r, :] = adv_in_ref[n] + COAGULATION * new_in_ref[n]
-    add_blocks(weights_ref, messages[count:], count, count - 1, count, dens_out_ref, new_out_ref, gain_out_ref)
     for n, r in enumerate(outer_rows(rows)):
-        density_ref[:, r, :] = adv_out_ref[n] + COAGULATION * new_out_ref[n]
+        density_ref[:, r, :] = adv_out_ref[n] + COAGULATION * gain_out_ref[n]
     copies[0].start()
     for copy in copies:
         copy.wait()
@@ -393,10 +397,13 @@
         gains.append(call(
             functools.partial(gain_kernel, groups), dense[n], weights, *some, scratch=dens[n:n + 1], loose=() if small else (0,),
         ))
+    gains[1] = call(
+        last_block_kernel, dense[1], weights, gains[1], *out_messages, scratch=dens[1:], loose=() if small else (0,),
+    )
     return call(
         functools.partial(last_kernel, groups), (field, field, field, flat, flat),
         passing, table, gas, gvr, gva, vr, va, weights, adv_in, adv_out, *gains, *in_messages, *out_messages,
-        scratch=[kept] * 3 + [pltpu.VMEM(gas.shape, F32)] * 2 + dense + dens
+        scratch=[kept] * 3 + [pltpu.VMEM(gas.shape, F32)] * 2 + dense[:1] + dens[:1]
         + [pltpu.VMEM((half + groups, 3, rows, cells), F32), halves_in, halves_out, pltpu.SemaphoreType.DMA((5,))],
         loose=() if small else (7,), spec=ANY,
     )

time: 30 us -> 28.9 us (0.963)
  waiting for transfers between devices: 8.33 us -> 6.93 us
    ppermute x1, waiting for transfers between devices: 6.46 us -> 5.06 us  [body(): lax.ppermute(plain_in, 'bin', xor_pairs('bin', at))]
    pallas_call x8 -> x9, Pallas kernels: 6.95 us -> 6.98 us  [call(): pl.pallas_call(kernel, out_shape=outs, in_specs=specs, out_specs=jax.tree...]
  transfers between devices with their start and end apart: 8 -> 8, of which waited for: 2 -> 2; matrix products, arithmetic and copies ran while one was open for 1% -> 1% of each run, Pallas kernels for 9% -> 11%
where the time goes in v7:
time: 28.9 us; the launch traced here: 28.7 us
  starting transfers between devices  13.2 us (46%)
  Pallas kernels  6.98 us (24%)
  waiting for transfers between devices  6.93 us (24%)
  between operations  0.79 us (3%)
  local copies, waits for them, and re-layouts  0.74 us (3%)
    pallas_call x9, Pallas kernels, call(): pl.pallas_call(kernel, out_shape=outs, in_specs=specs, out_specs=jax.tree...  6.98 us
    ppermute x1, waiting for transfers between devices, body(): lax.ppermute(plain_in, 'bin', xor_pairs('bin', at))  5.06 us
    ppermute x3, starting transfers between devices, body(): lax.ppermute(low_out, 'bin', xor_pairs('bin', at))  4.45 us
    ppermute x1, starting transfers between devices, body(): far_in = lax.ppermute(low_in, 'bin', xor_pairs('bin', half))  4.13 us
    ppermute x1, starting transfers between devices, body(): from_b = lax.ppermute(to_b, 'tile', odd_pairs('tile'))  2.56 us
    ppermute x1, waiting for transfers between devices, body(): from_b = lax.ppermute(to_b, 'tile', odd_pairs('tile'))  1.85 us
    ppermute x1, starting transfers between devices, body(): lax.ppermute(plain_in, 'bin', xor_pairs('bin', at))  1.35 us
    ppermute x1, starting transfers between devices, body(): lax.ppermute(passing, 'bin', xor_pairs('bin', at))  0.74 us
  transfers between devices with their start and end apart: 8, of which 2 were waited for; matrix products, arithmetic and copies ran while one was open for 1% of the time, Pallas kernels for 11%

profile of v7, /device:TPU:0, one launch (start us, length us, event | category | flops | bytes accessed | tf_op | source)
XLA Modules:
  0.0 28.7 jit_solution(15898895066503802624)
XLA Ops:
  0.7 1.3 %shard_map.119 = (bf16[3,16,512]{2,1,0:T(8,128)(2,1)S(1)}, bf16[3,16,512]{2,1,0:T(8,128)(2,1)S(1)}, f32[6,16,512]{2,1,0:T(8,128)S(1)}, f32[4,16,512]{2,1,0:T(8,1...) custom-call(f32[16,8,512]{2,1,0:T(8,128)} %rho_ref.1, f32[16,8,512]{2,1,0:T(8,128)} %vr_ref.3, ...), custom_call_target="tpu_custom_call" | custom-call | tf_op jit(solution)/shard_map/pallas_call | solution.py:321
  2.0 0.1 copy-done.2
  2.0 1.1 %shard_map.120 = (bf16[88,512]{1,0:T(8,128)(2,1)S(1)}, bf16[64,512]{1,0:T(8,128)(2,1)S(1)}, f32[4,16,512]{2,1,0:T(8,128)S(1)}, f32[4,16,512]{2,1,0:T(8,128)S(1)}) custom-call(f32[2,16,512]{2,1,0:T(8,128)S(1)} %get-tuple-element.17.table_ref, f32[16,8,512]{2,1,0:T(8,128)S(1)} %copy-done.2, f32[16,8,512]{2,1,0:T(8,128)S(1)} %copy-done, f32[16,8,512]{2,1,0:T(8,128)S(1)} %copy-done.1), custom_call_target="tpu_custom_call" | custom-call | tf_op jit(solution)/shard_map/pallas_call | solution.py:321
  3.1 4.1 %collective-permute-start = (bf16[88,512]{1,0:T(8,128)(2,1)S(1)}, bf16[88,512]{1,0:T(8,128)(2,1)S(1)}, u32[]{:S(2)}, u32[]{:S(2)}) collective-permute-start(bf16[88,512]{1,0:T(8,128)(2,1)S(1)} %get-tuple-element.18.own_ref.refs_0_), channel_id=1, source_target_pairs={{0,2},{1,3},{2,0},{3,1},{4,6},{5,7},{6,4},{7,5},{8,10},{9,11},{10,... | collective-permute-start | bytes 270344 | tf_op jit(solution)/shard_map/ppermute | solution.py:380
  7.2 0.0 collective-permute-start.1
  7.2 2.6 %collective-permute-start.2 = (bf16[3,16,512]{2,1,0:T(8,128)(2,1)S(1)}, bf16[3,16,512]{2,1,0:T(8,128)(2,1)S(1)}, u32[]{:S(2)}, u32[]{:S(2)}) collective-permute-start(bf16[3,16,512]{2,1,0:T(8,128)(2,1)S(1)} %get-tuple-element.25), channel_id=1, source_target_pairs={{0,28},{28,0},{4,8},{8,4},{12,16},{16,12},{20,24},{24,20},{1,29},{... | collective-permute-start | bytes 147464 | tf_op jit(solution)/shard_map/ppermute | solution.py:368
  9.8 0.0 collective-permute-done.1.from_a_ref
  9.8 1.9 %collective-permute-done.2.from_b_ref = bf16[3,16,512]{2,1,0:T(8,128)(2,1)S(1)} collective-permute-done((bf16[3,16,512]{2,1,0:T(8,128)(2,1)S(1)}, bf16[3,16,512]{2,1,0:T(8,128)(2,1)S(1)}, u32[]{:S(2)}, u32[]{:S(2)}) %collective-permute-start.2) | collective-permute-done | bytes 49184 | tf_op jit(solution)/shard_map/ppermute | solution.py:368
  11.6 0.3 shard_map.123
  11.9 0.0 copy-start.6
  11.9 0.3 %collective-permute-start.5 = (bf16[88,512]{1,0:T(8,128)(2,1)S(1)}, bf16[88,512]{1,0:T(8,128)(2,1)S(1)}, u32[]{:S(2)}, u32[]{:S(2)}) collective-permute-start(bf16[88,512]{1,0:T(8,128)(2,1)S(1)} %get-tuple-element.28.refs_0_.refs_4_), channel_id=1, source_target_pairs={{0,2},{1,3},{2,0},{3,1},{4,6},{5,7},{6,4},{7,5},{8,10},{9,11},{10,... | collective-permute-start | bytes 270344 | tf_op jit(solution)/shard_map/ppermute | solution.py:387
  12.2 1.7 %collective-permute-start.4 = (bf16[88,512]{1,0:T(8,128)(2,1)S(1)}, bf16[88,512]{1,0:T(8,128)(2,1)S(1)}, u32[]{:S(2)}, u32[]{:S(2)}) collective-permute-start(bf16[88,512]{1,0:T(8,128)(2,1)S(1)} %get-tuple-element.28.refs_0_.refs_4_), channel_id=1, source_target_pairs={{0,1},{1,0},{2,3},{3,2},{4,5},{5,4},{6,7},{7,6},{8,9},{9,8},{10,11... | collective-permute-start | bytes 270344 | tf_op jit(solution)/shard_map/ppermute | solution.py:386
  13.9 2.5 %collective-permute-start.6 = (bf16[88,512]{1,0:T(8,128)(2,1)S(1)}, bf16[88,512]{1,0:T(8,128)(2,1)S(1)}, u32[]{:S(2)}, u32[]{:S(2)}) collective-permute-start(bf16[88,512]{1,0:T(8,128)(2,1)S(1)} %get-tuple-element.28.refs_0_.refs_4_), channel_id=1, source_target_pairs={{0,3},{1,2},{2,1},{3,0},{4,7},{5,6},{6,5},{7,4},{8,11},{9,10},{10,... | collective-permute-start | bytes 270344 | tf_op jit(solution)/shard_map/ppermute | solution.py:387
  16.4 0.0 collective-permute-done.far_ref.refs_2_
  16.4 0.7 %collective-permute-start.7 = (bf16[88,512]{1,0:T(8,128)(2,1)S(1)}, bf16[88,512]{1,0:T(8,128)(2,1)S(1)}, u32[]{:S(2)}, u32[]{:S(2)}) collective-permute-start(bf16[88,512]{1,0:T(8,128)(2,1)S(1)} %shard_map.121.passing_ref), channel_id=1, source_target_pairs={{0,1},{1,0},{2,3},{3,2},{4,5},{5,4},{6,7},{7,6},{8,9},{9,8},{10,11... | collective-permute-start | bytes 270344 | tf_op jit(solution)/shard_map/ppermute | solution.py:389
  17.2 1.3 %collective-permute-start.3 = (bf16[64,512]{1,0:T(8,128)(2,1)S(1)}, bf16[64,512]{1,0:T(8,128)(2,1)S(1)}, u32[]{:S(2)}, u32[]{:S(2)}) collective-permute-start(bf16[64,512]{1,0:T(8,128)(2,1)S(1)} %get-tuple-element.27), channel_id=1, source_target_pairs={{0,1},{1,0},{2,3},{3,2},{4,5},{5,4},{6,7},{7,6},{8,9},{9,8},{10,11... | collective-permute-start | bytes 196616 | tf_op jit(solution)/shard_map/ppermute | solution.py:379
  18.5 0.2 copy.13
  18.7 0.3 copy.14
  18.9 0.3 %shard_map.122.weights_ref = bf16[1024,128]{1,0:T(8,128)(2,1)S(1)} custom-call(bf16[1024,64]{1,0:T(8,128)(2,1)S(1)} %bitcast.5, bf16[1024,64]{1,0:T(8,128)(2,1)S(1)} %bitcast.6), custom_call_target="tpu_custom_call" | custom-call | tf_op jit(solution)/shard_map/pallas_call | solution.py:321
  19.3 5.1 %collective-permute-done.3.refs_1_ = bf16[64,512]{1,0:T(8,128)(2,1)S(1)} collective-permute-done((bf16[64,512]{1,0:T(8,128)(2,1)S(1)}, bf16[64,512]{1,0:T(8,128)(2,1)S(1)}, u32[]{:S(2)}, u32[]{:S(2)}) %collective-permute-start.3) | collective-permute-done | bytes 65568 | tf_op jit(solution)/shard_map/ppermute | solution.py:379
  24.4 1.0 %shard_map.124.gain_in_ref = f32[4,16,512]{2,1,0:T(8,128)S(1)} custom-call(bf16[1024,128]{1,0:T(8,128)(2,1)S(1)} %shard_map.122.weights_ref, bf16[88,512]{1,0:T(8,128)(2,1)S(1)} %get-tuple-element.18.own_ref.refs_0_, bf16[64,512]{1,0:T(8,128)(2,1)S(1)} %collective-permute-done.3.refs_1_, bf16[88,512]{1,0:T(8,128)(2,1)S(1)} %collective-permute-done.far_ref.refs_2_), custom_call_target="tpu_custom_call" | custom-call | tf_op jit(solution)/shard_map/pallas_call | solution.py:321
  25.4 0.0 collective-permute-done.5.refs_2_.refs_6_
  25.4 0.0 collective-permute-done.4.refs_1_.refs_5_
  25.4 1.0 %shard_map.125.old_ref = f32[4,16,512]{2,1,0:T(8,128)S(1)} custom-call(bf16[1024,128]{1,0:T(8,128)(2,1)S(1)} %shard_map.122.weights_ref, bf16[88,512]{1,0:T(8,128)(2,1)S(1)} %get-tuple-element.28.refs_0_.refs_4_, bf16[88,512]{1,0:T(8,128)(2,1)S(1)} %collective-permute-done.4.refs_1_.refs_5_, bf16[88,512]{1,0:T(8,128)(2,1)S(1)} %collective-permute-done.5.refs_2_.refs_6_), custom_call_target="tpu_custom_call" | custom-call | tf_op jit(solution)/shard_map/pallas_call | solution.py:321
  26.4 0.0 copy-start.3
  26.4 0.0 copy-start.4
  26.4 0.0 copy-start.5
  26.4 0.5 %shard_map.126.gain_out_ref = f32[4,16,512]{2,1,0:T(8,128)S(1)} custom-call(bf16[1024,128]{1,0:T(8,128)(2,1)S(1)} %shard_map.122.weights_ref, f32[4,16,512]{2,1,0:T(8,128)S(1)} %shard_map.125.old_ref, bf16[88,512]{1,0:T(8,128)(2,1)S(1)} %get-tuple-element.28.refs_0_.refs_4_, bf16[88,512]{1,0:T(8,128)(2,1)S(1)} %collective-permute-done.4.refs_1_.refs_5_, ...), custom_call_target="tpu_custom_call" | custom-call | tf_op jit(solution)/shard_map/pallas_call | solution.py:321
  26.9 0.2 copy-done.3
  27.1 0.0 copy-done.4
  27.1 0.0 copy-done.5
  27.2 1.5 %shard_map.127 = (f32[16,8,512]{2,1,0:T(8,128)}, f32[16,8,512]{2,1,0:T(8,128)}, f32[16,8,512]{2,1,0:T(8,128)}, f32[8,512]{1,0:T(8,128)}, f32[8,512]{1,0:T(8,128)}) custom-call(bf16[88,512]{1,0:T(8,128)(2,1)S(1)} %shard_map.121.passing_ref, f32[2,16,512]{2,1,0:T(8,128)S(1)} %get-tuple-element.17.table_ref, f32[8,512]{1,0:T(8,128)S(1)} %copy-done.3, ...), custom_call_target="tpu_custom_call" | custom-call | tf_op jit(solution)/shard_map/pallas_call | solution.py:321
  (9 shorter events, 0.1 us)
Async XLA Ops:
  0.6 1.3 %copy-start = (f32[16,8,512]{2,1,0:T(8,128)S(1)}, f32[16,8,512]{2,1,0:T(8,128)}, u32[]{:S(2)}) copy-start(f32[16,8,512]{2,1,0:T(8,128)} %vr_ref.3) | copy-start | bytes 786436
  0.6 1.3 %copy-start.1 = (f32[16,8,512]{2,1,0:T(8,128)S(1)}, f32[16,8,512]{2,1,0:T(8,128)}, u32[]{:S(2)}) copy-start(f32[16,8,512]{2,1,0:T(8,128)} %va_ref.3) | copy-start | bytes 786436
  0.7 1.4 %copy-start.2 = (f32[16,8,512]{2,1,0:T(8,128)S(1)}, f32[16,8,512]{2,1,0:T(8,128)}, u32[]{:S(2)}) copy-start(f32[16,8,512]{2,1,0:T(8,128)} %rho_ref.1) | copy-start | bytes 786436
  3.1 13.3 %collective-permute-start = (bf16[88,512]{1,0:T(8,128)(2,1)S(1)}, bf16[88,512]{1,0:T(8,128)(2,1)S(1)}, u32[]{:S(2)}, u32[]{:S(2)}) collective-permute-start(bf16[88,512]{1,0:T(8,128)(2,1)S(1)} %get-tuple-element.18.own_ref.refs_0_), channel_id=1, source_target_pairs={{0,2},{1,3},{2,0},{3,1},{4,6},{5,7},{6,4},{7,5},{8,10},{9,11},{10,... | collective-permute-start | bytes 270344 | tf_op jit(solution)/shard_map/ppermute | solution.py:380
  7.2 2.6 %collective-permute-start.1 = (bf16[3,16,512]{2,1,0:T(8,128)(2,1)S(1)}, bf16[3,16,512]{2,1,0:T(8,128)(2,1)S(1)}, u32[]{:S(2)}, u32[]{:S(2)}) collective-permute-start(bf16[3,16,512]{2,1,0:T(8,128)(2,1)S(1)} %get-tuple-element.24), channel_id=1, source_target_pairs={{0,4},{4,0},{8,12},{12,8},{16,20},{20,16},{24,28},{28,24},{1,5},{5... | collective-permute-start | bytes 147464 | tf_op jit(solution)/shard_map/ppermute | solution.py:369
  7.2 4.4 %collective-permute-start.2 = (bf16[3,16,512]{2,1,0:T(8,128)(2,1)S(1)}, bf16[3,16,512]{2,1,0:T(8,128)(2,1)S(1)}, u32[]{:S(2)}, u32[]{:S(2)}) collective-permute-start(bf16[3,16,512]{2,1,0:T(8,128)(2,1)S(1)} %get-tuple-element.25), channel_id=1, source_target_pairs={{0,28},{28,0},{4,8},{8,4},{12,16},{16,12},{20,24},{24,20},{1,29},{... | collective-permute-start | bytes 147464 | tf_op jit(solution)/shard_map/ppermute | solution.py:368
  11.9 6.6 %copy-start.6 = (bf16[16,64,64]{2,1,0:T(8,128)(2,1)S(1)}, bf16[16,64,64]{2,1,0:T(8,128)(2,1)}, u32[]{:S(2)}) copy-start(bf16[16,64,64]{2,1,0:T(8,128)(2,1)} %param.15) | copy-start | bytes 393220
  11.9 13.5 %collective-permute-start.5 = (bf16[88,512]{1,0:T(8,128)(2,1)S(1)}, bf16[88,512]{1,0:T(8,128)(2,1)S(1)}, u32[]{:S(2)}, u32[]{:S(2)}) collective-permute-start(bf16[88,512]{1,0:T(8,128)(2,1)S(1)} %get-tuple-element.28.refs_0_.refs_4_), channel_id=1, source_target_pairs={{0,2},{1,3},{2,0},{3,1},{4,6},{5,7},{6,4},{7,5},{8,10},{9,11},{10,... | collective-permute-start | bytes 270344 | tf_op jit(solution)/shard_map/ppermute | solution.py:387
  12.2 13.2 %collective-permute-start.4 = (bf16[88,512]{1,0:T(8,128)(2,1)S(1)}, bf16[88,512]{1,0:T(8,128)(2,1)S(1)}, u32[]{:S(2)}, u32[]{:S(2)}) collective-permute-start(bf16[88,512]{1,0:T(8,128)(2,1)S(1)} %get-tuple-element.28.refs_0_.refs_4_), channel_id=1, source_target_pairs={{0,1},{1,0},{2,3},{3,2},{4,5},{5,4},{6,7},{7,6},{8,9},{9,8},{10,11... | collective-permute-start | bytes 270344 | tf_op jit(solution)/shard_map/ppermute | solution.py:386
  13.9 12.6 %collective-permute-start.6 = (bf16[88,512]{1,0:T(8,128)(2,1)S(1)}, bf16[88,512]{1,0:T(8,128)(2,1)S(1)}, u32[]{:S(2)}, u32[]{:S(2)}) collective-permute-start(bf16[88,512]{1,0:T(8,128)(2,1)S(1)} %get-tuple-element.28.refs_0_.refs_4_), channel_id=1, source_target_pairs={{0,3},{1,2},{2,1},{3,0},{4,7},{5,6},{6,5},{7,4},{8,11},{9,10},{10,... | collective-permute-start | bytes 270344 | tf_op jit(solution)/shard_map/ppermute | solution.py:387
  16.4 10.5 %collective-permute-start.7 = (bf16[88,512]{1,0:T(8,128)(2,1)S(1)}, bf16[88,512]{1,0:T(8,128)(2,1)S(1)}, u32[]{:S(2)}, u32[]{:S(2)}) collective-permute-start(bf16[88,512]{1,0:T(8,128)(2,1)S(1)} %shard_map.121.passing_ref), channel_id=1, source_target_pairs={{0,1},{1,0},{2,3},{3,2},{4,5},{5,4},{6,7},{7,6},{8,9},{9,8},{10,11... | collective-permute-start | bytes 270344 | tf_op jit(solution)/shard_map/ppermute | solution.py:389
  17.2 7.2 %collective-permute-start.3 = (bf16[64,512]{1,0:T(8,128)(2,1)S(1)}, bf16[64,512]{1,0:T(8,128)(2,1)S(1)}, u32[]{:S(2)}, u32[]{:S(2)}) collective-permute-start(bf16[64,512]{1,0:T(8,128)(2,1)S(1)} %get-tuple-element.27), channel_id=1, source_target_pairs={{0,1},{1,0},{2,3},{3,2},{4,5},{5,4},{6,7},{7,6},{8,9},{9,8},{10,11... | collective-permute-start | bytes 196616 | tf_op jit(solution)/shard_map/ppermute | solution.py:379
  26.4 0.7 %copy-start.3 = (f32[8,512]{1,0:T(8,128)S(1)}, f32[8,512]{1,0:T(8,128)}, u32[]{:S(2)}) copy-start(f32[8,512]{1,0:T(8,128)} %gas_ref.1) | copy-start | bytes 49156
  26.4 0.7 %copy-start.4 = (f32[8,512]{1,0:T(8,128)S(1)}, f32[8,512]{1,0:T(8,128)}, u32[]{:S(2)}) copy-start(f32[8,512]{1,0:T(8,128)} %gvr_ref.1) | copy-start | bytes 49156
  26.4 0.7 %copy-start.5 = (f32[8,512]{1,0:T(8,128)S(1)}, f32[8,512]{1,0:T(8,128)}, u32[]{:S(2)}) copy-start(f32[8,512]{1,0:T(8,128)} %gva_ref.1) | copy-start | bytes 49156

commit v8 on v7

--- a/solution.py
+++ b/solution.py
@@ -202,33 +202,24 @@
     return total_sums(at, offset, bit // 2) + total_sums(at, offset ^ bit, bit // 2)
 
 
-def drag(count, passing_ref, table_ref, gas_ref, gvr_ref, gva_ref, vr_ref, va_ref, messages, vr_out, va_out, gvr_out, gva_out, sums_ref, halves_in_ref, halves_out_ref):
-    bins, rows, _ = vr_ref.shape
-    half = count // 2
-    for offset in range(half):
-        passed = messages[half + offset] if offset else passing_ref
-        read_sums(passed, inner_rows(rows), bins, halves_in_ref, sums_ref.at[offset])
-    for offset in range(count):
-        read_sums(messages[count + offset], outer_rows(rows), bins, halves_out_ref, sums_ref.at[half + offset])
-    inner = [total_sums(lambda o, n=n: sums_ref[o, n], 0, half // 2) for n in range(3)]
-    outer = [total_sums(lambda o, n=n: sums_ref[half + o, n], 0, half) for n in range(3)]
-    row = lax.broadcasted_iota(jnp.int32, gas_ref.shape, 0)
+def new_gas(passed, total_ref, gases_ref, bins, sums_ref, halves_ref):
+    gas = gases_ref[0]
+    rows = gas.shape[0]
+    for offset, message in enumerate(passed):
+        read_sums(message, inner_rows(rows), bins, halves_ref, sums_ref.at[offset])
+    row = lax.broadcasted_iota(jnp.int32, gas.shape, 0)
     inside = (row >= HALO) & (row < rows - HALO)
-    sums = [jnp.where(inside, inner[n], outer[n]) for n in range(3)]
-    gas = gas_ref[...]
+    sums = []
+    for n in range(3):
+        inner = total_sums(lambda o, n=n: sums_ref[o, n], 0, len(passed) // 2)
+        sums.append(jnp.where(inside, inner, total_ref[n]))
     denom = gas + sums[2]
-    new_r = (gas * gvr_ref[...] + sums[0]) / denom
-    new_a = (gas * gva_ref[...] + sums[1]) / denom
-    gvr_out[...] = new_r
-    gva_out[...] = new_a
-    for b in range(bins):
-        coupling = jnp.broadcast_to(table_ref[0, b:b + 1, :], gas.shape)
-        scale = jnp.broadcast_to(table_ref[1, b:b + 1, :], gas.shape)
-        vr_out[b] = vr_ref[b] * scale + coupling * new_r
-        va_out[b] = va_ref[b] * scale + coupling * new_a
-
-
-def weights_kernel(rows_ref, swapped_ref, out_ref):
+    return (gas * gases_ref[1] + sums[0]) / denom, (gas * gases_ref[2] + sums[1]) / denom
+
+
+def weights_kernel(rows_ref, swapped_ref, gas_ref, gvr_ref, gva_ref, out_ref, gases_ref):
+    for n, ref in enumerate((gas_ref, gvr_ref, gva_ref)):
+        gases_ref[n] = ref[...]
     lines, total = rows_ref.shape
     bins = lines // total
     here = lax.axis_index("bin")
@@ -281,32 +272,51 @@
 
 
 def last_block_kernel(weights_ref, old_ref, *refs):
-    messages, (gain_ref, dens_ref) = refs[:-2], refs[-2:]
-    count = len(messages)
+    messages, (gain_ref, total_ref, dens_ref, sums_ref, halves_ref) = refs[:-5], refs[-5:]
+    count, bins = len(messages), gain_ref.shape[1]
     add_blocks(weights_ref, messages, count, count - 1, count, dens_ref, gain_ref, old_ref)
+    for offset in range(count):
+        read_sums(messages[offset], outer_rows(total_ref.shape[1]), bins, halves_ref, sums_ref.at[offset])
+    for n in range(3):
+        total_ref[n] = total_sums(lambda o, n=n: sums_ref[o, n], 0, count // 2)
 
 
 def last_kernel(
-    count, passing_ref, table_ref, gas_ref, gvr_ref, gva_ref, vr_ref, va_ref, weights_ref, adv_in_ref, adv_out_ref, gain_in_ref, gain_out_ref, *refs
+    count, pieces, passing_ref, total_ref, table_ref, gases_ref, vr_ref, va_ref, weights_ref, adv_in_ref, adv_out_ref,
+    gain_in_ref, gain_out_ref, *refs
 ):
-    messages, refs = refs[:-16], refs[-16:]
-    outs, kept, refs = refs[:5], refs[5:10], refs[10:]
-    new_in_ref, dens_in_ref, sums_ref, halves_in_ref, halves_out_ref, sems = refs
-    rows = vr_ref.shape[1]
-    copies = [pltpu.make_async_copy(kept[n], outs[n], sems.at[n]) for n in range(5)]
+    messages, refs = refs[:count], refs[count:]
+    outs, kept, (new_in_ref, dens_ref, sums_ref, halves_ref, sems) = refs[:5], refs[5:10], refs[10:]
     density_ref, vr_out, va_out, gvr_out, gva_out = kept
-    drag(
-        count, passing_ref, table_ref, gas_ref, gvr_ref, gva_ref, vr_ref, va_ref, messages,
-        vr_out, va_out, gvr_out, gva_out, sums_ref, halves_in_ref, halves_out_ref,
-    )
-    for copy in copies[1:]:
-        copy.start()
-    add_blocks(weights_ref, messages[:count], count, count // 2 + 1, count, dens_in_ref, new_in_ref, gain_in_ref)
+    bins, rows, _ = vr_ref.shape
+    copies = []
+
+    def send_out(n, part=None):
+        source, target = (kept[n], outs[n]) if part is None else (kept[n].at[part], outs[n].at[part])
+        copies.append(pltpu.make_async_copy(source, target, sems.at[len(copies)]))
+        copies[-1].start()
+
+    add_blocks(weights_ref, messages, count, count // 2 + 1, count, dens_ref, new_in_ref, gain_in_ref)
     for n, r in enumerate(inner_rows(rows)):
         density_ref[:, r, :] = adv_in_ref[n] + COAGULATION * new_in_ref[n]
     for n, r in enumerate(outer_rows(rows)):
         density_ref[:, r, :] = adv_out_ref[n] + COAGULATION * gain_out_ref[n]
-    copies[0].start()
+    send_out(0)
+    passed = (passing_ref, *messages[count // 2 + 1:])
+    new_r, new_a = new_gas(passed, total_ref, gases_ref, bins, sums_ref, halves_ref)
+    gvr_out[...] = new_r
+    gva_out[...] = new_a
+    send_out(3)
+    send_out(4)
+    part = bins // pieces
+    for start in range(0, bins, part):
+        for b in range(start, start + part):
+            coupling = jnp.broadcast_to(table_ref[0, b:b + 1, :], new_r.shape)
+            scale = jnp.broadcast_to(table_ref[1, b:b + 1, :], new_r.shape)
+            vr_out[b] = vr_ref[b] * scale + coupling * new_r
+            va_out[b] = va_ref[b] * scale + coupling * new_a
+        send_out(1, pl.ds(start, part))
+        send_out(2, pl.ds(start, part))
     for copy in copies:
         copy.wait()
 
@@ -349,9 +359,10 @@
     inner, outer = inner_rows(rows), outer_rows(rows)
     weights_size = (total * bins, 2 * total)
     small = 2 * weights_size[0] * weights_size[1] <= SMALL_BYTES
-    weights = call(
-        weights_kernel, (pltpu.VMEM if small else struct)(weights_size, BF16),
+    weights, gases = call(
+        weights_kernel, ((pltpu.VMEM if small else struct)(weights_size, BF16), pltpu.VMEM((3, rows, cells), F32)),
         jnp.transpose(coef, (1, 0, 2)).reshape(total * bins, total), jnp.transpose(coef, (2, 0, 1)).reshape(total * bins, total),
+        gas, gvr, gva,
     )
     field, kept = struct(rho.shape), pltpu.VMEM(rho.shape, F32)
     flat = struct(gas.shape)
@@ -397,15 +408,18 @@
         gains.append(call(
             functools.partial(gain_kernel, groups), dense[n], weights, *some, scratch=dens[n:n + 1], loose=() if small else (0,),
         ))
-    gains[1] = call(
-        last_block_kernel, dense[1], weights, gains[1], *out_messages, scratch=dens[1:], loose=() if small else (0,),
-    )
+    gain_out, outer_sums = call(
+        last_block_kernel, (dense[1], pltpu.VMEM((3, rows, cells), F32)), weights, gains[1], *out_messages,
+        scratch=[dens[1], pltpu.VMEM((groups, 3, rows, cells), F32), halves_out], loose=() if small else (0,),
+    )
+    pieces = 4
     return call(
-        functools.partial(last_kernel, groups), (field, field, field, flat, flat),
-        passing, table, gas, gvr, gva, vr, va, weights, adv_in, adv_out, *gains, *in_messages, *out_messages,
+        functools.partial(last_kernel, groups, pieces), (field, field, field, flat, flat),
+        passing, outer_sums, table, gases, vr, va, weights, adv_in, adv_out, gains[0], gain_out, *in_messages,
         scratch=[kept] * 3 + [pltpu.VMEM(gas.shape, F32)] * 2 + dense[:1] + dens[:1]
-        + [pltpu.VMEM((half + groups, 3, rows, cells), F32), halves_in, halves_out, pltpu.SemaphoreType.DMA((5,))],
-        loose=() if small else (7,), spec=ANY,
+        + [pltpu.VMEM((half, 3, rows, cells), F32), halves_in]
+        + [pltpu.SemaphoreType.DMA((3 + 2 * pieces,))],
+        loose=() if small else (6,), spec=ANY,
     )
 
 

time: 28.9 us -> 28.7 us (level)
  waiting for transfers between devices: 6.93 us -> 6.44 us
    ppermute x1, waiting for transfers between devices: 5.06 us -> 4.57 us  [body(): lax.ppermute(plain_in, 'bin', xor_pairs('bin', at))]
  transfers between devices with their start and end apart: 8 -> 8, of which waited for: 2 -> 2; matrix products, arithmetic and copies ran while one was open for 1% -> 2% of each run, Pallas kernels for 11% -> 11%
where the time goes in v8:
time: 28.7 us; the launch traced here: 28.4 us
  starting transfers between devices  13.2 us (46%)
  Pallas kernels  7.01 us (24%)
  waiting for transfers between devices  6.44 us (22%)
  local copies, waits for them, and re-layouts  0.97 us (3%)
  between operations  0.79 us (3%)
    pallas_call x9, Pallas kernels, call(): pl.pallas_call(kernel, out_shape=outs, in_specs=specs, out_specs=jax.tree...  7.01 us
    ppermute x1, waiting for transfers between devices, body(): lax.ppermute(plain_in, 'bin', xor_pairs('bin', at))  4.57 us
    ppermute x3, starting transfers between devices, body(): lax.ppermute(low_out, 'bin', xor_pairs('bin', at))  4.45 us
    ppermute x1, starting transfers between devices, body(): far_in = lax.ppermute(low_in, 'bin', xor_pairs('bin', half))  4.13 us
    ppermute x1, starting transfers between devices, body(): from_b = lax.ppermute(to_b, 'tile', odd_pairs('tile'))  2.56 us
    ppermute x1, waiting for transfers between devices, body(): from_b = lax.ppermute(to_b, 'tile', odd_pairs('tile'))  1.85 us
    ppermute x1, starting transfers between devices, body(): lax.ppermute(plain_in, 'bin', xor_pairs('bin', at))  1.35 us
    ppermute x1, starting transfers between devices, body(): lax.ppermute(passing, 'bin', xor_pairs('bin', at))  0.74 us
  transfers between devices with their start and end apart: 8, of which 2 were waited for; matrix products, arithmetic and copies ran while one was open for 2% of the time, Pallas kernels for 11%

profile of v8, /device:TPU:0, one launch (start us, length us, event | category | flops | bytes accessed | tf_op | source)
XLA Modules:
  0.0 28.4 jit_solution(10399970152314473494)
XLA Ops:
  0.7 1.3 %shard_map.119 = (bf16[3,16,512]{2,1,0:T(8,128)(2,1)S(1)}, bf16[3,16,512]{2,1,0:T(8,128)(2,1)S(1)}, f32[6,16,512]{2,1,0:T(8,128)S(1)}, f32[4,16,512]{2,1,0:T(8,1...) custom-call(f32[16,8,512]{2,1,0:T(8,128)} %rho_ref.1, f32[16,8,512]{2,1,0:T(8,128)} %vr_ref.3, ...), custom_call_target="tpu_custom_call" | custom-call | tf_op jit(solution)/shard_map/pallas_call | solution.py:331
  2.0 0.1 copy-done.2
  2.0 1.1 %shard_map.120 = (bf16[88,512]{1,0:T(8,128)(2,1)S(1)}, bf16[64,512]{1,0:T(8,128)(2,1)S(1)}, f32[4,16,512]{2,1,0:T(8,128)S(1)}, f32[4,16,512]{2,1,0:T(8,128)S(1)}) custom-call(f32[2,16,512]{2,1,0:T(8,128)S(1)} %get-tuple-element.21.table_ref, f32[16,8,512]{2,1,0:T(8,128)S(1)} %copy-done.2, f32[16,8,512]{2,1,0:T(8,128)S(1)} %copy-done, f32[16,8,512]{2,1,0:T(8,128)S(1)} %copy-done.1), custom_call_target="tpu_custom_call" | custom-call | tf_op jit(solution)/shard_map/pallas_call | solution.py:331
  3.1 4.1 %collective-permute-start = (bf16[88,512]{1,0:T(8,128)(2,1)S(1)}, bf16[88,512]{1,0:T(8,128)(2,1)S(1)}, u32[]{:S(2)}, u32[]{:S(2)}) collective-permute-start(bf16[88,512]{1,0:T(8,128)(2,1)S(1)} %get-tuple-element.22.own_ref.refs_0_), channel_id=1, source_target_pairs={{0,2},{1,3},{2,0},{3,1},{4,6},{5,7},{6,4},{7,5},{8,10},{9,11},{10,... | collective-permute-start | bytes 270344 | tf_op jit(solution)/shard_map/ppermute | solution.py:391
  7.2 0.0 collective-permute-start.1
  7.2 2.6 %collective-permute-start.2 = (bf16[3,16,512]{2,1,0:T(8,128)(2,1)S(1)}, bf16[3,16,512]{2,1,0:T(8,128)(2,1)S(1)}, u32[]{:S(2)}, u32[]{:S(2)}) collective-permute-start(bf16[3,16,512]{2,1,0:T(8,128)(2,1)S(1)} %get-tuple-element.29), channel_id=1, source_target_pairs={{0,28},{28,0},{4,8},{8,4},{12,16},{16,12},{20,24},{24,20},{1,29},{... | collective-permute-start | bytes 147464 | tf_op jit(solution)/shard_map/ppermute | solution.py:379
  9.8 0.0 collective-permute-done.1.from_a_ref
  9.8 1.9 %collective-permute-done.2.from_b_ref = bf16[3,16,512]{2,1,0:T(8,128)(2,1)S(1)} collective-permute-done((bf16[3,16,512]{2,1,0:T(8,128)(2,1)S(1)}, bf16[3,16,512]{2,1,0:T(8,128)(2,1)S(1)}, u32[]{:S(2)}, u32[]{:S(2)}) %collective-permute-start.2) | collective-permute-done | bytes 49184 | tf_op jit(solution)/shard_map/ppermute | solution.py:379
  11.6 0.3 shard_map.123
  11.9 0.0 copy-start.6
  11.9 0.3 %collective-permute-start.4 = (bf16[88,512]{1,0:T(8,128)(2,1)S(1)}, bf16[88,512]{1,0:T(8,128)(2,1)S(1)}, u32[]{:S(2)}, u32[]{:S(2)}) collective-permute-start(bf16[88,512]{1,0:T(8,128)(2,1)S(1)} %get-tuple-element.30.refs_0_), channel_id=1, source_target_pairs={{0,2},{1,3},{2,0},{3,1},{4,6},{5,7},{6,4},{7,5},{8,10},{9,11},{10,... | collective-permute-start | bytes 270344 | tf_op jit(solution)/shard_map/ppermute | solution.py:398
  12.2 1.7 %collective-permute-start.3 = (bf16[88,512]{1,0:T(8,128)(2,1)S(1)}, bf16[88,512]{1,0:T(8,128)(2,1)S(1)}, u32[]{:S(2)}, u32[]{:S(2)}) collective-permute-start(bf16[88,512]{1,0:T(8,128)(2,1)S(1)} %get-tuple-element.30.refs_0_), channel_id=1, source_target_pairs={{0,1},{1,0},{2,3},{3,2},{4,5},{5,4},{6,7},{7,6},{8,9},{9,8},{10,11... | collective-permute-start | bytes 270344 | tf_op jit(solution)/shard_map/ppermute | solution.py:397
  13.9 2.5 %collective-permute-start.5 = (bf16[88,512]{1,0:T(8,128)(2,1)S(1)}, bf16[88,512]{1,0:T(8,128)(2,1)S(1)}, u32[]{:S(2)}, u32[]{:S(2)}) collective-permute-start(bf16[88,512]{1,0:T(8,128)(2,1)S(1)} %get-tuple-element.30.refs_0_), channel_id=1, source_target_pairs={{0,3},{1,2},{2,1},{3,0},{4,7},{5,6},{6,5},{7,4},{8,11},{9,10},{10,... | collective-permute-start | bytes 270344 | tf_op jit(solution)/shard_map/ppermute | solution.py:398
  16.4 0.0 collective-permute-done.far_ref.refs_2_
  16.4 0.7 %collective-permute-start.7 = (bf16[88,512]{1,0:T(8,128)(2,1)S(1)}, bf16[88,512]{1,0:T(8,128)(2,1)S(1)}, u32[]{:S(2)}, u32[]{:S(2)}) collective-permute-start(bf16[88,512]{1,0:T(8,128)(2,1)S(1)} %shard_map.121.passing_ref), channel_id=1, source_target_pairs={{0,1},{1,0},{2,3},{3,2},{4,5},{5,4},{6,7},{7,6},{8,9},{9,8},{10,11... | collective-permute-start | bytes 270344 | tf_op jit(solution)/shard_map/ppermute | solution.py:400
  17.2 1.3 %collective-permute-start.6 = (bf16[64,512]{1,0:T(8,128)(2,1)S(1)}, bf16[64,512]{1,0:T(8,128)(2,1)S(1)}, u32[]{:S(2)}, u32[]{:S(2)}) collective-permute-start(bf16[64,512]{1,0:T(8,128)(2,1)S(1)} %get-tuple-element.35), channel_id=1, source_target_pairs={{0,1},{1,0},{2,3},{3,2},{4,5},{5,4},{6,7},{7,6},{8,9},{9,8},{10,11... | collective-permute-start | bytes 196616 | tf_op jit(solution)/shard_map/ppermute | solution.py:390
  18.5 0.2 copy.13
  18.7 0.0 copy-start.3
  18.7 0.0 copy-start.4
  18.7 0.0 copy-start.5
  18.7 0.3 copy.14
  19.0 0.4 %copy-done.3 = f32[8,512]{1,0:T(8,128)S(1)} copy-done((f32[8,512]{1,0:T(8,128)S(1)}, f32[8,512]{1,0:T(8,128)}, u32[]{:S(2)}) %copy-start.3) | copy-done | bytes 16408
  19.4 0.0 copy-done.4
  19.4 0.0 copy-done.5
  19.4 0.3 %shard_map.122 = (bf16[1024,128]{1,0:T(8,128)(2,1)S(1)}, f32[3,8,512]{2,1,0:T(8,128)S(1)}) custom-call(bf16[1024,64]{1,0:T(8,128)(2,1)S(1)} %bitcast.5, bf16[1024,64]{1,0:T(8,128)(2,1)S(1)} %bitcast.6, f32[8,512]{1,0:T(8,128)S(1)} %copy-done.3, f32[8,512]{1,0:T(8,128)S(1)} %copy-done.4, f32[8,512]{1,0:T(8,128)S(1)} %copy-done.5), custom_call_target="tpu_custom_call" | custom-call | tf_op jit(solution)/shard_map/pallas_call | solution.py:331
  19.8 4.6 %collective-permute-done.6.refs_1_ = bf16[64,512]{1,0:T(8,128)(2,1)S(1)} collective-permute-done((bf16[64,512]{1,0:T(8,128)(2,1)S(1)}, bf16[64,512]{1,0:T(8,128)(2,1)S(1)}, u32[]{:S(2)}, u32[]{:S(2)}) %collective-permute-start.6) | collective-permute-done | bytes 65568 | tf_op jit(solution)/shard_map/ppermute | solution.py:390
  24.4 1.0 %shard_map.126.gain_in_ref = f32[4,16,512]{2,1,0:T(8,128)S(1)} custom-call(bf16[1024,128]{1,0:T(8,128)(2,1)S(1)} %get-tuple-element.23.weights_ref, bf16[88,512]{1,0:T(8,128)(2,1)S(1)} %get-tuple-element.22.own_ref.refs_0_, bf16[64,512]{1,0:T(8,128)(2,1)S(1)} %collective-permute-done.6.refs_1_, bf16[88,512]{1,0:T(8,128)(2,1)S(1)} %collective-permute-done.far_ref.refs_2_), custom_call_target="tpu_custom_call" | custom-call | tf_op jit(solution)/shard_map/pallas_call | solution.py:331
  25.4 0.0 collective-permute-done.4.refs_2_
  25.4 1.0 %shard_map.124.old_ref = f32[4,16,512]{2,1,0:T(8,128)S(1)} custom-call(bf16[1024,128]{1,0:T(8,128)(2,1)S(1)} %get-tuple-element.23.weights_ref, bf16[88,512]{1,0:T(8,128)(2,1)S(1)} %get-tuple-element.30.refs_0_, bf16[88,512]{1,0:T(8,128)(2,1)S(1)} %collective-permute-done.3.refs_1_, bf16[88,512]{1,0:T(8,128)(2,1)S(1)} %collective-permute-done.4.refs_2_), custom_call_target="tpu_custom_call" | custom-call | tf_op jit(solution)/shard_map/pallas_call | solution.py:331
  26.4 0.5 %shard_map.125 = (f32[4,16,512]{2,1,0:T(8,128)S(1)}, f32[3,8,512]{2,1,0:T(8,128)S(1)}) custom-call(bf16[1024,128]{1,0:T(8,128)(2,1)S(1)} %get-tuple-element.23.weights_ref, f32[4,16,512]{2,1,0:T(8,128)S(1)} %shard_map.124.old_ref, bf16[88,512]{1,0:T(8,128)(2,1)S(1)} %get-tuple-element.30.refs_0_, bf16[88,512]{1,0:T(8,128)(2,1)S(1)} %collective-permute-done.3.refs_1_, ...), custom_call_target="tpu_custom_call" | custom-call | tf_op jit(solution)/shard_map/pallas_call | solution.py:331
  26.9 0.0 collective-permute-done.7.refs_3_
  27.0 1.5 %shard_map.127 = (f32[16,8,512]{2,1,0:T(8,128)}, f32[16,8,512]{2,1,0:T(8,128)}, f32[16,8,512]{2,1,0:T(8,128)}, f32[8,512]{1,0:T(8,128)}, f32[8,512]{1,0:T(8,128)}) custom-call(bf16[88,512]{1,0:T(8,128)(2,1)S(1)} %shard_map.121.passing_ref, f32[3,8,512]{2,1,0:T(8,128)S(1)} %get-tuple-element.31.total_ref, f32[2,16,512]{2,1,0:T(8,128)S(1)} %get-tuple-element.21.table_ref, ...), custom_call_target="tpu_custom_call" | custom-call | tf_op jit(solution)/shard_map/pallas_call | solution.py:331
  (9 shorter events, 0.1 us)
Async XLA Ops:
  0.6 1.3 %copy-start = (f32[16,8,512]{2,1,0:T(8,128)S(1)}, f32[16,8,512]{2,1,0:T(8,128)}, u32[]{:S(2)}) copy-start(f32[16,8,512]{2,1,0:T(8,128)} %vr_ref.3) | copy-start | bytes 786436
  0.6 1.3 %copy-start.1 = (f32[16,8,512]{2,1,0:T(8,128)S(1)}, f32[16,8,512]{2,1,0:T(8,128)}, u32[]{:S(2)}) copy-start(f32[16,8,512]{2,1,0:T(8,128)} %va_ref.3) | copy-start | bytes 786436
  0.7 1.4 %copy-start.2 = (f32[16,8,512]{2,1,0:T(8,128)S(1)}, f32[16,8,512]{2,1,0:T(8,128)}, u32[]{:S(2)}) copy-start(f32[16,8,512]{2,1,0:T(8,128)} %rho_ref.1) | copy-start | bytes 786436
  3.1 13.3 %collective-permute-start = (bf16[88,512]{1,0:T(8,128)(2,1)S(1)}, bf16[88,512]{1,0:T(8,128)(2,1)S(1)}, u32[]{:S(2)}, u32[]{:S(2)}) collective-permute-start(bf16[88,512]{1,0:T(8,128)(2,1)S(1)} %get-tuple-element.22.own_ref.refs_0_), channel_id=1, source_target_pairs={{0,2},{1,3},{2,0},{3,1},{4,6},{5,7},{6,4},{7,5},{8,10},{9,11},{10,... | collective-permute-start | bytes 270344 | tf_op jit(solution)/shard_map/ppermute | solution.py:391
  7.2 2.6 %collective-permute-start.1 = (bf16[3,16,512]{2,1,0:T(8,128)(2,1)S(1)}, bf16[3,16,512]{2,1,0:T(8,128)(2,1)S(1)}, u32[]{:S(2)}, u32[]{:S(2)}) collective-permute-start(bf16[3,16,512]{2,1,0:T(8,128)(2,1)S(1)} %get-tuple-element.28), channel_id=1, source_target_pairs={{0,4},{4,0},{8,12},{12,8},{16,20},{20,16},{24,28},{28,24},{1,5},{5... | collective-permute-start | bytes 147464 | tf_op jit(solution)/shard_map/ppermute | solution.py:380
  7.2 4.4 %collective-permute-start.2 = (bf16[3,16,512]{2,1,0:T(8,128)(2,1)S(1)}, bf16[3,16,512]{2,1,0:T(8,128)(2,1)S(1)}, u32[]{:S(2)}, u32[]{:S(2)}) collective-permute-start(bf16[3,16,512]{2,1,0:T(8,128)(2,1)S(1)} %get-tuple-element.29), channel_id=1, source_target_pairs={{0,28},{28,0},{4,8},{8,4},{12,16},{16,12},{20,24},{24,20},{1,29},{... | collective-permute-start | bytes 147464 | tf_op jit(solution)/shard_map/ppermute | solution.py:379
  11.9 6.6 %copy-start.6 = (bf16[16,64,64]{2,1,0:T(8,128)(2,1)S(1)}, bf16[16,64,64]{2,1,0:T(8,128)(2,1)}, u32[]{:S(2)}) copy-start(bf16[16,64,64]{2,1,0:T(8,128)(2,1)} %param.15) | copy-start | bytes 393220
  11.9 13.5 %collective-permute-start.4 = (bf16[88,512]{1,0:T(8,128)(2,1)S(1)}, bf16[88,512]{1,0:T(8,128)(2,1)S(1)}, u32[]{:S(2)}, u32[]{:S(2)}) collective-permute-start(bf16[88,512]{1,0:T(8,128)(2,1)S(1)} %get-tuple-element.30.refs_0_), channel_id=1, source_target_pairs={{0,2},{1,3},{2,0},{3,1},{4,6},{5,7},{6,4},{7,5},{8,10},{9,11},{10,... | collective-permute-start | bytes 270344 | tf_op jit(solution)/shard_map/ppermute | solution.py:398
  12.2 13.2 %collective-permute-start.3 = (bf16[88,512]{1,0:T(8,128)(2,1)S(1)}, bf16[88,512]{1,0:T(8,128)(2,1)S(1)}, u32[]{:S(2)}, u32[]{:S(2)}) collective-permute-start(bf16[88,512]{1,0:T(8,128)(2,1)S(1)} %get-tuple-element.30.refs_0_), channel_id=1, source_target_pairs={{0,1},{1,0},{2,3},{3,2},{4,5},{5,4},{6,7},{7,6},{8,9},{9,8},{10,11... | collective-permute-start | bytes 270344 | tf_op jit(solution)/shard_map/ppermute | solution.py:397
  13.9 12.5 %collective-permute-start.5 = (bf16[88,512]{1,0:T(8,128)(2,1)S(1)}, bf16[88,512]{1,0:T(8,128)(2,1)S(1)}, u32[]{:S(2)}, u32[]{:S(2)}) collective-permute-start(bf16[88,512]{1,0:T(8,128)(2,1)S(1)} %get-tuple-element.30.refs_0_), channel_id=1, source_target_pairs={{0,3},{1,2},{2,1},{3,0},{4,7},{5,6},{6,5},{7,4},{8,11},{9,10},{10,... | collective-permute-start | bytes 270344 | tf_op jit(solution)/shard_map/ppermute | solution.py:398
  16.4 10.5 %collective-permute-start.7 = (bf16[88,512]{1,0:T(8,128)(2,1)S(1)}, bf16[88,512]{1,0:T(8,128)(2,1)S(1)}, u32[]{:S(2)}, u32[]{:S(2)}) collective-permute-start(bf16[88,512]{1,0:T(8,128)(2,1)S(1)} %shard_map.121.passing_ref), channel_id=1, source_target_pairs={{0,1},{1,0},{2,3},{3,2},{4,5},{5,4},{6,7},{7,6},{8,9},{9,8},{10,11... | collective-permute-start | bytes 270344 | tf_op jit(solution)/shard_map/ppermute | solution.py:400
  17.2 7.2 %collective-permute-start.6 = (bf16[64,512]{1,0:T(8,128)(2,1)S(1)}, bf16[64,512]{1,0:T(8,128)(2,1)S(1)}, u32[]{:S(2)}, u32[]{:S(2)}) collective-permute-start(bf16[64,512]{1,0:T(8,128)(2,1)S(1)} %get-tuple-element.35), channel_id=1, source_target_pairs={{0,1},{1,0},{2,3},{3,2},{4,5},{5,4},{6,7},{7,6},{8,9},{9,8},{10,11... | collective-permute-start | bytes 196616 | tf_op jit(solution)/shard_map/ppermute | solution.py:390
  18.7 0.7 %copy-start.3 = (f32[8,512]{1,0:T(8,128)S(1)}, f32[8,512]{1,0:T(8,128)}, u32[]{:S(2)}) copy-start(f32[8,512]{1,0:T(8,128)} %gas_ref.1) | copy-start | bytes 49156
  18.7 0.7 %copy-start.4 = (f32[8,512]{1,0:T(8,128)S(1)}, f32[8,512]{1,0:T(8,128)}, u32[]{:S(2)}) copy-start(f32[8,512]{1,0:T(8,128)} %gvr_ref.1) | copy-start | bytes 49156
  18.7 0.7 %copy-start.5 = (f32[8,512]{1,0:T(8,128)S(1)}, f32[8,512]{1,0:T(8,128)}, u32[]{:S(2)}) copy-start(f32[8,512]{1,0:T(8,128)} %gva_ref.1) | copy-start | bytes 49156

commit v9 on v8

--- a/solution.py
+++ b/solution.py
@@ -124,7 +124,7 @@
     return (sums[0] + weight * vr, sums[1] + weight * va, sums[2] + weight)
 
 
-def inner_kernel(table_ref, rho_ref, vr_ref, va_ref, message_ref, plain_ref, adv_ref, part_ref, all_ref, halves_ref):
+def inner_kernel(table_ref, rho_ref, vr_ref, va_ref, message_ref, plain_ref, adv_ref, all_ref, halves_ref):
     bins, rows, cells = rho_ref.shape
     zero = jnp.zeros((rows, cells), F32)
     sums = (zero, zero, zero)
@@ -139,11 +139,9 @@
         adv_ref[n] = density
     write_message(message_ref, densities, [[x[r:r + 1] for r in picked] for x in sums], halves_ref)
     plain_ref[...] = message_ref[:plain_ref.shape[0], :]
-    for n, r in enumerate(outer_rows(rows)):
-        part_ref[n] = all_ref[:, r, :]
-
-
-def outer_kernel(table_ref, rho_ref, vr_ref, va_ref, part_ref, from_a_ref, from_b_ref, adv_ref, message_ref, halves_ref):
+
+
+def outer_kernel(table_ref, rho_ref, vr_ref, va_ref, all_ref, from_a_ref, from_b_ref, adv_ref, message_ref, halves_ref):
     tile, tiles = lax.axis_index("tile"), lax.axis_size("tile")
     even = tile % 2 == 0
     has_top = jnp.where(tile > 0, 1.0, 0.0)
@@ -168,7 +166,7 @@
 
     row = [rho_ref[n] for n in range(rho_ref.shape[0])]
     speed = [vr_ref[n] for n in range(vr_ref.shape[0])]
-    part = [part_ref[n] for n in range(part_ref.shape[0])]
+    part = [all_ref[:, r, :] for r in outer_rows(all_ref.shape[1])]
     first, second = edge(row[:3], part[:2], speed[:2], -1.0, top)
     last, before = edge(row[:2:-1], part[:1:-1], speed[:1:-1], 1.0, bottom)
     densities = [first, second, before, last]
@@ -382,17 +380,17 @@
     groups = lax.axis_size("bin")
     half = groups // 2
     dense = [pltpu.VMEM((len(picked), bins, cells), F32) for picked in (inner, outer)]
-    low_in, plain_in, adv_in, part_out = call(
+    low_in, plain_in, adv_in, part_all = call(
         inner_kernel,
-        (pltpu.VMEM((inner_lines, cells), BF16), pltpu.VMEM((bins * len(inner), cells), BF16), *dense), table, rho, vr, va,
-        scratch=[kept, halves_in],
+        (pltpu.VMEM((inner_lines, cells), BF16), pltpu.VMEM((bins * len(inner), cells), BF16), dense[0], kept), table, rho, vr, va,
+        scratch=[halves_in],
     )
     near_in = [lax.ppermute(plain_in, "bin", xor_pairs("bin", at)) for at in range(1, half)]
     far_in = lax.ppermute(low_in, "bin", xor_pairs("bin", half))
 
     adv_out, low_out = call(
         outer_kernel, (dense[1], pltpu.VMEM((outer_lines, cells), BF16)),
-        table, rho_edge, vr_edge, va_edge, part_out, from_a, from_b, scratch=[halves_out],
+        table, rho_edge, vr_edge, va_edge, part_all, from_a, from_b, scratch=[halves_out],
     )
     near_out = [lax.ppermute(low_out, "bin", xor_pairs("bin", at)) for at in range(1, half)]
     far_out = [lax.ppermute(low_out, "bin", xor_pairs("bin", at)) for at in range(half, groups)]

time: 28.7 us -> 28.7 us (level)
  no operation moved by 1% of the time
where the time goes in v9:
time: 28.7 us; the launch traced here: 28.4 us
  starting transfers between devices  13.2 us (46%)
  Pallas kernels  7.01 us (24%)
  waiting for transfers between devices  6.44 us (22%)
  local copies, waits for them, and re-layouts  0.97 us (3%)
  between operations  0.79 us (3%)
    pallas_call x9, Pallas kernels, call(): pl.pallas_call(kernel, out_shape=outs, in_specs=specs, out_specs=jax.tree...  7.01 us
    ppermute x1, waiting for transfers between devices, body(): lax.ppermute(plain_in, 'bin', xor_pairs('bin', at))  4.57 us
    ppermute x3, starting transfers between devices, body(): lax.ppermute(low_out, 'bin', xor_pairs('bin', at))  4.45 us
    ppermute x1, starting transfers between devices, body(): far_in = lax.ppermute(low_in, 'bin', xor_pairs('bin', half))  4.13 us
    ppermute x1, starting transfers between devices, body(): from_b = lax.ppermute(to_b, 'tile', odd_pairs('tile'))  2.56 us
    ppermute x1, waiting for transfers between devices, body(): from_b = lax.ppermute(to_b, 'tile', odd_pairs('tile'))  1.85 us
    ppermute x1, starting transfers between devices, body(): lax.ppermute(plain_in, 'bin', xor_pairs('bin', at))  1.35 us
    ppermute x1, starting transfers between devices, body(): lax.ppermute(passing, 'bin', xor_pairs('bin', at))  0.74 us
  transfers between devices with their start and end apart: 8, of which 2 were waited for; matrix products, arithmetic and copies ran while one was open for 2% of the time, Pallas kernels for 11%

profile of v9, /device:TPU:0, one launch (start us, length us, event | category | flops | bytes accessed | tf_op | source)
XLA Modules:
  0.0 28.4 jit_solution(8149551143858778008)
XLA Ops:
  0.7 1.3 %shard_map.119 = (bf16[3,16,512]{2,1,0:T(8,128)(2,1)S(1)}, bf16[3,16,512]{2,1,0:T(8,128)(2,1)S(1)}, f32[6,16,512]{2,1,0:T(8,128)S(1)}, f32[4,16,512]{2,1,0:T(8,1...) custom-call(f32[16,8,512]{2,1,0:T(8,128)} %rho_ref.1, f32[16,8,512]{2,1,0:T(8,128)} %vr_ref.3, ...), custom_call_target="tpu_custom_call" | custom-call | tf_op jit(solution)/shard_map/pallas_call | solution.py:329
  2.0 0.1 copy-done.2
  2.0 1.0 %shard_map.120 = (bf16[88,512]{1,0:T(8,128)(2,1)S(1)}, bf16[64,512]{1,0:T(8,128)(2,1)S(1)}, f32[4,16,512]{2,1,0:T(8,128)S(1)}, f32[16,8,512]{2,1,0:T(8,128)S(1)}) custom-call(f32[2,16,512]{2,1,0:T(8,128)S(1)} %get-tuple-element.21.table_ref, f32[16,8,512]{2,1,0:T(8,128)S(1)} %copy-done.2, f32[16,8,512]{2,1,0:T(8,128)S(1)} %copy-done, f32[16,8,512]{2,1,0:T(8,128)S(1)} %copy-done.1), custom_call_target="tpu_custom_call" | custom-call | tf_op jit(solution)/shard_map/pallas_call | solution.py:329
  3.1 4.1 %collective-permute-start = (bf16[88,512]{1,0:T(8,128)(2,1)S(1)}, bf16[88,512]{1,0:T(8,128)(2,1)S(1)}, u32[]{:S(2)}, u32[]{:S(2)}) collective-permute-start(bf16[88,512]{1,0:T(8,128)(2,1)S(1)} %get-tuple-element.22.own_ref.refs_0_), channel_id=1, source_target_pairs={{0,2},{1,3},{2,0},{3,1},{4,6},{5,7},{6,4},{7,5},{8,10},{9,11},{10,... | collective-permute-start | bytes 270344 | tf_op jit(solution)/shard_map/ppermute | solution.py:389
  7.2 2.6 %collective-permute-start.2 = (bf16[3,16,512]{2,1,0:T(8,128)(2,1)S(1)}, bf16[3,16,512]{2,1,0:T(8,128)(2,1)S(1)}, u32[]{:S(2)}, u32[]{:S(2)}) collective-permute-start(bf16[3,16,512]{2,1,0:T(8,128)(2,1)S(1)} %get-tuple-element.29), channel_id=1, source_target_pairs={{0,28},{28,0},{4,8},{8,4},{12,16},{16,12},{20,24},{24,20},{1,29},{... | collective-permute-start | bytes 147464 | tf_op jit(solution)/shard_map/ppermute | solution.py:377
  9.8 0.0 collective-permute-done.1.from_a_ref
  9.8 1.9 %collective-permute-done.2.from_b_ref = bf16[3,16,512]{2,1,0:T(8,128)(2,1)S(1)} collective-permute-done((bf16[3,16,512]{2,1,0:T(8,128)(2,1)S(1)}, bf16[3,16,512]{2,1,0:T(8,128)(2,1)S(1)}, u32[]{:S(2)}, u32[]{:S(2)}) %collective-permute-start.2) | collective-permute-done | bytes 49184 | tf_op jit(solution)/shard_map/ppermute | solution.py:377
  11.6 0.3 shard_map.123
  11.9 0.0 copy-start.6
  11.9 0.3 %collective-permute-start.4 = (bf16[88,512]{1,0:T(8,128)(2,1)S(1)}, bf16[88,512]{1,0:T(8,128)(2,1)S(1)}, u32[]{:S(2)}, u32[]{:S(2)}) collective-permute-start(bf16[88,512]{1,0:T(8,128)(2,1)S(1)} %get-tuple-element.30.refs_0_), channel_id=1, source_target_pairs={{0,2},{1,3},{2,0},{3,1},{4,6},{5,7},{6,4},{7,5},{8,10},{9,11},{10,... | collective-permute-start | bytes 270344 | tf_op jit(solution)/shard_map/ppermute | solution.py:396
  12.2 1.7 %collective-permute-start.3 = (bf16[88,512]{1,0:T(8,128)(2,1)S(1)}, bf16[88,512]{1,0:T(8,128)(2,1)S(1)}, u32[]{:S(2)}, u32[]{:S(2)}) collective-permute-start(bf16[88,512]{1,0:T(8,128)(2,1)S(1)} %get-tuple-element.30.refs_0_), channel_id=1, source_target_pairs={{0,1},{1,0},{2,3},{3,2},{4,5},{5,4},{6,7},{7,6},{8,9},{9,8},{10,11... | collective-permute-start | bytes 270344 | tf_op jit(solution)/shard_map/ppermute | solution.py:395
  13.9 2.5 %collective-permute-start.5 = (bf16[88,512]{1,0:T(8,128)(2,1)S(1)}, bf16[88,512]{1,0:T(8,128)(2,1)S(1)}, u32[]{:S(2)}, u32[]{:S(2)}) collective-permute-start(bf16[88,512]{1,0:T(8,128)(2,1)S(1)} %get-tuple-element.30.refs_0_), channel_id=1, source_target_pairs={{0,3},{1,2},{2,1},{3,0},{4,7},{5,6},{6,5},{7,4},{8,11},{9,10},{10,... | collective-permute-start | bytes 270344 | tf_op jit(solution)/shard_map/ppermute | solution.py:396
  16.4 0.7 %collective-permute-start.7 = (bf16[88,512]{1,0:T(8,128)(2,1)S(1)}, bf16[88,512]{1,0:T(8,128)(2,1)S(1)}, u32[]{:S(2)}, u32[]{:S(2)}) collective-permute-start(bf16[88,512]{1,0:T(8,128)(2,1)S(1)} %shard_map.121.passing_ref), channel_id=1, source_target_pairs={{0,1},{1,0},{2,3},{3,2},{4,5},{5,4},{6,7},{7,6},{8,9},{9,8},{10,11... | collective-permute-start | bytes 270344 | tf_op jit(solution)/shard_map/ppermute | solution.py:398
  17.2 1.3 %collective-permute-start.6 = (bf16[64,512]{1,0:T(8,128)(2,1)S(1)}, bf16[64,512]{1,0:T(8,128)(2,1)S(1)}, u32[]{:S(2)}, u32[]{:S(2)}) collective-permute-start(bf16[64,512]{1,0:T(8,128)(2,1)S(1)} %get-tuple-element.35), channel_id=1, source_target_pairs={{0,1},{1,0},{2,3},{3,2},{4,5},{5,4},{6,7},{7,6},{8,9},{9,8},{10,11... | collective-permute-start | bytes 196616 | tf_op jit(solution)/shard_map/ppermute | solution.py:388
  18.5 0.2 copy.13
  18.7 0.0 copy-start.3
  18.7 0.0 copy-start.4
  18.7 0.0 copy-start.5
  18.7 0.3 copy.14
  19.0 0.4 %copy-done.3 = f32[8,512]{1,0:T(8,128)S(1)} copy-done((f32[8,512]{1,0:T(8,128)S(1)}, f32[8,512]{1,0:T(8,128)}, u32[]{:S(2)}) %copy-start.3) | copy-done | bytes 16408
  19.4 0.0 copy-done.4
  19.4 0.0 copy-done.5
  19.4 0.3 %shard_map.122 = (bf16[1024,128]{1,0:T(8,128)(2,1)S(1)}, f32[3,8,512]{2,1,0:T(8,128)S(1)}) custom-call(bf16[1024,64]{1,0:T(8,128)(2,1)S(1)} %bitcast.5, bf16[1024,64]{1,0:T(8,128)(2,1)S(1)} %bitcast.6, f32[8,512]{1,0:T(8,128)S(1)} %copy-done.3, f32[8,512]{1,0:T(8,128)S(1)} %copy-done.4, f32[8,512]{1,0:T(8,128)S(1)} %copy-done.5), custom_call_target="tpu_custom_call" | custom-call | tf_op jit(solution)/shard_map/pallas_call | solution.py:329
  19.8 4.6 %collective-permute-done.6.refs_1_ = bf16[64,512]{1,0:T(8,128)(2,1)S(1)} collective-permute-done((bf16[64,512]{1,0:T(8,128)(2,1)S(1)}, bf16[64,512]{1,0:T(8,128)(2,1)S(1)}, u32[]{:S(2)}, u32[]{:S(2)}) %collective-permute-start.6) | collective-permute-done | bytes 65568 | tf_op jit(solution)/shard_map/ppermute | solution.py:388
  24.4 1.0 %shard_map.126.gain_in_ref = f32[4,16,512]{2,1,0:T(8,128)S(1)} custom-call(bf16[1024,128]{1,0:T(8,128)(2,1)S(1)} %get-tuple-element.23.weights_ref, bf16[88,512]{1,0:T(8,128)(2,1)S(1)} %get-tuple-element.22.own_ref.refs_0_, bf16[64,512]{1,0:T(8,128)(2,1)S(1)} %collective-permute-done.6.refs_1_, bf16[88,512]{1,0:T(8,128)(2,1)S(1)} %collective-permute-done.far_ref.refs_2_), custom_call_target="tpu_custom_call" | custom-call | tf_op jit(solution)/shard_map/pallas_call | solution.py:329
  25.4 0.0 collective-permute-done.4.refs_2_
  25.4 0.0 collective-permute-done.3.refs_1_
  25.4 1.0 %shard_map.124.old_ref = f32[4,16,512]{2,1,0:T(8,128)S(1)} custom-call(bf16[1024,128]{1,0:T(8,128)(2,1)S(1)} %get-tuple-element.23.weights_ref, bf16[88,512]{1,0:T(8,128)(2,1)S(1)} %get-tuple-element.30.refs_0_, bf16[88,512]{1,0:T(8,128)(2,1)S(1)} %collective-permute-done.3.refs_1_, bf16[88,512]{1,0:T(8,128)(2,1)S(1)} %collective-permute-done.4.refs_2_), custom_call_target="tpu_custom_call" | custom-call | tf_op jit(solution)/shard_map/pallas_call | solution.py:329
  26.4 0.0 collective-permute-done.5.refs_3_
  26.4 0.5 %shard_map.125 = (f32[4,16,512]{2,1,0:T(8,128)S(1)}, f32[3,8,512]{2,1,0:T(8,128)S(1)}) custom-call(bf16[1024,128]{1,0:T(8,128)(2,1)S(1)} %get-tuple-element.23.weights_ref, f32[4,16,512]{2,1,0:T(8,128)S(1)} %shard_map.124.old_ref, bf16[88,512]{1,0:T(8,128)(2,1)S(1)} %get-tuple-element.30.refs_0_, bf16[88,512]{1,0:T(8,128)(2,1)S(1)} %collective-permute-done.3.refs_1_, ...), custom_call_target="tpu_custom_call" | custom-call | tf_op jit(solution)/shard_map/pallas_call | solution.py:329
  26.9 0.0 collective-permute-done.7.refs_3_
  27.0 1.5 %shard_map.127 = (f32[16,8,512]{2,1,0:T(8,128)}, f32[16,8,512]{2,1,0:T(8,128)}, f32[16,8,512]{2,1,0:T(8,128)}, f32[8,512]{1,0:T(8,128)}, f32[8,512]{1,0:T(8,128)}) custom-call(bf16[88,512]{1,0:T(8,128)(2,1)S(1)} %shard_map.121.passing_ref, f32[3,8,512]{2,1,0:T(8,128)S(1)} %get-tuple-element.31.total_ref, f32[2,16,512]{2,1,0:T(8,128)S(1)} %get-tuple-element.21.table_ref, ...), custom_call_target="tpu_custom_call" | custom-call | tf_op jit(solution)/shard_map/pallas_call | solution.py:329
  (9 shorter events, 0.1 us)
Async XLA Ops:
  0.6 1.3 %copy-start = (f32[16,8,512]{2,1,0:T(8,128)S(1)}, f32[16,8,512]{2,1,0:T(8,128)}, u32[]{:S(2)}) copy-start(f32[16,8,512]{2,1,0:T(8,128)} %vr_ref.3) | copy-start | bytes 786436
  0.6 1.3 %copy-start.1 = (f32[16,8,512]{2,1,0:T(8,128)S(1)}, f32[16,8,512]{2,1,0:T(8,128)}, u32[]{:S(2)}) copy-start(f32[16,8,512]{2,1,0:T(8,128)} %va_ref.3) | copy-start | bytes 786436
  0.7 1.4 %copy-start.2 = (f32[16,8,512]{2,1,0:T(8,128)S(1)}, f32[16,8,512]{2,1,0:T(8,128)}, u32[]{:S(2)}) copy-start(f32[16,8,512]{2,1,0:T(8,128)} %rho_ref.1) | copy-start | bytes 786436
  3.1 13.3 %collective-permute-start = (bf16[88,512]{1,0:T(8,128)(2,1)S(1)}, bf16[88,512]{1,0:T(8,128)(2,1)S(1)}, u32[]{:S(2)}, u32[]{:S(2)}) collective-permute-start(bf16[88,512]{1,0:T(8,128)(2,1)S(1)} %get-tuple-element.22.own_ref.refs_0_), channel_id=1, source_target_pairs={{0,2},{1,3},{2,0},{3,1},{4,6},{5,7},{6,4},{7,5},{8,10},{9,11},{10,... | collective-permute-start | bytes 270344 | tf_op jit(solution)/shard_map/ppermute | solution.py:389
  7.2 2.6 %collective-permute-start.1 = (bf16[3,16,512]{2,1,0:T(8,128)(2,1)S(1)}, bf16[3,16,512]{2,1,0:T(8,128)(2,1)S(1)}, u32[]{:S(2)}, u32[]{:S(2)}) collective-permute-start(bf16[3,16,512]{2,1,0:T(8,128)(2,1)S(1)} %get-tuple-element.28), channel_id=1, source_target_pairs={{0,4},{4,0},{8,12},{12,8},{16,20},{20,16},{24,28},{28,24},{1,5},{5... | collective-permute-start | bytes 147464 | tf_op jit(solution)/shard_map/ppermute | solution.py:378
  7.2 4.4 %collective-permute-start.2 = (bf16[3,16,512]{2,1,0:T(8,128)(2,1)S(1)}, bf16[3,16,512]{2,1,0:T(8,128)(2,1)S(1)}, u32[]{:S(2)}, u32[]{:S(2)}) collective-permute-start(bf16[3,16,512]{2,1,0:T(8,128)(2,1)S(1)} %get-tuple-element.29), channel_id=1, source_target_pairs={{0,28},{28,0},{4,8},{8,4},{12,16},{16,12},{20,24},{24,20},{1,29},{... | collective-permute-start | bytes 147464 | tf_op jit(solution)/shard_map/ppermute | solution.py:377
  11.9 6.6 %copy-start.6 = (bf16[16,64,64]{2,1,0:T(8,128)(2,1)S(1)}, bf16[16,64,64]{2,1,0:T(8,128)(2,1)}, u32[]{:S(2)}) copy-start(bf16[16,64,64]{2,1,0:T(8,128)(2,1)} %param.15) | copy-start | bytes 393220
  11.9 13.5 %collective-permute-start.4 = (bf16[88,512]{1,0:T(8,128)(2,1)S(1)}, bf16[88,512]{1,0:T(8,128)(2,1)S(1)}, u32[]{:S(2)}, u32[]{:S(2)}) collective-permute-start(bf16[88,512]{1,0:T(8,128)(2,1)S(1)} %get-tuple-element.30.refs_0_), channel_id=1, source_target_pairs={{0,2},{1,3},{2,0},{3,1},{4,6},{5,7},{6,4},{7,5},{8,10},{9,11},{10,... | collective-permute-start | bytes 270344 | tf_op jit(solution)/shard_map/ppermute | solution.py:396
  12.2 13.2 %collective-permute-start.3 = (bf16[88,512]{1,0:T(8,128)(2,1)S(1)}, bf16[88,512]{1,0:T(8,128)(2,1)S(1)}, u32[]{:S(2)}, u32[]{:S(2)}) collective-permute-start(bf16[88,512]{1,0:T(8,128)(2,1)S(1)} %get-tuple-element.30.refs_0_), channel_id=1, source_target_pairs={{0,1},{1,0},{2,3},{3,2},{4,5},{5,4},{6,7},{7,6},{8,9},{9,8},{10,11... | collective-permute-start | bytes 270344 | tf_op jit(solution)/shard_map/ppermute | solution.py:395
  13.9 12.5 %collective-permute-start.5 = (bf16[88,512]{1,0:T(8,128)(2,1)S(1)}, bf16[88,512]{1,0:T(8,128)(2,1)S(1)}, u32[]{:S(2)}, u32[]{:S(2)}) collective-permute-start(bf16[88,512]{1,0:T(8,128)(2,1)S(1)} %get-tuple-element.30.refs_0_), channel_id=1, source_target_pairs={{0,3},{1,2},{2,1},{3,0},{4,7},{5,6},{6,5},{7,4},{8,11},{9,10},{10,... | collective-permute-start | bytes 270344 | tf_op jit(solution)/shard_map/ppermute | solution.py:396
  16.4 10.5 %collective-permute-start.7 = (bf16[88,512]{1,0:T(8,128)(2,1)S(1)}, bf16[88,512]{1,0:T(8,128)(2,1)S(1)}, u32[]{:S(2)}, u32[]{:S(2)}) collective-permute-start(bf16[88,512]{1,0:T(8,128)(2,1)S(1)} %shard_map.121.passing_ref), channel_id=1, source_target_pairs={{0,1},{1,0},{2,3},{3,2},{4,5},{5,4},{6,7},{7,6},{8,9},{9,8},{10,11... | collective-permute-start | bytes 270344 | tf_op jit(solution)/shard_map/ppermute | solution.py:398
  17.2 7.2 %collective-permute-start.6 = (bf16[64,512]{1,0:T(8,128)(2,1)S(1)}, bf16[64,512]{1,0:T(8,128)(2,1)S(1)}, u32[]{:S(2)}, u32[]{:S(2)}) collective-permute-start(bf16[64,512]{1,0:T(8,128)(2,1)S(1)} %get-tuple-element.35), channel_id=1, source_target_pairs={{0,1},{1,0},{2,3},{3,2},{4,5},{5,4},{6,7},{7,6},{8,9},{9,8},{10,11... | collective-permute-start | bytes 196616 | tf_op jit(solution)/shard_map/ppermute | solution.py:388
  18.7 0.7 %copy-start.3 = (f32[8,512]{1,0:T(8,128)S(1)}, f32[8,512]{1,0:T(8,128)}, u32[]{:S(2)}) copy-start(f32[8,512]{1,0:T(8,128)} %gas_ref.1) | copy-start | bytes 49156
  18.7 0.7 %copy-start.4 = (f32[8,512]{1,0:T(8,128)S(1)}, f32[8,512]{1,0:T(8,128)}, u32[]{:S(2)}) copy-start(f32[8,512]{1,0:T(8,128)} %gvr_ref.1) | copy-start | bytes 49156
  18.7 0.7 %copy-start.5 = (f32[8,512]{1,0:T(8,128)S(1)}, f32[8,512]{1,0:T(8,128)}, u32[]{:S(2)}) copy-start(f32[8,512]{1,0:T(8,128)} %gva_ref.1) | copy-start | bytes 49156
